TPU v7x, 32 devices: a whole 2x2x4 slice. The times are simulated.
32 devices in a mesh: patch: 8 (over y, x, core), tm: 4 (over z).
Axes of the slice: x: 2, y: 2, z: 4, core: 2. Of those that a mesh axis runs over, the one named last changes fastest.
Arguments:
- bits: int32 [32, 8, 26, 24], P('patch', 'tm'), may hold values 0 or 1
- partners: int32 [4, 32], P('tm'), may hold values from 0 to 31, as said below
- gate_round: int32 [4], P('tm'), may hold values from 0 to 7, as said below
- first_kernel: bfloat16 [3, 3, 3, 32], replicated, may hold values from -1.25 to 1.25
- second_kernels: bfloat16 [2, 3, 3, 3, 32, 32], replicated, may hold values from -0.21875 to 0.21875
- conv_bias: float32 [3, 32], replicated, may hold values from -3 to 3
- couple_down: bfloat16 [2, 32, 16], replicated, may hold values from -1 to 1
- couple_up: bfloat16 [2, 2, 16, 32], replicated, may hold values from -1.5 to 1.5
- head: bfloat16 [32], replicated, may hold values from -1 to 1
- cell_bias: float32 [624], replicated, may hold values from -4 to 4
Outputs:
- priors: float32 [32, 8, 624], P('patch', 'tm')
Inputs may be any that keep to these rules, and one draw needn't show every extreme that they name: `partners`: in each gate layer every patch has a partner other than itself, and the partner of the partner is the patch. Split the patches into aligned blocks of 4: no patch is paired within its own block, and a block pairs with exactly 4 other blocks, with exactly 1 of its patches in each. `gate_round`: gate layer g acts in one of the rounds g * 2 to (g + 1) * 2 - 1; the first gate layer acts in round 0 and the last in round 8 - 1.
All inputs are finite; a program needn't handle non-finite values. No bound on the sum of `bits` on one device may be relied on, other than what follows from the above.
Results may differ from a plain program's by a relative error of at most 0.0054.
Values may be sent and summed in bfloat16 or wider, within the bound.
No kernel may reach another device: no remote copies, remote signals or barrier semaphores. Data moves between devices by JAX's collectives and lax.ppermute only.
A program may use at most 64 MiB of HBM per device.

v0:
```python
import jax
import jax.numpy as jnp
import numpy as np
from jax import lax
from jax.sharding import PartitionSpec as P


def with_halo(block, sides, width):
    for axis, dim in sides:
        count = lax.axis_size(axis)
        forward = [(i, i + 1) for i in range(count - 1)]
        backward = [(target, source) for source, target in forward]
        low = lax.ppermute(
            lax.slice_in_dim(block, block.shape[dim] - width, None, axis=dim), axis, forward
        )
        high = lax.ppermute(lax.slice_in_dim(block, 0, width, axis=dim), axis, backward)
        block = jnp.concatenate([low, block, high], axis=dim)
    return block


def band_table(width_in, width_out):
    spread = np.arange(width_in)[None, :, None] - np.arange(width_out)[None, None, :]
    return (spread == np.arange(3)[:, None, None]).astype(np.float32)


def block_weights(kernel):
    chans = kernel.shape[-1]
    table = jnp.asarray(band_table(6, 4), jnp.bfloat16)
    full = jnp.einsum("wuv,abwio->abuivo", table, kernel, preferred_element_type=jnp.float32)
    return full.reshape(3, 3, 6 * chans, 4 * chans).astype(jnp.bfloat16)


def conv_layer(extended, weights, depth):
    chans = weights.shape[-1] // 4
    count, span, height, lanes = extended.shape
    block_groups = lanes // (4 * chans)
    padded = jnp.pad(extended, ((0, 0), (0, 0), (1, 1), (chans, chans)))
    stacked = jnp.stack(
        [
            padded[..., 4 * column_position * chans : (4 * column_position + 6) * chans]
            for column_position in range(block_groups)
        ],
        axis=3,
    )
    total = jnp.zeros((count, depth, height, block_groups, 4 * chans), jnp.float32)
    for time_tap in range(3):
        for row_tap in range(3):
            window = stacked[:, time_tap : time_tap + depth, row_tap : row_tap + height]
            total = total + jnp.einsum(
                "prhbk,kn->prhbn",
                window,
                weights[time_tap, row_tap],
                preferred_element_type=jnp.float32,
            )
    return total.reshape(count, depth, height, lanes)


def extend_rounds(activation_maps):
    return with_halo(activation_maps, (("tm", 1),), 1)


def couple(activation_maps, partner_row, gate_round, down, up_ctrl, up_targ):
    count, depth, height, lanes = activation_maps.shape
    chans = down.shape[0]
    width = lanes // chans
    devices = lax.axis_size("patch")
    capacity = max(1, 2 * count // devices)
    me = lax.axis_index("patch")
    local_moment = gate_round[0] - lax.axis_index("tm") * depth
    lattice_portion = lax.dynamic_index_in_dim(activation_maps, local_moment, 1, keepdims=False)
    identity = jnp.eye(width, dtype=jnp.bfloat16)
    down_full = jnp.kron(identity, down)
    ctrl_full = jnp.kron(identity, up_ctrl)
    targ_full = jnp.kron(identity, up_targ)
    ranks = jnp.arange(count)
    mine = lax.dynamic_slice_in_dim(partner_row, me * count, count)
    target_dev = mine // count
    preceding_cycle = ranks[None, :] < ranks[:, None]
    send_slots = jnp.sum((target_dev[None, :] == target_dev[:, None]) & preceding_cycle, axis=1)
    sender_mapping = (
        (jnp.arange(devices)[:, None, None] == target_dev[None, None, :])
        & (jnp.arange(capacity)[None, :, None] == send_slots[None, None, :])
    ).astype(jnp.bfloat16)
    owner_local = mine % count
    owner_rows = partner_row[target_dev[:, None] * count + ranks[None, :]]
    recv_slots = jnp.sum(
        (owner_rows // count == me) & (ranks[None, :] < owner_local[:, None]), axis=1
    )
    recv_table = (
        (jnp.arange(devices)[None, :, None] == target_dev[:, None, None])
        & (jnp.arange(capacity)[None, None, :] == recv_slots[:, None, None])
    ).astype(jnp.bfloat16)
    outgoing = jnp.einsum(
        "cjt,tqi->cjqi", sender_mapping, lattice_portion, preferred_element_type=jnp.float32
    ).astype(jnp.bfloat16)
    incoming = lax.all_to_all(outgoing, "patch", split_axis=0, concat_axis=0, tiled=True)
    mate_slab = jnp.einsum(
        "psc,schk->phk", recv_table, incoming, preferred_element_type=jnp.float32
    ).astype(jnp.bfloat16)
    latent_features = jnp.dot(mate_slab, down_full, preferred_element_type=jnp.float32).astype(
        jnp.bfloat16
    )
    control_qubit = (me * count + ranks < mine)[:, None, None]
    control_contribution = jnp.dot(latent_features, ctrl_full, preferred_element_type=jnp.float32)
    targ_term = jnp.dot(latent_features, targ_full, preferred_element_type=jnp.float32)
    updated = (
        lattice_portion.astype(jnp.float32)
        + jnp.where(control_qubit, control_contribution, targ_term)
    ).astype(jnp.bfloat16)
    return lax.dynamic_update_index_in_dim(activation_maps, updated, local_moment, 1)


def shards(
    bits,
    partners,
    gate_round,
    first_kernel,
    second_kernels,
    conv_bias,
    couple_down,
    couple_up,
    head,
    cell_bias,
):
    count, depth, height, width = bits.shape
    chans = first_kernel.shape[-1]
    events = bits.astype(jnp.bfloat16)
    table = jnp.asarray(band_table(width + 2, width), jnp.bfloat16)
    first_weights = jnp.einsum(
        "wuv,abwo->abuvo", table, first_kernel, preferred_element_type=jnp.float32
    )
    first_weights = first_weights.reshape(3, 3, width + 2, width * chans).astype(jnp.bfloat16)
    extended_events = with_halo(events, (("tm", 1),), 1)
    bordered_syndromes = jnp.pad(extended_events, ((0, 0), (0, 0), (1, 1), (1, 1)))
    first_total = jnp.zeros((count, depth, height, width * chans), jnp.float32)
    for time_tap in range(3):
        for row_tap in range(3):
            window = bordered_syndromes[:, time_tap : time_tap + depth, row_tap : row_tap + height]
            first_total = first_total + jnp.einsum(
                "prhu,un->prhn",
                window,
                first_weights[time_tap, row_tap],
                preferred_element_type=jnp.float32,
            )
    bias_one = jnp.tile(conv_bias[0], width)
    first = jax.nn.relu(first_total + bias_one).astype(jnp.bfloat16)
    partner_row = partners[0]
    coupled_one = couple(
        first, partner_row, gate_round, couple_down[0], couple_up[0, 0], couple_up[0, 1]
    )
    second_layer_weights = block_weights(second_kernels[0])
    total_two = conv_layer(extend_rounds(coupled_one), second_layer_weights, depth)
    second = (
        jax.nn.relu(total_two + jnp.tile(conv_bias[1], width)) + coupled_one.astype(jnp.float32)
    ).astype(jnp.bfloat16)
    linked_pair_output = couple(
        second, partner_row, gate_round, couple_down[1], couple_up[1, 0], couple_up[1, 1]
    )
    weights_three = block_weights(second_kernels[1])
    total_three = conv_layer(extend_rounds(linked_pair_output), weights_three, depth)
    third = jax.nn.relu(total_three + jnp.tile(conv_bias[2], width)) + linked_pair_output.astype(
        jnp.float32
    )
    readout = jnp.kron(jnp.eye(width, dtype=jnp.float32), head.astype(jnp.float32)[:, None])
    logits = jnp.dot(third, readout, precision=lax.Precision.HIGHEST) + cell_bias.reshape(
        height, width
    )
    return logits.reshape(count, depth, height * width)


def solution(mesh):
    in_specs = (
        P("patch", "tm", None, None),
        P("tm", None),
        P("tm"),
        P(),
        P(),
        P(),
        P(),
        P(),
        P(),
        P(),
    )
    out_specs = P("patch", "tm", None)
    return jax.shard_map(shards, mesh=mesh, in_specs=in_specs, out_specs=out_specs, check_vma=False)
```

profile of v0, /device:TPU:0, one launch (start us, length us, event | category | flops | bytes accessed | tf_op | source)
XLA Modules:
  0.0 120.9 jit_solution(12820019024356361579)
XLA Ops:
  0.0 1.1 copy.122
  1.1 5.0 %collective-permute-start = (bf16[4,1,26,24]{3,2,1,0:T(8,128)(2,1)S(1)}, bf16[4,1,26,24]{3,2,1,0:T(8,128)(2,1)S(1)}, u32[]{:S(2)}, u32[]{:S(2)}) collective-permute-start(bf16[4,1,26,24]{3,2,1,0:T(8,128)(2,1)S(1)} %get-tuple-element.33), channel_id=1, source_target_pairs={{0,1},{1,2},{2,3},{4,5},{5,6},{6,7},{8,9},{9,10},{10,11},{12,13},{... | collective-permute-start | bytes 14984 | tf_op jit(solution)/shard_map/ppermute | solution.py:13
  6.1 1.3 %collective-permute-start.1 = (bf16[4,1,26,24]{3,2,1,0:T(8,128)(2,1)S(1)}, bf16[4,1,26,24]{3,2,1,0:T(8,128)(2,1)S(1)}, u32[]{:S(2)}, u32[]{:S(2)}) collective-permute-start(bf16[4,1,26,24]{3,2,1,0:T(8,128)(2,1)S(1)} %get-tuple-element.34), channel_id=1, source_target_pairs={{1,0},{2,1},{3,2},{5,4},{6,5},{7,6},{9,8},{10,9},{11,10},{13,12},{... | collective-permute-start | bytes 14984 | tf_op jit(solution)/shard_map/ppermute | solution.py:16
  7.4 0.7 bitcast_compare_fusion
  8.6 1.3 %slice_bitcast_fusion.72 = (f32[32]{0:T(128)}, f32[32]{0:T(128)S(1)}, f32[32]{0:T(128)S(1)}) fusion(f32[3,32]{1,0:T(4,128)} %param.18), kind=kLoop, calls=%fused_computation.238 | loop fusion | bytes 768 | tf_op jit(solution)/shard_map/tile | solution.py:161
  9.9 0.7 gather_fusion
  10.8 2.0 %convert_bitcast_fusion.2 = bf16[3,3,26,24,32]{4,2,1,0,3:T(8,128)(2,1)} fusion(bf16[3,26,24,1,1]{1,0,4,3,2:T(4,128)(2,1)S(1)} %copy-done.9, bf16[3,3,3,32]{3,2,1,0:T(4,128)(2,1)S(1)} %copy-done), kind=kOutput, calls=%fused_computation.10 | convolution fusion | flops 1257984 | bytes 364896 | tf_op jit(solution)/shard_map/wuv,abwo->abuvo/dot_general | solution.py:129
  12.7 1.8 %broadcast_multiply_fusion.2 = (bf16[24,32,24,16]{1,0,3,2:T(8,128)(2,1)S(1)}, bf16[24,32,24,16]{1,0,3,2:T(8,128)(2,1)}) fusion(bf16[32,16]{0,1:T(8,128)(2,1)S(1)} %get-tuple-element.39, bf16[24,24]{0,1:T(8,128)(2,1)S(1)} %fusion.92, bf16[32,16]{0,1:T(8,128)(2,1)S(1)} %get-tuple-element.40), kind=kLoop, calls=%fused_computation.48 | loop fusion | flops 589824 | bytes 1182848 | tf_op jit(solution)/shard_map/jit(kron)/mul | solution.py:72
  14.5 3.8 %broadcast_multiply_fusion = (bf16[24,16,24,32]{3,2,1,0:T(8,128)(2,1)}, bf16[24,16,24,32]{3,2,1,0:T(8,128)(2,1)}, bf16[24,16,24,32]{3,2,1,0:T(8,128)(2,1)}, bf16[24,16,24,32]{3,2,1,0:T(8,128)(2,1)}) fusion(bf16[16,32]{1,0:T(8,128)(2,1)S(1)} %get-tuple-element.35, bf16[24,24]{1,0:T(8,128)(2,1)S(1)} %copy.129, bf16[16,32]{1,0:T(8,128)(2,1)S(1)} %get-tuple-element.36, ...), kind=kLoop, calls=%fused_computation.46 | loop fusion | flops 1179648 | bytes 2364544 | tf_op jit(solution)/shard_map/jit(kron)/mul | solution.py:74
  19.2 3.1 %copy.123 = bf16[3,3,26,24,32]{4,3,2,1,0:T(8,128)(2,1)} copy(bf16[3,3,26,24,32]{4,2,1,0,3:T(8,128)(2,1)} %convert_bitcast_fusion.2) | data formatting | bytes 718848 | tf_op jit(solution)/shard_map/convert_element_type | solution.py:132
  22.3 2.4 %convert_element_type.126 = bf16[3,3,26,768]{3,2,1,0:T(8,128)(2,1)S(1)} reshape(bf16[3,3,26,24,32]{4,3,2,1,0:T(8,128)(2,1)} %copy.123) | data formatting | bytes 718848 | tf_op jit(solution)/shard_map/convert_element_type | solution.py:132
  26.8 1.0 fusion.5
  28.3 0.9 copy.125
  29.1 3.7 %all-to-all-start = ((bf16[8,1,26,768]{3,2,1,0:T(8,128)(2,1)}), bf16[8,1,26,768]{3,2,1,0:T(8,128)(2,1)S(1)}, u32[]{:S(2)}, u32[]{:S(2)}) async-start(bf16[8,1,26,768]{3,2,1,0:T(8,128)(2,1)} %copy.125), calls=%async_computation | async-start | bytes 786432 | tf_op jit(solution)/shard_map/all_to_all | solution.py:96
  32.9 4.0 %mul.183 = bf16[768,384]{0,1:T(8,128)(2,1)} reshape(bf16[24,32,24,16]{1,0,3,2:T(8,128)(2,1)} %get-tuple-element.46) | data formatting | bytes 1179648 | tf_op jit(solution)/shard_map/jit(kron)/mul | solution.py:72
  37.0 4.0 %reshape.417 = bf16[384,768,1]{1,0,2:T(8,128)(2,1)} reshape(bf16[24,16,24,32]{3,2,1,0:T(8,128)(2,1)} %get-tuple-element.42) | data formatting | bytes 1179648 | tf_op jit(solution)/shard_map/jit(kron)/mul | solution.py:74
  41.0 4.0 %reshape.416 = bf16[384,768,1]{1,0,2:T(8,128)(2,1)} reshape(bf16[24,16,24,32]{3,2,1,0:T(8,128)(2,1)} %get-tuple-element.44) | data formatting | bytes 1179648 | tf_op jit(solution)/shard_map/jit(kron)/mul | solution.py:73
  45.0 1.8 %fusion.115 = (bf16[1,3,3,3,32,32]{5,4,3,2,1,0:T(8,128)(2,1)}, bf16[1,3,3,3,32,32]{5,4,3,2,1,0:T(8,128)(2,1)}) fusion(bf16[2,3,3,3,32,32]{5,4,3,2,1,0:T(8,128)(2,1)} %param.17), kind=kLoop, calls=%fused_computation.248 | loop fusion | bytes 221184 | tf_op jit(solution)/shard_map/slice | solution.py:159
  47.2 1.4 %convolution_convert_fusion.5 = bf16[4,26,384]{2,1,0:T(8,128)(2,1)S(1)} fusion(bf16[768,384]{0,1:T(8,128)(2,1)} %mul.183, bf16[4,26,768]{2,0,1:T(4,128)(2,1)S(1)} %convolution_convert_fusion.3), kind=kOutput, calls=%fused_computation.61 | convolution fusion | flops 61381632 | bytes 829440 | tf_op jit(solution)/shard_map/dot_general | solution.py:100
  48.6 1.4 %fusion.119 = f32[4,26,768]{2,1,0:T(8,128)S(1)} fusion(bf16[4,26,384]{2,1,0:T(8,128)(2,1)S(1)} %convolution_convert_fusion.5, bf16[384,768,1]{1,0,2:T(8,128)(2,1)} %reshape.416), kind=kOutput, calls=%fused_computation.252 | convolution fusion | flops 61341696 | bytes 989184 | tf_op jit(solution)/shard_map/dot_general | solution.py:104
  50.0 1.3 %fusion.15 = bf16[4,2,26,768]{3,2,1,0:T(8,128)(2,1)S(1)} fusion(bf16[4,2,26,768]{3,2,1,0:T(8,128)(2,1)S(1)} %fusion.5, s32[]{:T(128)S(6)} %select_n.73, f32[4,26,768]{2,1,0:T(8,128)S(1)} %fusion.119, bf16[4,26,384]{2,1,0:T(8,128)(2,1)S(1)} %convolution_convert_fusion.5, bf16[384,768,1]{1,0,2:T(8,128)(2,1)} %reshape.417, ...), kind=kOutput, calls=%fused_computation.59 | convolution fusion | flops 61661184 | bytes 1475076 | tf_op jit(solution)/shard_map/dot_general | solution.py:105
  51.3 4.6 %collective-permute-start.2 = (bf16[4,1,26,768]{3,2,1,0:T(8,128)(2,1)S(1)}, bf16[4,1,26,768]{3,2,1,0:T(8,128)(2,1)S(1)}, u32[]{:S(2)}, u32[]{:S(2)}) collective-permute-start(bf16[4,1,26,768]{3,2,1,0:T(8,128)(2,1)S(1)} %get-tuple-element.31), channel_id=1, source_target_pairs={{0,1},{1,2},{2,3},{4,5},{5,6},{6,7},{8,9},{9,10},{10,11},{12,13},{... | collective-permute-start | bytes 479240 | tf_op jit(solution)/shard_map/ppermute | solution.py:13
  55.9 1.5 %collective-permute-start.3 = (bf16[4,1,26,768]{3,2,1,0:T(8,128)(2,1)S(1)}, bf16[4,1,26,768]{3,2,1,0:T(8,128)(2,1)S(1)}, u32[]{:S(2)}, u32[]{:S(2)}) collective-permute-start(bf16[4,1,26,768]{3,2,1,0:T(8,128)(2,1)S(1)} %get-tuple-element.32), channel_id=1, source_target_pairs={{1,0},{2,1},{3,2},{5,4},{6,5},{7,6},{9,8},{10,9},{11,10},{13,12},{... | collective-permute-start | bytes 479240 | tf_op jit(solution)/shard_map/ppermute | solution.py:16
  57.4 1.1 convert_bitcast_fusion.1
  58.5 2.6 %copy.132 = bf16[3,3,6,32,4,32]{5,4,3,2,1,0:T(4,128)(2,1)} copy(bf16[3,3,6,32,4,32]{5,2,3,1,0,4:T(8,128)(2,1)S(1)} %convert_bitcast_fusion.1) | data formatting | bytes 884736 | tf_op jit(solution)/shard_map/convert_element_type | solution.py:30
  61.1 3.4 %convert_element_type.139 = bf16[3,3,192,128]{3,2,1,0:T(8,128)(2,1)} reshape(bf16[3,3,6,32,4,32]{5,4,3,2,1,0:T(4,128)(2,1)} %copy.132) | data formatting | bytes 884736 | tf_op jit(solution)/shard_map/convert_element_type | solution.py:30
  64.8 0.8 fusion.23
  65.8 1.7 %fusion.114 = (bf16[4,2,26,6,192]{4,2,1,0,3:T(8,128)(2,1)S(1)}, bf16[4,2,26,6,192]{4,2,1,0,3:T(8,128)(2,1)S(1)}, bf16[4,2,26,6,192]{4,2,1,0,3:T(8,128)(2,1)S(1)}...) fusion(bf16[4,4,28,6,192]{4,2,1,0,3:T(8,128)(2,1)S(1)} %fusion.62), kind=kLoop, calls=%fused_computation.247 | loop fusion | bytes 8626176 | tf_op jit(solution)/shard_map/slice | solution.py:48
  67.9 0.4 convolution_add_fusion.15
  68.3 0.4 convolution_add_fusion.14
  69.4 0.4 convolution_add_fusion.11
  69.7 0.4 convolution_add_fusion.10
  70.4 0.4 convolution_add_fusion.8
  70.8 1.3 %copy.197 = f32[4,2,26,6,128]{4,3,2,1,0:T(8,128)} copy(f32[4,2,26,6,128]{4,2,3,1,0:T(8,128)S(1)} %convolution_add_fusion.8) | data formatting | bytes 1277952 | tf_op jit(solution)/shard_map/reshape | solution.py:55
  72.1 2.2 %reshape.445 = f32[4,2,26,768]{3,2,1,0:T(8,128)} reshape(f32[4,2,26,6,128]{4,3,2,1,0:T(8,128)} %copy.197) | data formatting | bytes 1277952 | tf_op jit(solution)/shard_map/reshape | solution.py:55
  74.3 1.3 %add_convert_fusion = bf16[4,2,26,768]{3,2,1,0:T(8,128)(2,1)S(1)} fusion(bf16[4,2,26,768]{3,2,1,0:T(8,128)(2,1)S(1)} %fusion.15, f32[4,2,26,768]{3,2,1,0:T(8,128)} %reshape.445, f32[768]{0:T(1024)S(1)} %add.257), kind=kLoop, calls=%fused_computation.97 | loop fusion | flops 798720 | bytes 1281024 | tf_op jit(solution)/shard_map/convert_element_type | solution.py:155
  76.0 0.8 copy.145
  76.8 4.1 %all-to-all-start.1 = ((bf16[8,1,26,768]{3,2,1,0:T(8,128)(2,1)}), bf16[8,1,26,768]{3,2,1,0:T(8,128)(2,1)}, u32[]{:S(2)}, u32[]{:S(2)}) async-start(bf16[8,1,26,768]{3,2,1,0:T(8,128)(2,1)} %copy.145), calls=%async_computation.1 | async-start | bytes 786432 | tf_op jit(solution)/shard_map/all_to_all | solution.py:96
  81.0 0.7 add.270
  81.6 0.7 mul.208
  82.6 0.8 mul.206
  83.4 2.2 %mul.196 = bf16[768,384]{0,1:T(8,128)(2,1)} reshape(bf16[24,32,24,16]{1,0,3,2:T(8,128)(2,1)S(1)} %get-tuple-element.45) | data formatting | bytes 1179648 | tf_op jit(solution)/shard_map/jit(kron)/mul | solution.py:72
  85.6 3.4 %reshape.431 = bf16[384,768,1]{1,0,2:T(8,128)(2,1)S(1)} reshape(bf16[24,16,24,32]{3,2,1,0:T(8,128)(2,1)} %get-tuple-element.41) | data formatting | bytes 1179648 | tf_op jit(solution)/shard_map/jit(kron)/mul | solution.py:74
  89.0 2.2 %reshape.430 = bf16[384,768,1]{1,0,2:T(8,128)(2,1)} reshape(bf16[24,16,24,32]{3,2,1,0:T(8,128)(2,1)S(1)} %copy-done.3) | data formatting | bytes 1179648 | tf_op jit(solution)/shard_map/jit(kron)/mul | solution.py:73
  91.3 1.3 %convolution_convert_fusion.2 = bf16[4,26,768]{2,0,1:T(4,128)(2,1)S(1)} fusion(bf16[8,1,26,768]{3,2,1,0:T(8,128)(2,1)} %all-to-all-done.1, s32[4]{0:T(128)} %copy-done.14, pred[4]{0:T(512)(128)(4,1)} %copy-done.22), kind=kOutput, calls=%fused_computation.54 | convolution fusion | flops 1357888 | bytes 479252 | tf_op jit(solution)/shard_map/psc,schk->phk/dot_general | solution.py:97
  92.6 1.4 %convolution_convert_fusion.4 = bf16[4,26,384]{2,1,0:T(8,128)(2,1)S(1)} fusion(bf16[768,384]{0,1:T(8,128)(2,1)} %mul.196, bf16[4,26,768]{2,0,1:T(4,128)(2,1)S(1)} %convolution_convert_fusion.2), kind=kOutput, calls=%fused_computation.60 | convolution fusion | flops 61381632 | bytes 829440 | tf_op jit(solution)/shard_map/dot_general | solution.py:100
  94.0 1.4 %fusion.120 = f32[4,26,768]{2,1,0:T(8,128)S(1)} fusion(bf16[4,26,384]{2,1,0:T(8,128)(2,1)S(1)} %convolution_convert_fusion.4, bf16[384,768,1]{1,0,2:T(8,128)(2,1)} %reshape.430), kind=kOutput, calls=%fused_computation.253 | convolution fusion | flops 61341696 | bytes 989184 | tf_op jit(solution)/shard_map/dot_general | solution.py:104
  95.6 0.7 fusion.116
  96.3 5.1 %collective-permute-start.4 = (bf16[4,1,26,768]{3,2,1,0:T(8,128)(2,1)}, bf16[4,1,26,768]{3,2,1,0:T(8,128)(2,1)}, u32[]{:S(2)}, u32[]{:S(2)}) collective-permute-start(bf16[4,1,26,768]{3,2,1,0:T(8,128)(2,1)} %get-tuple-element.29), channel_id=1, source_target_pairs={{0,1},{1,2},{2,3},{4,5},{5,6},{6,7},{8,9},{9,10},{10,11},{12,13},{... | collective-permute-start | bytes 479240 | tf_op jit(solution)/shard_map/ppermute | solution.py:13
  101.4 1.5 %collective-permute-start.5 = (bf16[4,1,26,768]{3,2,1,0:T(8,128)(2,1)S(1)}, bf16[4,1,26,768]{3,2,1,0:T(8,128)(2,1)}, u32[]{:S(2)}, u32[]{:S(2)}) collective-permute-start(bf16[4,1,26,768]{3,2,1,0:T(8,128)(2,1)S(1)} %get-tuple-element.30), channel_id=1, source_target_pairs={{1,0},{2,1},{3,2},{5,4},{6,5},{7,6},{9,8},{10,9},{11,10},{13,12},{... | collective-permute-start | bytes 479240 | tf_op jit(solution)/shard_map/ppermute | solution.py:16
  103.0 1.1 convert_bitcast_fusion
  104.1 2.6 %copy.150 = bf16[3,3,6,32,4,32]{5,4,3,2,1,0:T(4,128)(2,1)} copy(bf16[3,3,6,32,4,32]{5,2,3,1,0,4:T(8,128)(2,1)S(1)} %convert_bitcast_fusion) | data formatting | bytes 884736 | tf_op jit(solution)/shard_map/convert_element_type | solution.py:30
  106.7 2.8 %convert_element_type.150 = bf16[3,3,192,128]{3,2,1,0:T(8,128)(2,1)S(1)} reshape(bf16[3,3,6,32,4,32]{5,4,3,2,1,0:T(4,128)(2,1)} %copy.150) | data formatting | bytes 884736 | tf_op jit(solution)/shard_map/convert_element_type | solution.py:30
  109.5 1.0 collective-permute-done.5
  110.4 1.9 %select_maximum_fusion = bf16[4,4,28,832]{3,2,1,0:T(8,128)(2,1)S(1)} fusion(bf16[4,1,26,768]{3,2,1,0:T(8,128)(2,1)} %collective-permute-done.5, bf16[4,2,26,768]{3,2,1,0:T(8,128)(2,1)S(1)} %fusion.13, bf16[4,1,26,768]{3,2,1,0:T(8,128)(2,1)} %collective-permute-done.4), kind=kLoop, calls=%fused_computation.63 | loop fusion | flops 7081984 | bytes 1384448 | tf_op jit(solution)/shard_map/concatenate | solution.py:17
  112.5 1.7 %fusion.113 = (bf16[4,2,26,6,192]{4,2,1,0,3:T(8,128)(2,1)S(1)}, bf16[4,2,26,6,192]{4,2,1,0,3:T(8,128)(2,1)S(1)}, bf16[4,2,26,6,192]{4,2,1,0,3:T(8,128)(2,1)S(1)}...) fusion(bf16[4,4,28,6,192]{4,2,1,0,3:T(8,128)(2,1)S(1)} %fusion.56), kind=kLoop, calls=%fused_computation.246 | loop fusion | bytes 8626176 | tf_op jit(solution)/shard_map/slice | solution.py:48
  114.6 0.4 convolution_add_fusion.7
  114.9 0.4 convolution_add_fusion.6
  115.3 0.4 convolution_add_fusion.5
  115.6 0.4 convolution_add_fusion.4
  116.4 0.4 convolution_add_fusion.2
  117.5 0.4 copy.199
  118.3 1.7 %convolution_add_fusion.24 = f32[4,2,26,24]{2,3,1,0:T(8,128)S(1)} fusion(bf16[4,2,26,768]{3,2,1,0:T(8,128)(2,1)S(1)} %fusion.13, f32[4,2,26,768]{3,2,1,0:T(8,128)S(1)} %reshape.448, f32[768]{0:T(1024)S(1)} %copy-done.11, f32[768,24]{0,1:T(8,128)S(1)} %copy-done.8, f32[26,24]{0,1:T(8,128)S(1)} %copy.162, f32[768]{0:T(1024)S(1)} %copy-done.12), kind=kOutput, calls=%fused_computation.62 | convolution fusion | flops 46668672 | bytes 1060800 | tf_op jit(solution)/shard_map/dot_general | solution.py:165
  120.1 0.7 reshape.392
  (119 shorter events, 8.6 us)
Async XLA Ops:
  0.0 10.7 %copy-start = (bf16[3,3,3,32]{3,2,1,0:T(4,128)(2,1)S(1)}, bf16[3,3,3,32]{3,2,1,0:T(4,128)(2,1)}, u32[]{:S(2)}) copy-start(bf16[3,3,3,32]{3,2,1,0:T(4,128)(2,1)} %param.16) | copy-start | bytes 5188
  0.0 10.7 %copy-start.9 = (bf16[3,26,24,1,1]{1,0,4,3,2:T(4,128)(2,1)S(1)}, bf16[3,26,24,1,1]{1,0,4,3,2:T(4,128)(2,1)}, u32[]{:S(2)}) copy-start(bf16[3,26,24,1,1]{1,0,4,3,2:T(4,128)(2,1)} %constant.97) | copy-start | bytes 11236
  0.0 9.9 %copy-start.2 = (s32[1,32]{1,0:T(1,128)S(1)}, s32[1,32]{1,0:T(1,128)}, u32[]{:S(2)}) copy-start(s32[1,32]{1,0:T(1,128)} %param.14) | copy-start | bytes 388
  0.0 10.7 %copy-start.15 = (bf16[2,32,16]{1,2,0:T(8,128)(2,1)S(1)}, bf16[2,32,16]{1,2,0:T(8,128)(2,1)}, u32[]{:S(2)}) copy-start(bf16[2,32,16]{1,2,0:T(8,128)(2,1)} %param.19) | copy-start | bytes 6148
  0.0 10.7 %copy-start.13 = (bf16[2,2,16,32]{3,2,1,0:T(8,128)(2,1)S(1)}, bf16[2,2,16,32]{3,2,1,0:T(8,128)(2,1)}, u32[]{:S(2)}) copy-start(bf16[2,2,16,32]{3,2,1,0:T(8,128)(2,1)} %param.20) | copy-start | bytes 12292
  1.1 23.6 %collective-permute-start = (bf16[4,1,26,24]{3,2,1,0:T(8,128)(2,1)S(1)}, bf16[4,1,26,24]{3,2,1,0:T(8,128)(2,1)S(1)}, u32[]{:S(2)}, u32[]{:S(2)}) collective-permute-start(bf16[4,1,26,24]{3,2,1,0:T(8,128)(2,1)S(1)} %get-tuple-element.33), channel_id=1, source_target_pairs={{0,1},{1,2},{2,3},{4,5},{5,6},{6,7},{8,9},{9,10},{10,11},{12,13},{... | collective-permute-start | bytes 14984 | tf_op jit(solution)/shard_map/ppermute | solution.py:13
  6.1 18.7 %collective-permute-start.1 = (bf16[4,1,26,24]{3,2,1,0:T(8,128)(2,1)S(1)}, bf16[4,1,26,24]{3,2,1,0:T(8,128)(2,1)S(1)}, u32[]{:S(2)}, u32[]{:S(2)}) collective-permute-start(bf16[4,1,26,24]{3,2,1,0:T(8,128)(2,1)S(1)} %get-tuple-element.34), channel_id=1, source_target_pairs={{1,0},{2,1},{3,2},{5,4},{6,5},{7,6},{9,8},{10,9},{11,10},{13,12},{... | collective-permute-start | bytes 14984 | tf_op jit(solution)/shard_map/ppermute | solution.py:16
  8.1 41.8 %copy-start.16 = (pred[4]{0:T(512)(128)(4,1)}, pred[4]{0:T(512)(128)(4,1)S(1)}, u32[]{:S(2)}) copy-start(pred[4]{0:T(512)(128)(4,1)S(1)} %get-tuple-element.5) | copy-start | bytes 16
  8.2 67.5 %copy-start.14 = (s32[4]{0:T(128)}, s32[4]{0:T(128)S(1)}, u32[]{:S(2)}) copy-start(s32[4]{0:T(128)S(1)} %get-tuple-element.8) | copy-start | bytes 52
  8.4 19.5 %copy-start.20 = (pred[4]{0:T(512)(128)(4,1)}, pred[4]{0:T(512)(128)(4,1)S(1)}, u32[]{:S(2)}) copy-start(pred[4]{0:T(512)(128)(4,1)S(1)} %broadcast_compare_fusion) | copy-start | bytes 16
  24.7 1.8 %copy-start.4 = (bf16[3,3,26,768]{3,2,1,0:T(8,128)(2,1)}, bf16[3,3,26,768]{3,2,1,0:T(8,128)(2,1)S(1)}, u32[]{:S(2)}) copy-start(bf16[3,3,26,768]{3,2,1,0:T(8,128)(2,1)S(1)} %convert_element_type.126) | copy-start | bytes 1078276
  29.1 17.7 %all-to-all-start = ((bf16[8,1,26,768]{3,2,1,0:T(8,128)(2,1)}), bf16[8,1,26,768]{3,2,1,0:T(8,128)(2,1)S(1)}, u32[]{:S(2)}, u32[]{:S(2)}) async-start(bf16[8,1,26,768]{3,2,1,0:T(8,128)(2,1)} %copy.125), calls=%async_computation | async-start | bytes 786432 | tf_op jit(solution)/shard_map/all_to_all | solution.py:96
  32.9 14.0 %copy-start.22 = (pred[4]{0:T(512)(128)(4,1)}, pred[4]{0:T(512)(128)(4,1)S(1)}, u32[]{:S(2)}) copy-start(pred[4]{0:T(512)(128)(4,1)S(1)} %broadcast_compare_fusion.1) | copy-start | bytes 16
  48.6 8.8 %copy-start.7 = (bf16[1,3,3,3,32,32]{5,4,3,2,1,0:T(8,128)(2,1)S(1)}, bf16[1,3,3,3,32,32]{5,4,3,2,1,0:T(8,128)(2,1)}, u32[]{:S(2)}) copy-start(bf16[1,3,3,3,32,32]{5,4,3,2,1,0:T(8,128)(2,1)} %get-tuple-element.28) | copy-start | bytes 165892
  48.6 8.8 %copy-start.10 = (bf16[3,6,4,1,1,1]{1,0,5,4,3,2:T(4,128)(2,1)S(1)}, bf16[3,6,4,1,1,1]{1,0,5,4,3,2:T(4,128)(2,1)}, u32[]{:S(2)}) copy-start(bf16[3,6,4,1,1,1]{1,0,5,4,3,2:T(4,128)(2,1)} %constant.98) | copy-start | bytes 436
  51.3 13.3 %collective-permute-start.2 = (bf16[4,1,26,768]{3,2,1,0:T(8,128)(2,1)S(1)}, bf16[4,1,26,768]{3,2,1,0:T(8,128)(2,1)S(1)}, u32[]{:S(2)}, u32[]{:S(2)}) collective-permute-start(bf16[4,1,26,768]{3,2,1,0:T(8,128)(2,1)S(1)} %get-tuple-element.31), channel_id=1, source_target_pairs={{0,1},{1,2},{2,3},{4,5},{5,6},{6,7},{8,9},{9,10},{10,11},{12,13},{... | collective-permute-start | bytes 479240 | tf_op jit(solution)/shard_map/ppermute | solution.py:13
  55.9 8.9 %collective-permute-start.3 = (bf16[4,1,26,768]{3,2,1,0:T(8,128)(2,1)S(1)}, bf16[4,1,26,768]{3,2,1,0:T(8,128)(2,1)S(1)}, u32[]{:S(2)}, u32[]{:S(2)}) collective-permute-start(bf16[4,1,26,768]{3,2,1,0:T(8,128)(2,1)S(1)} %get-tuple-element.32), channel_id=1, source_target_pairs={{1,0},{2,1},{3,2},{5,4},{6,5},{7,6},{9,8},{10,9},{11,10},{13,12},{... | collective-permute-start | bytes 479240 | tf_op jit(solution)/shard_map/ppermute | solution.py:16
  65.8 1.7 %copy-start.5 = (bf16[3,3,192,128]{3,2,1,0:T(8,128)(2,1)S(1)}, bf16[3,3,192,128]{3,2,1,0:T(8,128)(2,1)}, u32[]{:S(2)}) copy-start(bf16[3,3,192,128]{3,2,1,0:T(8,128)(2,1)} %convert_element_type.139) | copy-start | bytes 1327108
  72.1 3.5 %copy-start.21 = (pred[4]{0:T(512)(128)(4,1)S(1)}, pred[4]{0:T(512)(128)(4,1)}, u32[]{:S(2)}) copy-start(pred[4]{0:T(512)(128)(4,1)} %copy-done.20) | copy-start | bytes 16
  74.3 6.6 %copy-start.19 = (f32[32]{0:T(128)S(1)}, f32[32]{0:T(128)}, u32[]{:S(2)}) copy-start(f32[32]{0:T(128)} %get-tuple-element.47) | copy-start | bytes 388
  74.3 7.3 %copy-start.23 = (bf16[32]{0:T(256)(128)(2,1)S(1)}, bf16[32]{0:T(256)(128)(2,1)}, u32[]{:S(2)}) copy-start(bf16[32]{0:T(256)(128)(2,1)} %param.21) | copy-start | bytes 196
  74.3 8.0 %copy-start.18 = (f32[624]{0:T(1024)S(1)}, f32[624]{0:T(1024)}, u32[]{:S(2)}) copy-start(f32[624]{0:T(1024)} %param.22) | copy-start | bytes 7492
  76.8 14.4 %all-to-all-start.1 = ((bf16[8,1,26,768]{3,2,1,0:T(8,128)(2,1)}), bf16[8,1,26,768]{3,2,1,0:T(8,128)(2,1)}, u32[]{:S(2)}, u32[]{:S(2)}) async-start(bf16[8,1,26,768]{3,2,1,0:T(8,128)(2,1)} %copy.145), calls=%async_computation.1 | async-start | bytes 786432 | tf_op jit(solution)/shard_map/all_to_all | solution.py:96
  85.6 3.4 %copy-start.3 = (bf16[24,16,24,32]{3,2,1,0:T(8,128)(2,1)S(1)}, bf16[24,16,24,32]{3,2,1,0:T(8,128)(2,1)}, u32[]{:S(2)}) copy-start(bf16[24,16,24,32]{3,2,1,0:T(8,128)(2,1)} %get-tuple-element.43) | copy-start | bytes 1769476
  91.2 4.1 %copy-start.17 = (pred[4]{0:T(512)(128)(4,1)S(1)}, pred[4]{0:T(512)(128)(4,1)}, u32[]{:S(2)}) copy-start(pred[4]{0:T(512)(128)(4,1)} %copy-done.16) | copy-start | bytes 16
  94.0 9.0 %copy-start.6 = (bf16[1,3,3,3,32,32]{5,4,3,2,1,0:T(8,128)(2,1)S(1)}, bf16[1,3,3,3,32,32]{5,4,3,2,1,0:T(8,128)(2,1)}, u32[]{:S(2)}) copy-start(bf16[1,3,3,3,32,32]{5,4,3,2,1,0:T(8,128)(2,1)} %get-tuple-element.27) | copy-start | bytes 165892
  96.3 13.1 %collective-permute-start.4 = (bf16[4,1,26,768]{3,2,1,0:T(8,128)(2,1)}, bf16[4,1,26,768]{3,2,1,0:T(8,128)(2,1)}, u32[]{:S(2)}, u32[]{:S(2)}) collective-permute-start(bf16[4,1,26,768]{3,2,1,0:T(8,128)(2,1)} %get-tuple-element.29), channel_id=1, source_target_pairs={{0,1},{1,2},{2,3},{4,5},{5,6},{6,7},{8,9},{9,10},{10,11},{12,13},{... | collective-permute-start | bytes 479240 | tf_op jit(solution)/shard_map/ppermute | solution.py:13
  101.4 9.0 %collective-permute-start.5 = (bf16[4,1,26,768]{3,2,1,0:T(8,128)(2,1)S(1)}, bf16[4,1,26,768]{3,2,1,0:T(8,128)(2,1)}, u32[]{:S(2)}, u32[]{:S(2)}) collective-permute-start(bf16[4,1,26,768]{3,2,1,0:T(8,128)(2,1)S(1)} %get-tuple-element.30), channel_id=1, source_target_pairs={{1,0},{2,1},{3,2},{5,4},{6,5},{7,6},{9,8},{10,9},{11,10},{13,12},{... | collective-permute-start | bytes 479240 | tf_op jit(solution)/shard_map/ppermute | solution.py:16
  117.4 0.9 copy-start.8
  117.4 0.9 copy-start.11
  117.4 0.9 copy-start.12
  117.5 3.4 %copy-start.1 = (bf16[3,3,3,32]{3,2,1,0:T(4,128)(2,1)S(1)}, bf16[3,3,3,32]{3,2,1,0:T(4,128)(2,1)}, u32[]{:S(2)}) copy-start(bf16[3,3,3,32]{3,2,1,0:T(4,128)(2,1)} %param.16) | copy-start | bytes 5188
where the time goes:
time: 122 us; the launch traced here: 121 us
  local copies, waits for them, and re-layouts  56 us (46%)
  starting transfers between devices  26.7 us (22%)
  matrix products  24.5 us (20%)
  other arithmetic  10.9 us (9%)
  between operations  1.48 us (1%)
  waiting for transfers between devices  1.24 us (1%)
    ppermute x3, starting transfers between devices, with_halo(): lax.ppermute(lax.slice_in_dim(block, block.shape[dim] - width, None, axis...  14.6 us
    convert_element_type x4, local copies, waits for them, and re-layouts, block_weights(): return full.reshape(3, 3, 6 * chans, 4 * chans).astype(jnp.bfloat16)  11.5 us
    all_to_all x2, starting transfers between devices, couple(): lax.all_to_all(outgoing, 'patch', split_axis=0, concat_axis=0, tiled=True)  7.81 us
    mul x3, local copies, waits for them, and re-layouts, couple(): targ_full = jnp.kron(identity, up_targ)  7.46 us
    dot_general x18, matrix products, conv_layer(): jnp.einsum('prhbk,kn->prhbn', window, weights[time_tap, row_tap], preferr...  6.37 us
    mul x3, local copies, waits for them, and re-layouts, couple(): down_full = jnp.kron(identity, down)  6.25 us
    mul x2, local copies, waits for them, and re-layouts, couple(): ctrl_full = jnp.kron(identity, up_ctrl)  6.24 us
    convert_element_type x2, local copies, waits for them, and re-layouts, shards(): first_weights.reshape(3, 3, width + 2, width * chans).astype(jnp.bfloat16)  5.52 us
  transfers between devices with their start and end apart: 8, of which 2 were waited for; matrix products, arithmetic and copies ran while one was open for 45% of the time, Pallas kernels for 0%

commit v1 on v0

v1 whole, which is shorter than its diff:
```python
import functools

import jax
import jax.numpy as jnp
from jax import lax
from jax.experimental import pallas as pl
from jax.experimental.pallas import tpu as pltpu
from jax.sharding import PartitionSpec as P

F32 = jnp.float32
BF16 = jnp.bfloat16
LANES = 128
COUNT = 4
DEPTH = 2
HEIGHT = 26
WIDTH = 24
CHANS = 32
WINDOW = 6
SLOTS = 8
BLOCKS = WIDTH // WINDOW
WIDE = SLOTS * CHANS
FLAT = 640
OWN, MATE, UNITS = 24, 16, 96
HALF = HEIGHT // 2


def iota(shape, dim):
    return lax.broadcasted_iota(jnp.int32, shape, dim)


def rounded(x):
    return x.astype(BF16).astype(F32)


def dot(a, b):
    return jnp.dot(a, b, preferred_element_type=F32)


def pack_kernel(bits_ref, partners_ref, gate_ref, out_ref):
    units = COUNT * DEPTH
    bits = bits_ref[...].reshape(units, HEIGHT, WIDTH).astype(F32)
    rows = [bits[:, y, :] for y in range(HEIGHT)]
    flat = jnp.concatenate(rows + [jnp.zeros((units, FLAT - HEIGHT * WIDTH), F32)], axis=1)
    out_ref[:, :FLAT] = flat.astype(BF16)
    patches = partners_ref.shape[1]
    names = partners_ref[...].astype(F32)
    if patches < LANES:
        names = jnp.concatenate([names, jnp.full((1, LANES - patches), -1.0, F32)], axis=1)
    moment = jnp.full((1, LANES), gate_ref[0], jnp.int32).astype(F32)
    sub = iota((units, LANES), 0)
    out_ref[:, FLAT:] = jnp.where(sub == 0, names, jnp.where(sub == 1, moment, 0.0)).astype(BF16)


def weights_kernel(
    first_ref, second_ref, bias_ref, down_ref, up_ref, head_ref,
    wf_ref, w2_ref, w3_ref, dn_ref, un_ref, rd_ref, bs_ref, scr_ref,
):
    total = BLOCKS * WIDE
    spread = (iota((CHANS, WIDE), 1) % CHANS == iota((CHANS, WIDE), 0)).astype(BF16)
    slot = iota((CHANS, WIDE), 1) // CHANS
    inner = (slot >= 1) & (slot <= WINDOW)
    for layer, w_ref in enumerate((w2_ref, w3_ref)):
        for tap in range(9):
            base = (layer * 27 + tap * 3) * CHANS
            tiled = dot(second_ref[base : base + 3 * CHANS, :], spread)
            for kc in range(SLOTS):
                block = jnp.zeros((CHANS, WIDE), F32)
                for dc in range(3):
                    block = jnp.where(
                        inner & (slot == kc - dc + 1), tiled[dc * CHANS : (dc + 1) * CHANS], block
                    )
                w_ref[tap * WIDE + kc * CHANS : tap * WIDE + (kc + 1) * CHANS, :] = block.astype(BF16)
    across = (iota((CHANS, total), 1) % CHANS == iota((CHANS, total), 0)).astype(BF16)
    taps = dot(first_ref[...], across)
    lane = iota((WIDTH, total), 1)
    column = (lane // WIDE) * WINDOW - 1 + (lane % WIDE) // CHANS
    real = (column >= 0) & (column < WIDTH)
    offset = iota((WIDTH, total), 0) - column + 1
    for pair in range(9):
        block = jnp.zeros((WIDTH, total), F32)
        for dc in range(3):
            block = jnp.where(real & (offset == dc), taps[pair * 3 + dc : pair * 3 + dc + 1, :], block)
        scr_ref[pair * WIDTH : (pair + 1) * WIDTH, :] = block
    scr_ref[9 * WIDTH :, :] = jnp.zeros((WIDE - 9 * WIDTH, total), F32)
    wf_ref[...] = scr_ref[...].astype(BF16)
    latent = down_ref.shape[1]
    low = SLOTS * latent
    thin = (iota((latent, low), 1) % latent == iota((latent, low), 0)).astype(BF16)
    for layer in range(2):
        tiled = dot(down_ref[layer * CHANS : (layer + 1) * CHANS, :], thin)
        for kc in range(SLOTS):
            keep = iota((CHANS, low), 1) // latent == kc
            dn_ref[layer * WIDE + kc * CHANS : layer * WIDE + (kc + 1) * CHANS, :] = jnp.where(
                keep, tiled, 0.0
            ).astype(BF16)
        for role in range(2):
            at = (layer * 2 + role) * latent
            tiled = dot(up_ref[at : at + latent, :], spread)
            for kc in range(SLOTS):
                keep = iota((latent, WIDE), 1) // CHANS == kc
                top = (layer * 2 + role) * low + kc * latent
                un_ref[top : top + latent, :] = jnp.where(keep, tiled, 0.0).astype(BF16)
    row = iota((total, CHANS), 0)
    chosen = jnp.where(row % CHANS == iota((total, CHANS), 1), head_ref[...].astype(F32), 0.0)
    values = dot(chosen.astype(BF16), jnp.ones((CHANS, LANES), BF16))
    row = iota((total, LANES), 0)
    place = (row % WIDE) // CHANS
    target = (row // WIDE) * WINDOW - 1 + place
    keep = (place >= 1) & (place <= WINDOW) & (target == iota((total, LANES), 1))
    rd_ref[...] = jnp.where(keep, values, 0.0).astype(BF16)
    biases = jnp.dot(
        bias_ref[...], across.astype(F32), preferred_element_type=F32, precision=lax.Precision.HIGHEST
    )
    lane = iota((8, total), 1)
    place = (lane % WIDE) // CHANS
    column = (lane // WIDE) * WINDOW - 1 + place
    real = (column >= 0) & (column < WIDTH)
    inside = (place >= 1) & (place <= WINDOW)
    top = iota((8, total), 0) == 0
    keep = (top & real) | (~top & inside)
    bs_ref[...] = jnp.where(keep, biases, 0.0)


def window_rows(gathered, y, lane):
    start = WIDTH * (y - 1)
    length = 3 * WIDTH
    tiles = [None, None]
    for dt in range(3):
        begin = length * dt
        shift = begin - start
        for src in range(FLAT // LANES):
            lo = max(start, 0, src * LANES)
            hi = min(start + length, FLAT, (src + 1) * LANES)
            if lo >= hi:
                continue
            source = gathered[dt][:, src * LANES : (src + 1) * LANES]
            turned = pltpu.roll(source, shift % LANES, 1) if shift % LANES else source
            for dst in range(2):
                a = max(lo + shift, dst * LANES) - dst * LANES
                b = min(hi + shift, (dst + 1) * LANES) - dst * LANES
                if a >= b:
                    continue
                old = jnp.zeros_like(turned) if tiles[dst] is None else tiles[dst]
                tiles[dst] = jnp.where((lane >= a) & (lane < b), turned, old)
    return tiles


def main_kernel(
    sizes, all_ref, meta_ref, wf_ref, w2_ref, w3_ref, dn_ref, un_ref, rd_ref, bs_ref, cell_ref,
    out_ref, x_ref, f_ref, s_ref, c2_ref, s3_ref,
):
    devices, steps, exact = sizes
    near = meta_ref.shape[0] // 8
    me = lax.axis_index("patch")
    now = lax.axis_index("tm")
    sub = iota((8, LANES), 0)
    low_half = sub < 4

    names, moments = [], []
    for j in range(3):
        there = now - 1 + j
        valid = (there >= 0) & (there < steps)
        safe = jnp.clip(there, 0, steps - 1)
        block = (safe ^ now) if exact else (2, 0, 1)[j]
        tile = meta_ref[pl.ds(pl.multiple_of(block * 8, 8), 8), :].astype(F32).astype(jnp.int32)
        names.append(jnp.where(valid, tile[0:1, :], -1))
        moments.append(jnp.broadcast_to(jnp.where(valid, tile[1:2, :], -1000), (8, LANES)))
    first_round = 2 * now - 2
    own_patch = COUNT * me + sub % COUNT

    def pair(parts):
        return jnp.concatenate(
            [jnp.where(low_half, parts[0], parts[1]), jnp.where(low_half, parts[1], parts[2])], axis=0
        )

    hot = [(jnp.broadcast_to(names[j], (8, LANES)) == own_patch).astype(F32) for j in range(3)]
    hot24 = jnp.concatenate(hot, axis=0).astype(BF16)
    hot16f = pair(hot)
    hot16 = hot16f.astype(BF16)
    square = iota((LANES, LANES), 0)
    even = moments[1] == 2 * now
    other = jnp.where(even[0:1, :], names[0], names[2])
    perm_one = (square == names[1]).astype(BF16)
    perm_other = (square == other).astype(BF16)
    middle = (iota((16, LANES), 0) >= 4) & (iota((16, LANES), 0) < 12)
    hot_far = jnp.where(middle, dot(hot16, perm_other), dot(hot16, perm_one))
    hots = jnp.concatenate([hot24, hot_far.astype(BF16), hot16], axis=0)
    index = dot(hots, square.astype(F32).astype(BF16)).astype(jnp.int32)
    mate24, far16, mate16 = index[0:24], index[24:40], index[40:56]
    own24 = jnp.concatenate([own_patch] * 3, axis=0)
    own16 = jnp.concatenate([own_patch] * 2, axis=0)

    moment24 = jnp.concatenate(moments, axis=0)
    moment16 = pair(moments)
    round24 = first_round + iota((24, LANES), 0) // 4
    round16 = first_round + 1 + iota((16, LANES), 0) // 4
    last = DEPTH * steps - 1
    step_far = pair([jnp.full((8, LANES), 1, jnp.int32), jnp.where(even, -1, 1), jnp.full((8, LANES), -1, jnp.int32)])
    moment_far = pair([moments[1], jnp.where(even, moments[0], moments[2]), moments[1]])
    touches = moment_far == moment16 + step_far
    far_low = touches & (step_far < 0)
    far_high = touches & (step_far > 0)

    columns = all_ref.shape[0]
    col = iota((1, columns), 1)
    block = col // (8 * near)
    half = devices // 2
    source = me ^ (2 * (block % half) + block // half) if devices > 1 else me + 0 * block
    patch_of = COUNT * source + (col % 8) // DEPTH
    step = (col // 8) % near
    if exact:
        time_of = now ^ step
    else:
        time_of = now + jnp.where(step == 1, 1, jnp.where(step == 2, -1, jnp.where(step == 3, 2, jnp.where(step == 4, -2, 0))))
    round_of = DEPTH * time_of + col % DEPTH
    expand = (iota((LANES, columns), 0) == patch_of).astype(BF16)
    spread = dot(hots, expand)

    def lanes_of(x):
        return jnp.broadcast_to(x[:, :1], (x.shape[0], columns))

    is_own = (patch_of == lanes_of(own24)).astype(F32)
    patch_sel = jnp.concatenate(
        [is_own, spread[0:24], spread[24:40], spread[40:56], spread[40:56]], axis=0
    )
    want = jnp.concatenate(
        [
            lanes_of(round24),
            lanes_of(moment24),
            lanes_of(moment16 + step_far),
            lanes_of(moment16 - 1),
            lanes_of(moment16 + 1),
        ],
        axis=0,
    )
    gathered = []
    for dt in range(3):
        choose = jnp.where(round_of == want + (dt - 1), patch_sel, 0.0).astype(BF16)
        gathered.append(dot(choose, all_ref[...]))
    lane = iota((UNITS, LANES), 1)
    for y in range(HEIGHT):
        tiles = window_rows(gathered, y, lane)
        x_ref[y * UNITS : (y + 1) * UNITS, :] = jnp.concatenate(tiles, axis=1).astype(BF16)

    s_ref[:, 0:32, :] = jnp.zeros((3, 32, WIDE), BF16)
    s_ref[:, 27 * 32 :, :] = jnp.zeros((3, 32, WIDE), BF16)

    def wide(mask):
        return jnp.concatenate([mask.astype(jnp.int32)] * 2, axis=1) != 0

    ctrl_up = jnp.concatenate([mate24 - own24, own16 - mate16, far16 - mate16], axis=0) > 0
    gate24 = wide(round24 == moment24)
    gate16 = wide(round16 == moment16)
    ok24 = wide((round24 >= 0) & (round24 <= last))
    ok16 = wide((round16 >= 0) & (round16 <= last))
    ok_low = wide((moment16 - 1 >= 0) & (moment16 - 1 <= last))
    ok_high = wide((moment16 + 1 >= 0) & (moment16 + 1 <= last))
    far_low, far_high = wide(far_low), wide(far_high)
    ctrl_own16 = own16 < mate16
    at_moment = round24 == moment24

    def swap(x):
        return pltpu.roll(x, 4, 0)

    def body(b, carry):
        lanes = pl.ds(pl.multiple_of(b * WIDE, WIDE), WIDE)
        bias1 = bs_ref[0:1, lanes]
        bias2 = bs_ref[1:2, lanes]
        total = dot(x_ref[...], wf_ref[:, lanes])
        f_ref[...] = rounded(jnp.maximum(total + bias1, 0.0)).reshape(HEIGHT, UNITS, WIDE)
        packed = f_ref[:, 0:64, :].reshape(HEIGHT * 64, WIDE).astype(BF16)
        latent = rounded(dot(packed, dn_ref[0:WIDE, :])).reshape(HEIGHT, 64, LANES)
        rows = []
        for y in range(HEIGHT):
            lat = latent[y]
            mine = [lat[8 * j : 8 * j + 8] for j in range(3)]
            mine = [jnp.where(at_moment[8 * j : 8 * j + 8], mine[j], swap(mine[j])) for j in range(3)]
            rows.append(jnp.concatenate([lat[24:48], pair(mine), lat[48:64]], axis=0))
        given = jnp.stack(rows, axis=0)
        both = jnp.concatenate(
            [jnp.where(ctrl_up, given, 0.0), jnp.where(ctrl_up, 0.0, given)], axis=2
        ).reshape(HEIGHT * 56, WIDE)
        added = dot(both.astype(BF16), un_ref[0:WIDE, :]).reshape(HEIGHT, 56, WIDE)
        half_mask = wide(low_half)
        for y in range(HEIGHT):
            here = f_ref[y]
            add = added[y]
            own = rounded(here[0:24] + jnp.where(gate24, add[0:24], 0.0))
            own = jnp.where(ok24, own, 0.0)
            m = [here[24 + 8 * j : 32 + 8 * j] for j in range(3)]
            mid = jnp.concatenate(
                [jnp.where(half_mask, m[0], m[1]), jnp.where(half_mask, m[1], m[2])], axis=0
            )
            mid = rounded(mid + add[24:40])
            far = add[40:56]
            lower = jnp.where(ok_low, rounded(here[64:80] + jnp.where(far_low, far, 0.0)), 0.0)
            upper = jnp.where(ok_high, rounded(here[80:96] + jnp.where(far_high, far, 0.0)), 0.0)
            turned = [swap(own[8 * j : 8 * j + 8]) for j in range(3)]
            center = jnp.concatenate(
                [jnp.where(half_mask, turned[0], turned[1]), jnp.where(half_mask, turned[1], turned[2])], axis=0
            )
            top = (y + 1) * 32
            s_ref[0, top : top + 32, :] = jnp.concatenate([own[0:16], lower], axis=0).astype(BF16)
            s_ref[1, top : top + 32, :] = jnp.concatenate([center, mid], axis=0).astype(BF16)
            s_ref[2, top : top + 32, :] = jnp.concatenate([own[8:24], upper], axis=0).astype(BF16)
        size = HEIGHT * 32
        acc = jnp.zeros((size, WIDE), F32)
        for tap in range(9):
            dt, dr = divmod(tap, 3)
            acc = acc + dot(
                s_ref[dt, dr * 32 : dr * 32 + size, :], w2_ref[tap * WIDE : (tap + 1) * WIDE, :]
            )
        second = jnp.maximum(acc + bias2, 0.0) + s_ref[1, 32 : 32 + size, :].astype(F32)
        second = second.reshape(HEIGHT, 32, WIDE)
        mates = second[:, 16:32, :].reshape(HEIGHT * 16, WIDE).astype(BF16)
        latent = rounded(dot(mates, dn_ref[WIDE:, :])).reshape(HEIGHT, 16, LANES)
        both = jnp.concatenate(
            [jnp.where(ctrl_own16, latent, 0.0), jnp.where(ctrl_own16, 0.0, latent)], axis=2
        ).reshape(HEIGHT * 16, WIDE)
        added = dot(both.astype(BF16), un_ref[WIDE:, :]).reshape(HEIGHT, 16, WIDE)
        two = rounded(rounded(second[:, 0:16, :]) + jnp.where(gate16, added, 0.0))
        c2_ref[b] = jnp.where(ok16, two, 0.0)
        return carry

    lax.fori_loop(0, BLOCKS, body, 0)

    lane8 = iota((8, LANES), 1)

    def placed(y, dt):
        if y < 0 or y >= HEIGHT:
            return jnp.zeros((8, BLOCKS * WIDE), F32)
        tiles = []
        for b in range(BLOCKS):
            for t in range(2):
                group = c2_ref[b, y, :, t * LANES : (t + 1) * LANES]
                if t == 0:
                    old = pltpu.roll(c2_ref[b - 1, y, :, LANES:], 64, 1) if b else jnp.zeros((16, LANES), F32)
                    group = jnp.where(iota((16, LANES), 1) < CHANS, old, group)
                else:
                    old = pltpu.roll(c2_ref[b + 1, y, :, :LANES], 64, 1) if b + 1 < BLOCKS else jnp.zeros((16, LANES), F32)
                    group = jnp.where(iota((16, LANES), 1) >= LANES - CHANS, old, group)
                if dt == 0:
                    group = group[0:8]
                elif dt == 2:
                    group = group[8:16]
                else:
                    group = jnp.where(low_half, swap(group[0:8]), swap(group[8:16]))
                tiles.append(group)
        return jnp.concatenate(tiles, axis=1)

    for dt in range(3):
        for r in range(HALF + 2):
            s3_ref[dt, r * 16 : (r + 1) * 16, :] = jnp.concatenate(
                [placed(r - 1, dt), placed(r + HALF - 1, dt)], axis=0
            ).astype(BF16)

    size = HALF * 16
    logits = jnp.zeros((size, LANES), F32)
    for b in range(BLOCKS):
        lanes = slice(b * WIDE, (b + 1) * WIDE)
        acc = jnp.zeros((size, WIDE), F32)
        for tap in range(9):
            dt, dr = divmod(tap, 3)
            acc = acc + dot(
                s3_ref[dt, dr * 16 : dr * 16 + size, lanes], w3_ref[tap * WIDE : (tap + 1) * WIDE, :]
            )
        third = jnp.maximum(acc + bs_ref[2:3, lanes], 0.0) + s3_ref[1, 16 : 16 + size, lanes].astype(F32)
        high = third.astype(BF16)
        rest = (third - high.astype(F32)).astype(BF16)
        logits = logits + dot(high, rd_ref[lanes, :]) + dot(rest, rd_ref[lanes, :])
    logits = logits.reshape(HALF, 16, LANES)
    flat = [jnp.zeros((8, LANES), F32) for _ in range(FLAT // LANES)]
    for y in range(HEIGHT):
        row = logits[y % HALF, (y // HALF) * 8 : (y // HALF) * 8 + 8]
        begin = y * WIDTH
        turned = pltpu.roll(row, begin % LANES, 1) if begin % LANES else row
        for dst in range(FLAT // LANES):
            a = max(begin, dst * LANES) - dst * LANES
            e = min(begin + WIDTH, (dst + 1) * LANES) - dst * LANES
            if a < e:
                flat[dst] = jnp.where((lane8 >= a) & (lane8 < e), turned, flat[dst])
    flat = jnp.concatenate(flat, axis=1)[:, : HEIGHT * WIDTH] + cell_ref[...]
    for j in range(DEPTH):
        for p in range(COUNT):
            out_ref[p, j : j + 1, :] = flat[4 * j + p : 4 * j + p + 1, :]


def swapped(block, axis, mask):
    count = lax.axis_size(axis)
    return lax.ppermute(block, axis, [(i, i ^ mask) for i in range(count)])


def shifted(block, axis, offset):
    count = lax.axis_size(axis)
    return lax.ppermute(block, axis, [(i, i - offset) for i in range(count) if 0 <= i - offset < count])


def shards(
    bits, partners, gate_round, first_kernel, second_kernels, conv_bias, couple_down, couple_up, head, cell_bias
):
    devices, steps = lax.axis_size("patch"), lax.axis_size("tm")
    latent = couple_down.shape[-1]
    total = BLOCKS * WIDE
    vmem = pl.BlockSpec(memory_space=pltpu.VMEM)
    smem = pl.BlockSpec(memory_space=pltpu.SMEM)
    mine = pl.pallas_call(
        pack_kernel,
        out_shape=jax.ShapeDtypeStruct((8, FLAT + LANES), BF16),
        in_specs=[vmem, vmem, smem],
        out_specs=vmem,
        name="pack",
    )(bits, partners, gate_round)

    exact = steps <= 4
    if exact:
        blocks = [mine] + [
            lax.ppermute(mine, "tm", [(i, i ^ k) for i in range(steps) if abs(i - (i ^ k)) <= 2])
            for k in range(1, steps)
        ]
    else:
        blocks = [mine] + [shifted(mine, "tm", k) for k in (1, -1, 2, -2)]
    near = jnp.concatenate(blocks, axis=0)
    meta = near[:, FLAT:]
    every = near[:, :FLAT]
    parts = [every] + [swapped(every, "patch", 2 * m) for m in range(1, devices // 2)]
    every = jnp.concatenate(parts, axis=0)
    every = jnp.concatenate([every, swapped(every, "patch", 1)], axis=0)

    weights = pl.pallas_call(
        weights_kernel,
        out_shape=[
            jax.ShapeDtypeStruct((WIDE, total), BF16),
            jax.ShapeDtypeStruct((9 * WIDE, WIDE), BF16),
            jax.ShapeDtypeStruct((9 * WIDE, WIDE), BF16),
            jax.ShapeDtypeStruct((2 * WIDE, SLOTS * latent), BF16),
            jax.ShapeDtypeStruct((4 * SLOTS * latent, WIDE), BF16),
            jax.ShapeDtypeStruct((total, LANES), BF16),
            jax.ShapeDtypeStruct((8, total), F32),
        ],
        in_specs=[vmem] * 6,
        out_specs=[vmem] * 7,
        scratch_shapes=[pltpu.VMEM((WIDE, total), F32)],
        cost_estimate=pl.CostEstimate(flops=10**9, bytes_accessed=10**7, transcendentals=0),
        name="weights",
    )(
        first_kernel.reshape(27, CHANS),
        second_kernels.reshape(54 * CHANS, CHANS),
        jnp.pad(conv_bias, ((0, 5), (0, 0))),
        couple_down.reshape(2 * CHANS, latent),
        couple_up.reshape(4 * latent, CHANS),
        head.reshape(1, CHANS),
    )

    return pl.pallas_call(
        functools.partial(main_kernel, (devices, steps, exact)),
        out_shape=jax.ShapeDtypeStruct((COUNT, DEPTH, HEIGHT * WIDTH), F32),
        in_specs=[vmem] * 10,
        out_specs=vmem,
        scratch_shapes=[
            pltpu.VMEM((HEIGHT * UNITS, WIDE), BF16),
            pltpu.VMEM((HEIGHT, UNITS, WIDE), F32),
            pltpu.VMEM((3, 28 * 32, WIDE), BF16),
            pltpu.VMEM((BLOCKS, HEIGHT, 16, WIDE), F32),
            pltpu.VMEM((3, (HALF + 2) * 16, total), BF16),
        ],
        name="decode",
    )(every, meta, *weights, cell_bias.reshape(1, HEIGHT * WIDTH))


def solution(mesh):
    in_specs = (
        P("patch", "tm", None, None),
        P("tm", None),
        P("tm"),
        P(),
        P(),
        P(),
        P(),
        P(),
        P(),
        P(),
    )
    out_specs = P("patch", "tm", None)
    return jax.shard_map(shards, mesh=mesh, in_specs=in_specs, out_specs=out_specs, check_vma=False)
```

time: 122 us -> 49.6 us (0.41)
  the two profiles are of different devices: /device:TPU:0 before, /device:TPU:9 now
where the time goes in v1:
time: 49.6 us; the launch traced here: 48.7 us
  Pallas kernels  25.8 us (52%)
  starting transfers between devices  10.5 us (21%)
  local copies, waits for them, and re-layouts  7.02 us (14%)
  waiting for transfers between devices  4.02 us (8%)
  between operations  0.72 us (1%)
  other arithmetic  0.62 us (1%)
    pallas_call x1, Pallas kernels, shards(): pl.pallas_call(functools.partial(main_kernel, (devices, steps, exact)), o...  20.9 us
    ppermute x4, starting transfers between devices, swapped(): return lax.ppermute(block, axis, [(i, i ^ mask) for i in range(count)])  5.91 us
    ppermute x3, starting transfers between devices, shards(): lax.ppermute(mine, 'tm', [(i, i ^ k) for i in range(steps) if abs(i - (i...  4.54 us
    ppermute x4, waiting for transfers between devices, swapped(): return lax.ppermute(block, axis, [(i, i ^ mask) for i in range(count)])  4.02 us
    unnamed x11, local copies, waits for them, and re-layouts  3.82 us
    pallas_call x1, Pallas kernels, shards(): pl.pallas_call(weights_kernel, out_shape=[jax.ShapeDtypeStruct((WIDE, tot...  3.36 us
    pallas_call x1, Pallas kernels, shards(): pl.pallas_call(pack_kernel, out_shape=jax.ShapeDtypeStruct((8, FLAT + LAN...  1.63 us
    reshape x1, local copies, waits for them, and re-layouts, shards(): first_kernel.reshape(27, CHANS)  1.3 us
  transfers between devices with their start and end apart: 7, of which 3 were waited for; matrix products, arithmetic and copies ran while one was open for 11% of the time, Pallas kernels for 7%

profile of v1, /device:TPU:9, one launch (start us, length us, event | category | flops | bytes accessed | tf_op | source)
XLA Modules:
  0.0 48.7 jit_solution(10627976474152181398)
XLA Ops:
  0.0 1.7 %copy.11.bits_ref = s32[4,2,26,24]{3,2,1,0:T(8,128)} copy(s32[4,2,26,24]{2,3,1,0:T(8,128)} %param.10) | data formatting | bytes 39936 | tf_op args[0]
  2.3 1.6 %pack.1 = bf16[8,768]{1,0:T(8,128)(2,1)} custom-call(s32[4,2,26,24]{3,2,1,0:T(8,128)} %copy.11.bits_ref, s32[1,32]{1,0:T(1,128)} %partners_ref.1, s32[1]{0:T(128)S(6)} %copy.17.gate_ref), custom_call_target="tpu_custom_call" | custom-call | tf_op jit(solution)/shard_map/pack/pallas_call | solution.py:406
  3.9 0.0 collective-permute-start
  3.9 2.5 %collective-permute-start.1 = (bf16[8,768]{1,0:T(8,128)(2,1)}, bf16[8,768]{1,0:T(8,128)(2,1)S(1)}, u32[]{:S(2)}, u32[]{:S(2)}) collective-permute-start(bf16[8,768]{1,0:T(8,128)(2,1)} %pack.1), channel_id=1, source_target_pairs={{0,2},{1,3},{2,0},{3,1},{4,6},{5,7},{6,4},{7,5},{8,10},{9,11},{10,... | collective-permute-start | bytes 36872 | tf_op jit(solution)/shard_map/ppermute | solution.py:417
  6.4 2.1 %collective-permute-start.2 = (bf16[8,768]{1,0:T(8,128)(2,1)}, bf16[8,768]{1,0:T(8,128)(2,1)S(1)}, u32[]{:S(2)}, u32[]{:S(2)}) collective-permute-start(bf16[8,768]{1,0:T(8,128)(2,1)} %pack.1), channel_id=1, source_target_pairs={{1,2},{2,1},{5,6},{6,5},{9,10},{10,9},{13,14},{14,13},{17,18},{18,... | collective-permute-start | bytes 36872 | tf_op jit(solution)/shard_map/ppermute | solution.py:417
  8.5 1.4 %copy.12 = bf16[2,32,16]{2,1,0:T(8,128)(2,1)} copy(bf16[2,32,16]{1,2,0:T(8,128)(2,1)} %param.16) | data formatting | bytes 4096 | tf_op args[6]
  9.9 1.3 %reshape.18.first_ref = bf16[27,32]{1,0:T(8,128)(2,1)} reshape(bf16[3,3,3,32]{3,2,1,0:T(4,128)(2,1)} %param.13) | data formatting | bytes 3456 | tf_op jit(solution)/shard_map/reshape | solution.py:446
  11.2 1.3 %pad.4.bias_ref = f32[8,32]{1,0:T(8,128)} pad(f32[3,32]{1,0:T(4,128)} %param.15, f32[]{:T(128)} %constant.2.clone.1), padding=0_5x0_0 | pad | bytes 1412 | tf_op jit(solution)/shard_map/jit(_pad)/pad | solution.py:448
  12.4 0.0 copy-start.2
  12.4 0.0 copy-start.1
  12.5 3.4 %weights.1 = (bf16[256,1024]{1,0:T(8,128)(2,1)}, bf16[2304,256]{1,0:T(8,128)(2,1)}, bf16[2304,256]{1,0:T(8,128)(2,1)}, bf16[512,128]{1,0:T(8,128)(2,1)}, bf16[51...) custom-call(bf16[27,32]{1,0:T(8,128)(2,1)} %reshape.18.first_ref, bf16[1728,32]{1,0:T(8,128)(2,1)} %bitcast.5, ...), custom_call_target="tpu_custom_call" | custom-call | flops 1000000000 | bytes 10000000 | tf_op jit(solution)/shard_map/weights/pallas_call | solution.py:429
  15.8 0.0 copy-done.2
  15.8 0.6 %reshape.23.cell_ref = f32[1,624]{1,0:T(1,128)} reshape(f32[624]{0:T(1024)S(1)} %copy-done.2) | data formatting | bytes 4992 | tf_op jit(solution)/shard_map/reshape | solution.py:467
  16.4 0.0 collective-permute-done
  16.4 0.0 collective-permute-done.1
  16.4 0.0 collective-permute-done.2
  16.4 0.0 copy-done.1
  16.5 1.3 %collective-permute-start.3 = (bf16[32,640]{1,0:T(8,128)(2,1)S(1)}, bf16[32,640]{1,0:T(8,128)(2,1)S(1)}, u32[]{:S(2)}, u32[]{:S(2)}) collective-permute-start(bf16[32,640]{1,0:T(8,128)(2,1)S(1)} %get-tuple-element.19), channel_id=1, source_target_pairs={{0,8},{4,12},{8,0},{12,4},{16,24},{20,28},{24,16},{28,20},{1,9},{5... | collective-permute-start | bytes 122888 | tf_op jit(solution)/shard_map/ppermute | solution.py:390
  17.7 1.2 %collective-permute-start.4 = (bf16[32,640]{1,0:T(8,128)(2,1)S(1)}, bf16[32,640]{1,0:T(8,128)(2,1)S(1)}, u32[]{:S(2)}, u32[]{:S(2)}) collective-permute-start(bf16[32,640]{1,0:T(8,128)(2,1)S(1)} %get-tuple-element.19), channel_id=1, source_target_pairs={{0,16},{4,20},{8,24},{12,28},{16,0},{20,4},{24,8},{28,12},{1,17},{... | collective-permute-start | bytes 122888 | tf_op jit(solution)/shard_map/ppermute | solution.py:390
  19.0 0.2 collective-permute-start.5
  19.2 0.6 %pad_maximum_fusion.2.meta_ref = bf16[32,128]{1,0:T(8,128)(2,1)} fusion(bf16[8,768]{1,0:T(8,128)(2,1)S(1)} %collective-permute-done.2, bf16[8,768]{1,0:T(8,128)(2,1)S(1)} %collective-permute-done.1, bf16[8,768]{1,0:T(8,128)(2,1)S(1)} %collective-permute-done, bf16[8,768]{1,0:T(8,128)(2,1)S(1)} %copy-done.1), kind=kLoop, calls=%fused_computation.7 | loop fusion | flops 32768 | bytes 57344 | tf_op jit(solution)/shard_map/slice | solution.py:423
  19.8 0.0 collective-permute-done.3
  19.8 0.8 %collective-permute-done.4 = bf16[32,640]{1,0:T(8,128)(2,1)S(1)} collective-permute-done((bf16[32,640]{1,0:T(8,128)(2,1)S(1)}, bf16[32,640]{1,0:T(8,128)(2,1)S(1)}, u32[]{:S(2)}, u32[]{:S(2)}) %collective-permute-start.4) | collective-permute-done | bytes 40992 | tf_op jit(solution)/shard_map/ppermute | solution.py:390
  20.6 2.2 %collective-permute-done.5 = bf16[32,640]{1,0:T(8,128)(2,1)S(1)} collective-permute-done((bf16[32,640]{1,0:T(8,128)(2,1)S(1)}, bf16[32,640]{1,0:T(8,128)(2,1)S(1)}, u32[]{:S(2)}, u32[]{:S(2)}) %collective-permute-start.5) | collective-permute-done | bytes 40992 | tf_op jit(solution)/shard_map/ppermute | solution.py:390
  22.8 3.2 %collective-permute-start.6 = (bf16[128,640]{1,0:T(8,128)(2,1)S(1)}, bf16[128,640]{1,0:T(8,128)(2,1)S(1)}, u32[]{:S(2)}, u32[]{:S(2)}) collective-permute-start(bf16[128,640]{1,0:T(8,128)(2,1)S(1)} %pad_maximum_fusion), channel_id=1, source_target_pairs={{0,4},{4,0},{8,12},{12,8},{16,20},{20,16},{24,28},{28,24},{1,5},{5... | collective-permute-start | bytes 491528 | tf_op jit(solution)/shard_map/ppermute | solution.py:390
  26.1 1.0 %collective-permute-done.6 = bf16[128,640]{1,0:T(8,128)(2,1)S(1)} collective-permute-done((bf16[128,640]{1,0:T(8,128)(2,1)S(1)}, bf16[128,640]{1,0:T(8,128)(2,1)S(1)}, u32[]{:S(2)}, u32[]{:S(2)}) %collective-permute-start.6) | collective-permute-done | bytes 163872 | tf_op jit(solution)/shard_map/ppermute | solution.py:390
  27.1 0.0 copy-start
  27.1 0.7 %copy-done = bf16[256,640]{1,0:T(8,128)(2,1)} copy-done((bf16[256,640]{1,0:T(8,128)(2,1)}, bf16[256,640]{1,0:T(8,128)(2,1)S(1)}, u32[]{:S(2)}) %copy-start) | copy-done | bytes 327704
  27.8 20.9 %decode.1 = f32[4,2,624]{2,1,0:T(2,128)} custom-call(bf16[256,640]{1,0:T(8,128)(2,1)} %copy-done, bf16[32,128]{1,0:T(8,128)(2,1)} %pad_maximum_fusion.2.meta_ref, bf16[256,1024]{1,0:T(8,128)(2,1)} %get-tuple-element.12.wf_ref, bf16[2304,256]{1,0:T(8,128)(2,1)} %get-tuple-element.13.w2_ref, bf16[2304,256]{1,0:T(8,128)(2,1)} %get-tuple-element.14.w3_ref, ...), custom_call_target="tpu_custom_call" | custom-call | tf_op jit(solution)/shard_map/decode/pallas_call | solution.py:454
  (7 shorter events, 0.1 us)
Async XLA Ops:
  3.9 12.5 %collective-permute-start = (bf16[8,768]{1,0:T(8,128)(2,1)}, bf16[8,768]{1,0:T(8,128)(2,1)S(1)}, u32[]{:S(2)}, u32[]{:S(2)}) collective-permute-start(bf16[8,768]{1,0:T(8,128)(2,1)} %pack.1), channel_id=1, source_target_pairs={{0,1},{1,0},{2,3},{3,2},{4,5},{5,4},{6,7},{7,6},{8,9},{9,8},{10,11... | collective-permute-start | bytes 36872 | tf_op jit(solution)/shard_map/ppermute | solution.py:417
  3.9 12.5 %collective-permute-start.1 = (bf16[8,768]{1,0:T(8,128)(2,1)}, bf16[8,768]{1,0:T(8,128)(2,1)S(1)}, u32[]{:S(2)}, u32[]{:S(2)}) collective-permute-start(bf16[8,768]{1,0:T(8,128)(2,1)} %pack.1), channel_id=1, source_target_pairs={{0,2},{1,3},{2,0},{3,1},{4,6},{5,7},{6,4},{7,5},{8,10},{9,11},{10,... | collective-permute-start | bytes 36872 | tf_op jit(solution)/shard_map/ppermute | solution.py:417
  6.4 10.0 %collective-permute-start.2 = (bf16[8,768]{1,0:T(8,128)(2,1)}, bf16[8,768]{1,0:T(8,128)(2,1)S(1)}, u32[]{:S(2)}, u32[]{:S(2)}) collective-permute-start(bf16[8,768]{1,0:T(8,128)(2,1)} %pack.1), channel_id=1, source_target_pairs={{1,2},{2,1},{5,6},{6,5},{9,10},{10,9},{13,14},{14,13},{17,18},{18,... | collective-permute-start | bytes 36872 | tf_op jit(solution)/shard_map/ppermute | solution.py:417
  12.4 3.4 %copy-start.2 = (f32[624]{0:T(1024)S(1)}, f32[624]{0:T(1024)}, u32[]{:S(2)}) copy-start(f32[624]{0:T(1024)} %param.19) | copy-start | bytes 7492
  12.4 4.0 %copy-start.1 = (bf16[8,768]{1,0:T(8,128)(2,1)S(1)}, bf16[8,768]{1,0:T(8,128)(2,1)}, u32[]{:S(2)}) copy-start(bf16[8,768]{1,0:T(8,128)(2,1)} %pack.1) | copy-start | bytes 36868
  16.5 3.3 %collective-permute-start.3 = (bf16[32,640]{1,0:T(8,128)(2,1)S(1)}, bf16[32,640]{1,0:T(8,128)(2,1)S(1)}, u32[]{:S(2)}, u32[]{:S(2)}) collective-permute-start(bf16[32,640]{1,0:T(8,128)(2,1)S(1)} %get-tuple-element.19), channel_id=1, source_target_pairs={{0,8},{4,12},{8,0},{12,4},{16,24},{20,28},{24,16},{28,20},{1,9},{5... | collective-permute-start | bytes 122888 | tf_op jit(solution)/shard_map/ppermute | solution.py:390
  17.7 2.9 %collective-permute-start.4 = (bf16[32,640]{1,0:T(8,128)(2,1)S(1)}, bf16[32,640]{1,0:T(8,128)(2,1)S(1)}, u32[]{:S(2)}, u32[]{:S(2)}) collective-permute-start(bf16[32,640]{1,0:T(8,128)(2,1)S(1)} %get-tuple-element.19), channel_id=1, source_target_pairs={{0,16},{4,20},{8,24},{12,28},{16,0},{20,4},{24,8},{28,12},{1,17},{... | collective-permute-start | bytes 122888 | tf_op jit(solution)/shard_map/ppermute | solution.py:390
  19.0 3.8 %collective-permute-start.5 = (bf16[32,640]{1,0:T(8,128)(2,1)S(1)}, bf16[32,640]{1,0:T(8,128)(2,1)S(1)}, u32[]{:S(2)}, u32[]{:S(2)}) collective-permute-start(bf16[32,640]{1,0:T(8,128)(2,1)S(1)} %get-tuple-element.19), channel_id=1, source_target_pairs={{0,24},{4,28},{8,16},{12,20},{16,8},{20,12},{24,0},{28,4},{1,25},{... | collective-permute-start | bytes 122888 | tf_op jit(solution)/shard_map/ppermute | solution.py:390
  22.8 4.2 %collective-permute-start.6 = (bf16[128,640]{1,0:T(8,128)(2,1)S(1)}, bf16[128,640]{1,0:T(8,128)(2,1)S(1)}, u32[]{:S(2)}, u32[]{:S(2)}) collective-permute-start(bf16[128,640]{1,0:T(8,128)(2,1)S(1)} %pad_maximum_fusion), channel_id=1, source_target_pairs={{0,4},{4,0},{8,12},{12,8},{16,20},{20,16},{24,28},{28,24},{1,5},{5... | collective-permute-start | bytes 491528 | tf_op jit(solution)/shard_map/ppermute | solution.py:390
  27.1 0.8 %copy-start = (bf16[256,640]{1,0:T(8,128)(2,1)}, bf16[256,640]{1,0:T(8,128)(2,1)S(1)}, u32[]{:S(2)}) copy-start(bf16[256,640]{1,0:T(8,128)(2,1)S(1)} %constant_dynamic-update-slice_fusion.all_ref) | copy-start | bytes 983044

commit v2 on v1

--- a/solution.py
+++ b/solution.py
@@ -36,9 +36,19 @@
     return jnp.dot(a, b, preferred_element_type=F32)
 
 
-def pack_kernel(bits_ref, partners_ref, gate_ref, out_ref):
+def fetch(pairs, sems):
+    copies = [pltpu.make_async_copy(src, dst, sems.at[i]) for i, (src, dst) in enumerate(pairs)]
+    for copy in copies:
+        copy.start()
+    for copy in copies:
+        copy.wait()
+
+
+def pack_kernel(bits_hbm, partners_hbm, gate_ref, out_ref, bits_ref, partners_ref, sems):
+    fetch(((bits_hbm, bits_ref), (partners_hbm, partners_ref)), sems)
     units = COUNT * DEPTH
-    bits = bits_ref[...].reshape(units, HEIGHT, WIDTH).astype(F32)
+    bits = bits_ref[...].reshape(units, WIDTH, HEIGHT).astype(F32)
+    bits = jnp.swapaxes(bits, 1, 2)
     rows = [bits[:, y, :] for y in range(HEIGHT)]
     flat = jnp.concatenate(rows + [jnp.zeros((units, FLAT - HEIGHT * WIDTH), F32)], axis=1)
     out_ref[:, :FLAT] = flat.astype(BF16)
@@ -52,9 +62,12 @@
 
 
 def weights_kernel(
-    first_ref, second_ref, bias_ref, down_ref, up_ref, head_ref,
-    wf_ref, w2_ref, w3_ref, dn_ref, un_ref, rd_ref, bs_ref, scr_ref,
+    first_hbm, second_hbm, bias_hbm, down_hbm, up_hbm, head_hbm,
+    wf_ref, w2_ref, w3_ref, dn_ref, un_ref, rd_ref, bs_ref,
+    scr_ref, first_ref, second_ref, bias_ref, down_ref, up_ref, head_ref, sems,
 ):
+    sources = (first_hbm, second_hbm, bias_hbm, down_hbm, up_hbm, head_hbm)
+    fetch(zip(sources, (first_ref, second_ref, bias_ref, down_ref, up_ref, head_ref)), sems)
     total = BLOCKS * WIDE
     spread = (iota((CHANS, WIDE), 1) % CHANS == iota((CHANS, WIDE), 0)).astype(BF16)
     slot = iota((CHANS, WIDE), 1) // CHANS
@@ -71,7 +84,9 @@
                     )
                 w_ref[tap * WIDE + kc * CHANS : tap * WIDE + (kc + 1) * CHANS, :] = block.astype(BF16)
     across = (iota((CHANS, total), 1) % CHANS == iota((CHANS, total), 0)).astype(BF16)
-    taps = dot(first_ref[...], across)
+    for pair in range(9):
+        scr_ref[8 * pair : 8 * pair + 3, :CHANS] = first_ref[pair // 3, pair % 3].astype(F32)
+    taps = dot(scr_ref[0:72, :CHANS].astype(BF16), across)
     lane = iota((WIDTH, total), 1)
     column = (lane // WIDE) * WINDOW - 1 + (lane % WIDE) // CHANS
     real = (column >= 0) & (column < WIDTH)
@@ -79,7 +94,7 @@
     for pair in range(9):
         block = jnp.zeros((WIDTH, total), F32)
         for dc in range(3):
-            block = jnp.where(real & (offset == dc), taps[pair * 3 + dc : pair * 3 + dc + 1, :], block)
+            block = jnp.where(real & (offset == dc), taps[pair * 8 + dc : pair * 8 + dc + 1, :], block)
         scr_ref[pair * WIDTH : (pair + 1) * WIDTH, :] = block
     scr_ref[9 * WIDTH :, :] = jnp.zeros((WIDE - 9 * WIDTH, total), F32)
     wf_ref[...] = scr_ref[...].astype(BF16)
@@ -87,15 +102,16 @@
     low = SLOTS * latent
     thin = (iota((latent, low), 1) % latent == iota((latent, low), 0)).astype(BF16)
     for layer in range(2):
-        tiled = dot(down_ref[layer * CHANS : (layer + 1) * CHANS, :], thin)
+        tiled = lax.dot_general(
+            down_ref[layer], thin, (((0,), (0,)), ((), ())), preferred_element_type=F32
+        )
         for kc in range(SLOTS):
             keep = iota((CHANS, low), 1) // latent == kc
             dn_ref[layer * WIDE + kc * CHANS : layer * WIDE + (kc + 1) * CHANS, :] = jnp.where(
                 keep, tiled, 0.0
             ).astype(BF16)
         for role in range(2):
-            at = (layer * 2 + role) * latent
-            tiled = dot(up_ref[at : at + latent, :], spread)
+            tiled = dot(up_ref[layer, role], spread)
             for kc in range(SLOTS):
                 keep = iota((latent, WIDE), 1) // CHANS == kc
                 top = (layer * 2 + role) * low + kc * latent
@@ -108,8 +124,10 @@
     target = (row // WIDE) * WINDOW - 1 + place
     keep = (place >= 1) & (place <= WINDOW) & (target == iota((total, LANES), 1))
     rd_ref[...] = jnp.where(keep, values, 0.0).astype(BF16)
+    scr_ref[0:8, :CHANS] = jnp.zeros((8, CHANS), F32)
+    scr_ref[0:3, :CHANS] = bias_ref[...]
     biases = jnp.dot(
-        bias_ref[...], across.astype(F32), preferred_element_type=F32, precision=lax.Precision.HIGHEST
+        scr_ref[0:8, :CHANS], across.astype(F32), preferred_element_type=F32, precision=lax.Precision.HIGHEST
     )
     lane = iota((8, total), 1)
     place = (lane % WIDE) // CHANS
@@ -146,7 +164,7 @@
 
 
 def main_kernel(
-    sizes, all_ref, meta_ref, wf_ref, w2_ref, w3_ref, dn_ref, un_ref, rd_ref, bs_ref, cell_ref,
+    sizes, here_ref, there_ref, meta_ref, wf_ref, w2_ref, w3_ref, dn_ref, un_ref, rd_ref, bs_ref, cell_ref,
     out_ref, x_ref, f_ref, s_ref, c2_ref, s3_ref,
 ):
     devices, steps, exact = sizes
@@ -162,7 +180,7 @@
         valid = (there >= 0) & (there < steps)
         safe = jnp.clip(there, 0, steps - 1)
         block = (safe ^ now) if exact else (2, 0, 1)[j]
-        tile = meta_ref[pl.ds(pl.multiple_of(block * 8, 8), 8), :].astype(F32).astype(jnp.int32)
+        tile = meta_ref[pl.ds(pl.multiple_of(block * 8, 8), 8), FLAT:].astype(F32).astype(jnp.int32)
         names.append(jnp.where(valid, tile[0:1, :], -1))
         moments.append(jnp.broadcast_to(jnp.where(valid, tile[1:2, :], -1000), (8, LANES)))
     first_round = 2 * now - 2
@@ -201,7 +219,8 @@
     far_low = touches & (step_far < 0)
     far_high = touches & (step_far > 0)
 
-    columns = all_ref.shape[0]
+    columns = 2 * here_ref.shape[0]
+    events = jnp.concatenate([here_ref[...], there_ref[...]], axis=0)
     col = iota((1, columns), 1)
     block = col // (8 * near)
     half = devices // 2
@@ -236,7 +255,7 @@
     gathered = []
     for dt in range(3):
         choose = jnp.where(round_of == want + (dt - 1), patch_sel, 0.0).astype(BF16)
-        gathered.append(dot(choose, all_ref[...]))
+        gathered.append(dot(choose, events))
     lane = iota((UNITS, LANES), 1)
     for y in range(HEIGHT):
         tiles = window_rows(gathered, y, lane)
@@ -385,6 +404,10 @@
             out_ref[p, j : j + 1, :] = flat[4 * j + p : 4 * j + p + 1, :]
 
 
+def in_hbm(x):
+    return pltpu.with_memory_space_constraint(x, pltpu.HBM)
+
+
 def swapped(block, axis, mask):
     count = lax.axis_size(axis)
     return lax.ppermute(block, axis, [(i, i ^ mask) for i in range(count)])
@@ -402,14 +425,20 @@
     latent = couple_down.shape[-1]
     total = BLOCKS * WIDE
     vmem = pl.BlockSpec(memory_space=pltpu.VMEM)
-    smem = pl.BlockSpec(memory_space=pltpu.SMEM)
+    hbm = pl.BlockSpec(memory_space=pltpu.HBM)
     mine = pl.pallas_call(
         pack_kernel,
         out_shape=jax.ShapeDtypeStruct((8, FLAT + LANES), BF16),
-        in_specs=[vmem, vmem, smem],
+        in_specs=[hbm, hbm, pl.BlockSpec(memory_space=pltpu.SMEM)],
         out_specs=vmem,
+        scratch_shapes=[
+            pltpu.VMEM((COUNT, DEPTH, WIDTH, HEIGHT), jnp.int32),
+            pltpu.VMEM(partners.shape, jnp.int32),
+            pltpu.SemaphoreType.DMA((2,)),
+        ],
+        compiler_params=pltpu.CompilerParams(vmem_limit_bytes=2 << 20),
         name="pack",
-    )(bits, partners, gate_round)
+    )(in_hbm(jnp.swapaxes(bits, 2, 3)), in_hbm(partners), gate_round)
 
     exact = steps <= 4
     if exact:
@@ -420,12 +449,14 @@
     else:
         blocks = [mine] + [shifted(mine, "tm", k) for k in (1, -1, 2, -2)]
     near = jnp.concatenate(blocks, axis=0)
-    meta = near[:, FLAT:]
-    every = near[:, :FLAT]
-    parts = [every] + [swapped(every, "patch", 2 * m) for m in range(1, devices // 2)]
-    every = jnp.concatenate(parts, axis=0)
-    every = jnp.concatenate([every, swapped(every, "patch", 1)], axis=0)
-
+    params = (
+        first_kernel,
+        second_kernels.reshape(54 * CHANS, CHANS),
+        conv_bias,
+        jnp.swapaxes(couple_down, 1, 2),
+        couple_up,
+        head.reshape(1, CHANS),
+    )
     weights = pl.pallas_call(
         weights_kernel,
         out_shape=[
@@ -437,24 +468,26 @@
             jax.ShapeDtypeStruct((total, LANES), BF16),
             jax.ShapeDtypeStruct((8, total), F32),
         ],
-        in_specs=[vmem] * 6,
+        in_specs=[hbm] * 6,
         out_specs=[vmem] * 7,
-        scratch_shapes=[pltpu.VMEM((WIDE, total), F32)],
+        scratch_shapes=[pltpu.VMEM((WIDE, total), F32)]
+        + [pltpu.VMEM(x.shape, x.dtype) for x in params]
+        + [pltpu.SemaphoreType.DMA((6,))],
         cost_estimate=pl.CostEstimate(flops=10**9, bytes_accessed=10**7, transcendentals=0),
+        compiler_params=pltpu.CompilerParams(vmem_limit_bytes=12 << 20),
         name="weights",
-    )(
-        first_kernel.reshape(27, CHANS),
-        second_kernels.reshape(54 * CHANS, CHANS),
-        jnp.pad(conv_bias, ((0, 5), (0, 0))),
-        couple_down.reshape(2 * CHANS, latent),
-        couple_up.reshape(4 * latent, CHANS),
-        head.reshape(1, CHANS),
-    )
+    )(*map(in_hbm, params))
+
+    near, weights = lax.optimization_barrier((near, weights))
+    every = near[:, :FLAT]
+    parts = [every] + [swapped(every, "patch", 2 * m) for m in range(1, devices // 2)]
+    every = jnp.concatenate(parts, axis=0)
+    others = swapped(every, "patch", 1)
 
     return pl.pallas_call(
         functools.partial(main_kernel, (devices, steps, exact)),
         out_shape=jax.ShapeDtypeStruct((COUNT, DEPTH, HEIGHT * WIDTH), F32),
-        in_specs=[vmem] * 10,
+        in_specs=[vmem] * 11,
         out_specs=vmem,
         scratch_shapes=[
             pltpu.VMEM((HEIGHT * UNITS, WIDE), BF16),
@@ -463,8 +496,9 @@
             pltpu.VMEM((BLOCKS, HEIGHT, 16, WIDE), F32),
             pltpu.VMEM((3, (HALF + 2) * 16, total), BF16),
         ],
+        compiler_params=pltpu.CompilerParams(vmem_limit_bytes=40 << 20),
         name="decode",
-    )(every, meta, *weights, cell_bias.reshape(1, HEIGHT * WIDTH))
+    )(every, others, near, *weights, cell_bias.reshape(1, HEIGHT * WIDTH))
 
 
 def solution(mesh):

time: 49.6 us -> 39.5 us (0.80)
  the two profiles are of different devices: /device:TPU:9 before, /device:TPU:0 now
where the time goes in v2:
time: 39.5 us; the launch traced here: 39.3 us
  Pallas kernels  22.2 us (56%)
  starting transfers between devices  10.3 us (26%)
  waiting for transfers between devices  5.99 us (15%)
  between operations  0.73 us (2%)
    pallas_call x1, Pallas kernels, shards(): pl.pallas_call(functools.partial(main_kernel, (devices, steps, exact)), o...  18.8 us
    ppermute x3, starting transfers between devices, shards(): lax.ppermute(mine, 'tm', [(i, i ^ k) for i in range(steps) if abs(i - (i...  6.68 us
    ppermute x4, waiting for transfers between devices, swapped(): return lax.ppermute(block, axis, [(i, i ^ mask) for i in range(count)])  4.83 us
    ppermute x4, starting transfers between devices, swapped(): return lax.ppermute(block, axis, [(i, i ^ mask) for i in range(count)])  3.62 us
    pallas_call x1, Pallas kernels, shards(): pl.pallas_call(weights_kernel, out_shape=[jax.ShapeDtypeStruct((WIDE, tot...  2.31 us
    ppermute x3, waiting for transfers between devices, shards(): lax.ppermute(mine, 'tm', [(i, i ^ k) for i in range(steps) if abs(i - (i...  1.16 us
    pallas_call x1, Pallas kernels, shards(): pl.pallas_call(pack_kernel, out_shape=jax.ShapeDtypeStruct((8, FLAT + LAN...  1.11 us
  transfers between devices with their start and end apart: 7, of which 5 were waited for; matrix products, arithmetic and copies ran while one was open for 0% of the time, Pallas kernels for 6%

profile of v2, /device:TPU:0, one launch (start us, length us, event | category | flops | bytes accessed | tf_op | source)
XLA Modules:
  0.0 39.3 jit_solution(4509258894817936692)
XLA Ops:
  0.7 1.1 %pack.1 = bf16[8,768]{1,0:T(8,128)(2,1)S(1)} custom-call(s32[4,2,24,26]{3,2,1,0:T(8,128)} %bitcast.4, s32[1,32]{1,0:T(1,128)} %partners_hbm.1, s32[1]{0:T(128)S(6)} %copy.11.gate_ref), custom_call_target="tpu_custom_call" | custom-call | tf_op jit(solution)/shard_map/pack/pallas_call | solution.py:429
  1.8 0.7 %collective-permute-start.2 = (bf16[8,768]{1,0:T(8,128)(2,1)S(1)}, bf16[8,768]{1,0:T(8,128)(2,1)S(1)}, u32[]{:S(2)}, u32[]{:S(2)}) collective-permute-start(bf16[8,768]{1,0:T(8,128)(2,1)S(1)} %pack.1), channel_id=1, source_target_pairs={{1,2},{2,1},{5,6},{6,5},{9,10},{10,9},{13,14},{14,13},{17,18},{18,... | collective-permute-start | bytes 36872 | tf_op jit(solution)/shard_map/ppermute | solution.py:446
  2.4 5.8 %collective-permute-start.1 = (bf16[8,768]{1,0:T(8,128)(2,1)S(1)}, bf16[8,768]{1,0:T(8,128)(2,1)S(1)}, u32[]{:S(2)}, u32[]{:S(2)}) collective-permute-start(bf16[8,768]{1,0:T(8,128)(2,1)S(1)} %pack.1), channel_id=1, source_target_pairs={{0,2},{1,3},{2,0},{3,1},{4,6},{5,7},{6,4},{7,5},{8,10},{9,11},{10,... | collective-permute-start | bytes 36872 | tf_op jit(solution)/shard_map/ppermute | solution.py:446
  8.3 0.2 collective-permute-start
  8.5 0.0 copy-start
  8.5 2.3 %weights.1 = (bf16[256,1024]{1,0:T(8,128)(2,1)S(1)}, bf16[2304,256]{1,0:T(8,128)(2,1)S(1)}, bf16[2304,256]{1,0:T(8,128)(2,1)S(1)}, bf16[512,128]{1,0:T(8,128)(2,...) custom-call(bf16[3,3,3,32]{3,2,1,0:T(4,128)(2,1)} %first_hbm.1, ...), custom_call_target="tpu_custom_call" | custom-call | flops 1000000000 | bytes 10000000 | tf_op jit(solution)/shard_map/weights/pallas_call | solution.py:460
  10.8 0.0 collective-permute-done.2
  10.8 0.0 collective-permute-done.1
  10.8 1.2 %collective-permute-done = bf16[8,768]{1,0:T(8,128)(2,1)S(1)} collective-permute-done((bf16[8,768]{1,0:T(8,128)(2,1)S(1)}, bf16[8,768]{1,0:T(8,128)(2,1)S(1)}, u32[]{:S(2)}, u32[]{:S(2)}) %collective-permute-start) | collective-permute-done | bytes 12320 | tf_op jit(solution)/shard_map/ppermute | solution.py:446
  12.0 2.5 %collective-permute-start.5 = (bf16[32,640]{1,0:T(8,128)(2,1)S(1)}, bf16[32,640]{1,0:T(8,128)(2,1)S(1)}, u32[]{:S(2)}, u32[]{:S(2)}) collective-permute-start(bf16[32,640]{1,0:T(8,128)(2,1)S(1)} %slice.3), channel_id=1, source_target_pairs={{0,24},{4,28},{8,16},{12,20},{16,8},{20,12},{24,0},{28,4},{1,25},{... | collective-permute-start | bytes 122888 | tf_op jit(solution)/shard_map/ppermute | solution.py:413
  14.5 0.5 %collective-permute-start.4 = (bf16[32,640]{1,0:T(8,128)(2,1)S(1)}, bf16[32,640]{1,0:T(8,128)(2,1)S(1)}, u32[]{:S(2)}, u32[]{:S(2)}) collective-permute-start(bf16[32,640]{1,0:T(8,128)(2,1)S(1)} %slice.3), channel_id=1, source_target_pairs={{0,16},{4,20},{8,24},{12,28},{16,0},{20,4},{24,8},{28,12},{1,17},{... | collective-permute-start | bytes 122888 | tf_op jit(solution)/shard_map/ppermute | solution.py:413
  15.0 0.5 %collective-permute-start.3 = (bf16[32,640]{1,0:T(8,128)(2,1)S(1)}, bf16[32,640]{1,0:T(8,128)(2,1)S(1)}, u32[]{:S(2)}, u32[]{:S(2)}) collective-permute-start(bf16[32,640]{1,0:T(8,128)(2,1)S(1)} %slice.3), channel_id=1, source_target_pairs={{0,8},{4,12},{8,0},{12,4},{16,24},{20,28},{24,16},{28,20},{1,9},{5... | collective-permute-start | bytes 122888 | tf_op jit(solution)/shard_map/ppermute | solution.py:413
  15.5 1.5 %collective-permute-done.5 = bf16[32,640]{1,0:T(8,128)(2,1)S(1)} collective-permute-done((bf16[32,640]{1,0:T(8,128)(2,1)S(1)}, bf16[32,640]{1,0:T(8,128)(2,1)S(1)}, u32[]{:S(2)}, u32[]{:S(2)}) %collective-permute-start.5) | collective-permute-done | bytes 40992 | tf_op jit(solution)/shard_map/ppermute | solution.py:413
  17.0 1.5 %collective-permute-done.4 = bf16[32,640]{1,0:T(8,128)(2,1)S(1)} collective-permute-done((bf16[32,640]{1,0:T(8,128)(2,1)S(1)}, bf16[32,640]{1,0:T(8,128)(2,1)S(1)}, u32[]{:S(2)}, u32[]{:S(2)}) %collective-permute-start.4) | collective-permute-done | bytes 40992 | tf_op jit(solution)/shard_map/ppermute | solution.py:413
  18.5 0.5 %collective-permute-done.3 = bf16[32,640]{1,0:T(8,128)(2,1)S(1)} collective-permute-done((bf16[32,640]{1,0:T(8,128)(2,1)S(1)}, bf16[32,640]{1,0:T(8,128)(2,1)S(1)}, u32[]{:S(2)}, u32[]{:S(2)}) %collective-permute-start.3) | collective-permute-done | bytes 40992 | tf_op jit(solution)/shard_map/ppermute | solution.py:413
  19.0 0.1 collective-permute-start.6
  19.1 0.0 copy-done
  19.1 1.4 %collective-permute-done.6.there_ref = bf16[128,640]{1,0:T(8,128)(2,1)S(1)} collective-permute-done((bf16[128,640]{1,0:T(8,128)(2,1)S(1)}, bf16[128,640]{1,0:T(8,128)(2,1)S(1)}, u32[]{:S(2)}, u32[]{:S(2)}) %collective-permute-start.6) | collective-permute-done | bytes 163872 | tf_op jit(solution)/shard_map/ppermute | solution.py:413
  20.5 18.8 %decode.1 = f32[4,2,624]{2,1,0:T(2,128)} custom-call(bf16[128,640]{1,0:T(8,128)(2,1)S(1)} %pad_maximum_fusion.here_ref, bf16[128,640]{1,0:T(8,128)(2,1)S(1)} %collective-permute-done.6.there_ref, bf16[32,768]{1,0:T(8,128)(2,1)S(1)} %pad_maximum_fusion.1.meta_ref, bf16[256,1024]{1,0:T(8,128)(2,1)S(1)} %get-tuple-element.28.wf_ref, ...), custom_call_target="tpu_custom_call" | custom-call | tf_op jit(solution)/shard_map/decode/pallas_call | solution.py:487
  (4 shorter events, 0.0 us)
Async XLA Ops:
  1.8 9.0 %collective-permute-start.2 = (bf16[8,768]{1,0:T(8,128)(2,1)S(1)}, bf16[8,768]{1,0:T(8,128)(2,1)S(1)}, u32[]{:S(2)}, u32[]{:S(2)}) collective-permute-start(bf16[8,768]{1,0:T(8,128)(2,1)S(1)} %pack.1), channel_id=1, source_target_pairs={{1,2},{2,1},{5,6},{6,5},{9,10},{10,9},{13,14},{14,13},{17,18},{18,... | collective-permute-start | bytes 36872 | tf_op jit(solution)/shard_map/ppermute | solution.py:446
  2.4 8.4 %collective-permute-start.1 = (bf16[8,768]{1,0:T(8,128)(2,1)S(1)}, bf16[8,768]{1,0:T(8,128)(2,1)S(1)}, u32[]{:S(2)}, u32[]{:S(2)}) collective-permute-start(bf16[8,768]{1,0:T(8,128)(2,1)S(1)} %pack.1), channel_id=1, source_target_pairs={{0,2},{1,3},{2,0},{3,1},{4,6},{5,7},{6,4},{7,5},{8,10},{9,11},{10,... | collective-permute-start | bytes 36872 | tf_op jit(solution)/shard_map/ppermute | solution.py:446
  8.3 3.7 %collective-permute-start = (bf16[8,768]{1,0:T(8,128)(2,1)S(1)}, bf16[8,768]{1,0:T(8,128)(2,1)S(1)}, u32[]{:S(2)}, u32[]{:S(2)}) collective-permute-start(bf16[8,768]{1,0:T(8,128)(2,1)S(1)} %pack.1), channel_id=1, source_target_pairs={{0,1},{1,0},{2,3},{3,2},{4,5},{5,4},{6,7},{7,6},{8,9},{9,8},{10,11... | collective-permute-start | bytes 36872 | tf_op jit(solution)/shard_map/ppermute | solution.py:446
  8.5 10.6 %copy-start = (f32[624]{0:T(1024)S(1)}, f32[624]{0:T(1024)}, u32[]{:S(2)}) copy-start(f32[624]{0:T(1024)} %param.19) | copy-start | bytes 7492
  12.0 5.0 %collective-permute-start.5 = (bf16[32,640]{1,0:T(8,128)(2,1)S(1)}, bf16[32,640]{1,0:T(8,128)(2,1)S(1)}, u32[]{:S(2)}, u32[]{:S(2)}) collective-permute-start(bf16[32,640]{1,0:T(8,128)(2,1)S(1)} %slice.3), channel_id=1, source_target_pairs={{0,24},{4,28},{8,16},{12,20},{16,8},{20,12},{24,0},{28,4},{1,25},{... | collective-permute-start | bytes 122888 | tf_op jit(solution)/shard_map/ppermute | solution.py:413
  14.5 4.0 %collective-permute-start.4 = (bf16[32,640]{1,0:T(8,128)(2,1)S(1)}, bf16[32,640]{1,0:T(8,128)(2,1)S(1)}, u32[]{:S(2)}, u32[]{:S(2)}) collective-permute-start(bf16[32,640]{1,0:T(8,128)(2,1)S(1)} %slice.3), channel_id=1, source_target_pairs={{0,16},{4,20},{8,24},{12,28},{16,0},{20,4},{24,8},{28,12},{1,17},{... | collective-permute-start | bytes 122888 | tf_op jit(solution)/shard_map/ppermute | solution.py:413
  15.0 4.0 %collective-permute-start.3 = (bf16[32,640]{1,0:T(8,128)(2,1)S(1)}, bf16[32,640]{1,0:T(8,128)(2,1)S(1)}, u32[]{:S(2)}, u32[]{:S(2)}) collective-permute-start(bf16[32,640]{1,0:T(8,128)(2,1)S(1)} %slice.3), channel_id=1, source_target_pairs={{0,8},{4,12},{8,0},{12,4},{16,24},{20,28},{24,16},{28,20},{1,9},{5... | collective-permute-start | bytes 122888 | tf_op jit(solution)/shard_map/ppermute | solution.py:413
  19.0 1.5 %collective-permute-start.6 = (bf16[128,640]{1,0:T(8,128)(2,1)S(1)}, bf16[128,640]{1,0:T(8,128)(2,1)S(1)}, u32[]{:S(2)}, u32[]{:S(2)}) collective-permute-start(bf16[128,640]{1,0:T(8,128)(2,1)S(1)} %pad_maximum_fusion.here_ref), channel_id=1, source_target_pairs={{0,4},{4,0},{8,12},{12,8},{16,20},{20,16},{24,28},{28,24},{1,5},{5... | collective-permute-start | bytes 491528 | tf_op jit(solution)/shard_map/ppermute | solution.py:413

commit v3 on v2

--- a/solution.py
+++ b/solution.py
@@ -174,15 +174,7 @@
     sub = iota((8, LANES), 0)
     low_half = sub < 4
 
-    names, moments = [], []
-    for j in range(3):
-        there = now - 1 + j
-        valid = (there >= 0) & (there < steps)
-        safe = jnp.clip(there, 0, steps - 1)
-        block = (safe ^ now) if exact else (2, 0, 1)[j]
-        tile = meta_ref[pl.ds(pl.multiple_of(block * 8, 8), 8), FLAT:].astype(F32).astype(jnp.int32)
-        names.append(jnp.where(valid, tile[0:1, :], -1))
-        moments.append(jnp.broadcast_to(jnp.where(valid, tile[1:2, :], -1000), (8, LANES)))
+    names, moments = gate_layers(meta_ref, now, steps, exact)
     first_round = 2 * now - 2
     own_patch = COUNT * me + sub % COUNT
 
@@ -343,7 +335,6 @@
 
     lax.fori_loop(0, BLOCKS, body, 0)
 
-    lane8 = iota((8, LANES), 1)
 
     def placed(y, dt):
         if y < 0 or y >= HEIGHT:
@@ -387,7 +378,292 @@
         high = third.astype(BF16)
         rest = (third - high.astype(F32)).astype(BF16)
         logits = logits + dot(high, rd_ref[lanes, :]) + dot(rest, rd_ref[lanes, :])
-    logits = logits.reshape(HALF, 16, LANES)
+    finish(logits.reshape(HALF, 16, LANES), cell_ref, out_ref)
+
+
+def gate_layers(near_ref, now, steps, exact):
+    names, moments = [], []
+    for j in range(3):
+        there = now - 1 + j
+        valid = (there >= 0) & (there < steps)
+        safe = jnp.clip(there, 0, steps - 1)
+        block = (safe ^ now) if exact else (2, 0, 1)[j]
+        tile = near_ref[pl.ds(pl.multiple_of(block * 8, 8), 8), FLAT:].astype(F32).astype(jnp.int32)
+        names.append(jnp.where(valid, tile[0:1, :], -1))
+        moments.append(jnp.broadcast_to(jnp.where(valid, tile[1:2, :], -1000), (8, LANES)))
+    return names, moments
+
+
+def event_rows(gathered, x_ref, units):
+    lane = iota((units, LANES), 1)
+    for y in range(HEIGHT):
+        tiles = window_rows(gathered, y, lane)
+        x_ref[y * units : (y + 1) * units, :] = jnp.concatenate(tiles, axis=1).astype(BF16)
+
+
+MASKS = (("up", 40), ("gate24", 24), ("ok24", 24), ("low", 8), ("high", 8), ("far_low", 8), ("far_high", 8), ("own", 16), ("gate16", 16), ("ok16", 16))
+MASK_AT = {}
+MASK_ROWS = 0
+for _name, _rows in MASKS:
+    MASK_AT[_name] = (MASK_ROWS, _rows)
+    MASK_ROWS += _rows
+MATES = 48
+
+
+def early_kernel(
+    sizes, near_ref, wf_ref, dn_ref, bs_ref, own_ref, pick_ref, choose_ref, mask_ref, x_ref, f_ref
+):
+    devices, steps = sizes
+    near = steps
+    me = lax.axis_index("patch")
+    now = lax.axis_index("tm")
+    sub = iota((8, LANES), 0)
+    low_half = sub < 4
+    names, moments = gate_layers(near_ref, now, steps, True)
+    late = now < steps // 2
+    first_round = 2 * now - 2
+    last = DEPTH * steps - 1
+    own8 = COUNT * me + sub % COUNT
+    name_x = jnp.where(late, names[2], names[0])
+    moment_x = jnp.where(late, moments[2], moments[0])
+
+    def half(a, b):
+        return jnp.where(low_half, a, b)
+
+    def hot(name):
+        return (jnp.broadcast_to(name, (8, LANES)) == own8).astype(F32)
+
+    hots = [hot(name) for name in names]
+    hot8 = half(hots[1], hot(name_x))
+    moment8 = half(moments[1], moment_x)
+    even = moments[1] == 2 * now
+    other = jnp.where(even[0:1, :], names[0], names[2])
+    square = iota((LANES, LANES), 0)
+    wide_hot = jnp.concatenate([hot8, hot8], axis=0).astype(BF16)
+    to_own = dot(wide_hot, (square == names[1]).astype(BF16))[0:8]
+    to_other = dot(wide_hot, (square == other).astype(BF16))[0:8]
+    hot_far = half(to_other, to_own)
+    every = jnp.concatenate(hots + [hot_far, hot8, jnp.zeros((8, LANES), F32)], axis=0).astype(BF16)
+    index = dot(every, square.astype(F32).astype(BF16)).astype(jnp.int32)
+    mate24, far8, mate8 = index[0:24], index[24:32], index[32:40]
+    own24 = jnp.concatenate([own8] * 3, axis=0)
+    moment24 = jnp.concatenate(moments, axis=0)
+    round24 = first_round + iota((24, LANES), 0) // 4
+    round16 = first_round + 1 + iota((16, LANES), 0) // 4
+    moment16 = jnp.concatenate([half(moments[0], moments[1]), half(moments[1], moments[2])], axis=0)
+    step_far = half(jnp.where(even, -1, 1), jnp.where(late, -1, 1))
+    moment_far = half(jnp.where(even, moments[0], moments[2]), moments[1])
+    touches = (moment_far == moment8 + step_far).astype(F32)
+    values = dict(
+        up=jnp.concatenate([(own24 < mate24).astype(F32), (mate8 < own8).astype(F32), (mate8 < far8).astype(F32)], axis=0),
+        gate24=(round24 == moment24).astype(F32),
+        ok24=((round24 >= 0) & (round24 <= last)).astype(F32),
+        low=((moment8 - 1 >= 0) & (moment8 - 1 <= last)).astype(F32),
+        high=((moment8 + 1 >= 0) & (moment8 + 1 <= last)).astype(F32),
+        far_low=jnp.where(step_far < 0, touches, 0.0),
+        far_high=jnp.where(step_far > 0, touches, 0.0),
+        own=jnp.concatenate([(own8 < mate8).astype(F32)] * 2, axis=0),
+        gate16=(round16 == moment16).astype(F32),
+        ok16=((round16 >= 0) & (round16 <= last)).astype(F32),
+    )
+    for name, (at, rows) in MASK_AT.items():
+        mask_ref[at : at + rows, :] = values[name]
+
+    columns = choose_ref.shape[1]
+    col = iota((1, columns), 1)
+    block = col // (8 * near)
+    some = devices // 2
+    source = me ^ (2 * (block % some) + block // some)
+    patch_of = COUNT * source + (col % 8) // DEPTH
+    round_of = DEPTH * (now ^ ((col // 8) % near)) + col % DEPTH
+    spread = dot(every, (iota((LANES, columns), 0) == patch_of).astype(BF16))
+    patch_sel = jnp.concatenate([spread[0:24], spread[24:32], spread[32:40], spread[32:40]], axis=0)
+
+    def lanes_of(x):
+        return jnp.broadcast_to(x[:, :1], (x.shape[0], columns))
+
+    want = jnp.concatenate(
+        [lanes_of(moment24), lanes_of(moment8 + step_far), lanes_of(moment8 - 1), lanes_of(moment8 + 1)], axis=0
+    )
+    for dt in range(3):
+        choose = jnp.where(round_of == want + (dt - 1), patch_sel, 0.0)
+        choose_ref[dt * MATES : (dt + 1) * MATES, :] = choose.astype(BF16)
+
+    rows = near_ref.shape[0]
+    col = iota((1, rows), 1)
+    patch_of = (col % 8) // DEPTH
+    round_of = DEPTH * (now ^ (col // 8)) + col % DEPTH
+    unit = iota((24, rows), 0)
+    gathered = []
+    for dt in range(3):
+        choose = (patch_of == unit % COUNT) & (round_of == first_round + unit // 4 + (dt - 1))
+        gathered.append(dot(choose.astype(F32).astype(BF16), near_ref[:, :FLAT]))
+    event_rows(gathered, x_ref, OWN)
+    ahead = [moments[j] == round24[8 * j : 8 * j + 8] for j in range(3)]
+    for b in range(BLOCKS):
+        lanes = slice(b * WIDE, (b + 1) * WIDE)
+        total = dot(x_ref[...], wf_ref[:, lanes])
+        own = rounded(jnp.maximum(total + bs_ref[0:1, lanes], 0.0))
+        own_ref[:, :, lanes] = own.reshape(HEIGHT, OWN, WIDE)
+        latent = rounded(dot(own.astype(BF16), dn_ref[0:WIDE, :])).reshape(HEIGHT, OWN, LANES)
+        for y in range(HEIGHT):
+            mine = [latent[y, 8 * j : 8 * j + 8] for j in range(3)]
+            mine = [jnp.where(ahead[j], mine[j], pltpu.roll(mine[j], 4, 0)) for j in range(3)]
+            pick_ref[b, y] = half(mine[1], jnp.where(late, mine[2], mine[0]))
+
+
+def late_kernel(
+    here_ref, there_ref, own_ref, pick_ref, choose_ref, mask_ref, wf_ref, w2_ref, w3_ref, dn_ref, un_ref, rd_ref, bs_ref,
+    cell_ref, out_ref, x_ref, f_ref, s_ref, t_ref, c2_ref, s3_ref,
+):
+    now = lax.axis_index("tm")
+    steps = lax.axis_size("tm")
+    late = now < steps // 2
+    low_half = iota((8, LANES), 0) < 4
+
+    def mask(name, wide=True):
+        at, rows = MASK_AT[name]
+        value = mask_ref[at : at + rows, :]
+        return (jnp.concatenate([value] * 2, axis=1) if wide else value) > 0.5
+
+    def swap(x):
+        return pltpu.roll(x, 4, 0)
+
+    events = jnp.concatenate([here_ref[...], there_ref[...]], axis=0)
+    picked = dot(choose_ref[...], events)
+    event_rows([picked[dt * MATES : (dt + 1) * MATES] for dt in range(3)], x_ref, MATES)
+
+    half_mask = jnp.concatenate([low_half.astype(F32)] * 2, axis=1) > 0.5
+
+    def half(a, b):
+        return jnp.where(half_mask, a, b)
+
+    up_mask = mask("up", False)
+    gate24, ok24 = mask("gate24"), mask("ok24")
+    ok_low, ok_high, far_low, far_high = mask("low"), mask("high"), mask("far_low"), mask("far_high")
+    own_mask = mask("own", False)
+    gate16, ok16 = mask("gate16"), mask("ok16")
+    size = HEIGHT * 16
+    part = HALF * 16
+    zero = jnp.zeros((8, WIDE), F32)
+    s_ref[:, :, 0:16, :] = jnp.zeros((2, 3, 16, WIDE), BF16)
+    s_ref[:, :, 27 * 16 :, :] = jnp.zeros((2, 3, 16, WIDE), BF16)
+
+    for b in range(BLOCKS):
+        lanes = slice(b * WIDE, (b + 1) * WIDE)
+        turn = b % 2
+        bias1 = bs_ref[0:1, lanes]
+        bias2 = bs_ref[1:2, lanes]
+        total = dot(x_ref[...], wf_ref[:, lanes])
+        f_ref[turn] = rounded(jnp.maximum(total + bias1, 0.0)).reshape(HEIGHT, MATES, WIDE)
+        packed = f_ref[turn, :, 0:32, :].reshape(HEIGHT * 32, WIDE).astype(BF16)
+        latent = rounded(dot(packed, dn_ref[0:WIDE, :])).reshape(HEIGHT, 32, LANES)
+        given = jnp.concatenate([latent[:, 0:24], pick_ref[b], latent[:, 24:32]], axis=1)
+        both = jnp.concatenate([jnp.where(up_mask, given, 0.0), jnp.where(up_mask, 0.0, given)], axis=2)
+        added = dot(both.reshape(HEIGHT * 40, WIDE).astype(BF16), un_ref[0:WIDE, :]).reshape(HEIGHT, 40, WIDE)
+
+        def mate(y):
+            here = f_ref[turn, y]
+            add = added[y]
+            own = rounded(own_ref[y, :, lanes] + jnp.where(gate24, add[0:24], 0.0))
+            own = jnp.where(ok24, own, 0.0)
+            turned = [swap(own[8 * j : 8 * j + 8]) for j in range(3)]
+            center = jnp.concatenate([half(turned[0], turned[1]), half(turned[1], turned[2])], axis=0)
+            top = (y + 1) * 16
+            s_ref[turn, 0, top : top + 16, :] = own[0:16].astype(BF16)
+            s_ref[turn, 1, top : top + 16, :] = center.astype(BF16)
+            s_ref[turn, 2, top : top + 16, :] = own[8:24].astype(BF16)
+            middle = half(here[8:16], jnp.where(late, here[16:24], here[0:8]))
+            middle = rounded(middle + add[24:32])
+            far = add[32:40]
+            lower = jnp.where(ok_low, rounded(here[32:40] + jnp.where(far_low, far, 0.0)), 0.0)
+            upper = jnp.where(ok_high, rounded(here[40:48] + jnp.where(far_high, far, 0.0)), 0.0)
+            return lower, middle, upper
+
+        def put(r, top, bottom):
+            for dt in range(3):
+                t_ref[turn, dt, r * 16 : (r + 1) * 16, :] = jnp.concatenate([top[dt], bottom[dt]], axis=0).astype(BF16)
+
+        nothing = (zero, zero, zero)
+        for y in range(HALF):
+            top, bottom = mate(y), mate(y + HALF)
+            put(y + 1, top, bottom)
+            if y == 0:
+                put(HALF + 1, bottom, nothing)
+            if y == HALF - 1:
+                put(0, nothing, top)
+
+        acc = jnp.zeros((size + part, WIDE), F32)
+        for tap in range(9):
+            dt, dr = divmod(tap, 3)
+            lhs = jnp.concatenate(
+                [s_ref[turn, dt, dr * 16 : dr * 16 + size, :], t_ref[turn, dt, dr * 16 : dr * 16 + part, :]], axis=0
+            )
+            acc = acc + dot(lhs, w2_ref[tap * WIDE : (tap + 1) * WIDE, :])
+        acc = jnp.maximum(acc + bias2, 0.0)
+        mates = acc[size:] + t_ref[turn, 1, 16 : 16 + part, :].astype(F32)
+        latent = rounded(dot(mates.astype(BF16), dn_ref[WIDE:, :])).reshape(HALF, 16, LANES)
+        both = jnp.concatenate([jnp.where(own_mask, latent, 0.0), jnp.where(own_mask, 0.0, latent)], axis=2)
+        added = dot(both.reshape(part, WIDE).astype(BF16), un_ref[WIDE:, :]).reshape(HALF, 16, WIDE)
+        second = rounded(acc[:size] + s_ref[turn, 1, 16 : 16 + size, :].astype(F32)).reshape(HEIGHT, 16, WIDE)
+        for y in range(HEIGHT):
+            at = (y // HALF) * 8
+            add = added[y % HALF, at : at + 8]
+            add = jnp.concatenate([swap(add), add], axis=0)
+            two = rounded(second[y] + jnp.where(gate16, add, 0.0))
+            c2_ref[b, y] = jnp.where(ok16, two, 0.0)
+
+    lane = iota((16, LANES), 1)
+    left, right = lane < CHANS, lane >= LANES - CHANS
+
+    def filled(y):
+        tiles = []
+        for b in range(BLOCKS):
+            old = pltpu.roll(c2_ref[b - 1, y, :, LANES:], 64, 1) if b else jnp.zeros((16, LANES), F32)
+            tiles.append(jnp.where(left, old, c2_ref[b, y, :, :LANES]))
+            old = pltpu.roll(c2_ref[b + 1, y, :, :LANES], 64, 1) if b + 1 < BLOCKS else jnp.zeros((16, LANES), F32)
+            tiles.append(jnp.where(right, old, c2_ref[b, y, :, LANES:]))
+        whole = jnp.concatenate(tiles, axis=1)
+        low, high = whole[0:8], whole[8:16]
+        keep = iota((8, BLOCKS * WIDE), 0) < 4
+        return low, jnp.where(keep, swap(low), swap(high)), high
+
+    def store(r, top, bottom):
+        for dt in range(3):
+            s3_ref[dt, r * 16 : (r + 1) * 16, :] = jnp.concatenate([top[dt], bottom[dt]], axis=0).astype(BF16)
+
+    nothing = (jnp.zeros((8, BLOCKS * WIDE), F32),) * 3
+    for y in range(HALF):
+        top, bottom = filled(y), filled(y + HALF)
+        store(y + 1, top, bottom)
+        if y == 0:
+            store(HALF + 1, bottom, nothing)
+        if y == HALF - 1:
+            store(0, nothing, top)
+
+    def windows(dt, start):
+        return jnp.concatenate(
+            [s3_ref[dt, start : start + part, b * WIDE : (b + 1) * WIDE] for b in range(BLOCKS)], axis=0
+        )
+
+    acc = jnp.zeros((BLOCKS * part, WIDE), F32)
+    for tap in range(9):
+        dt, dr = divmod(tap, 3)
+        acc = acc + dot(windows(dt, dr * 16), w3_ref[tap * WIDE : (tap + 1) * WIDE, :])
+    logits = jnp.zeros((part, LANES), F32)
+    for b in range(BLOCKS):
+        lanes = slice(b * WIDE, (b + 1) * WIDE)
+        third = jnp.maximum(acc[b * part : (b + 1) * part] + bs_ref[2:3, lanes], 0.0)
+        third = third + s3_ref[1, 16 : 16 + part, lanes].astype(F32)
+        high = third.astype(BF16)
+        rest = (third - high.astype(F32)).astype(BF16)
+        sums = dot(jnp.concatenate([high, rest], axis=0), rd_ref[lanes, :])
+        logits = logits + sums[:part] + sums[part:]
+    finish(logits.reshape(HALF, 16, LANES), cell_ref, out_ref)
+
+
+def finish(logits, cell_ref, out_ref):
+    lane8 = iota((8, LANES), 1)
     flat = [jnp.zeros((8, LANES), F32) for _ in range(FLAT // LANES)]
     for y in range(HEIGHT):
         row = logits[y % HALF, (y // HALF) * 8 : (y // HALF) * 8 + 8]
@@ -440,7 +716,7 @@
         name="pack",
     )(in_hbm(jnp.swapaxes(bits, 2, 3)), in_hbm(partners), gate_round)
 
-    exact = steps <= 4
+    exact = steps == 4 and devices > 1
     if exact:
         blocks = [mine] + [
             lax.ppermute(mine, "tm", [(i, i ^ k) for i in range(steps) if abs(i - (i ^ k)) <= 2])
@@ -484,6 +760,39 @@
     every = jnp.concatenate(parts, axis=0)
     others = swapped(every, "patch", 1)
 
+    if exact:
+        wf, w2, w3, dn, un, rd, bs = weights
+        early = pl.pallas_call(
+            functools.partial(early_kernel, (devices, steps)),
+            out_shape=[
+                jax.ShapeDtypeStruct((HEIGHT, OWN, total), F32),
+                jax.ShapeDtypeStruct((BLOCKS, HEIGHT, 8, LANES), F32),
+                jax.ShapeDtypeStruct((3 * MATES, 8 * steps * devices), BF16),
+                jax.ShapeDtypeStruct((MASK_ROWS, LANES), F32),
+            ],
+            in_specs=[vmem] * 4,
+            out_specs=[vmem] * 4,
+            scratch_shapes=[pltpu.VMEM((HEIGHT * OWN, WIDE), BF16), pltpu.VMEM((8, LANES), F32)],
+            cost_estimate=pl.CostEstimate(flops=10**9, bytes_accessed=10**7, transcendentals=0),
+            compiler_params=pltpu.CompilerParams(vmem_limit_bytes=14 << 20),
+            name="early",
+        )(near, wf, dn, bs)
+        return pl.pallas_call(
+            late_kernel,
+            out_shape=jax.ShapeDtypeStruct((COUNT, DEPTH, HEIGHT * WIDTH), F32),
+            in_specs=[vmem] * 14,
+            out_specs=vmem,
+            scratch_shapes=[
+                pltpu.VMEM((HEIGHT * MATES, WIDE), BF16),
+                pltpu.VMEM((2, HEIGHT, MATES, WIDE), F32),
+                pltpu.VMEM((2, 3, 28 * 16, WIDE), BF16),
+                pltpu.VMEM((2, 3, (HALF + 2) * 16, WIDE), BF16),
+                pltpu.VMEM((BLOCKS, HEIGHT, 16, WIDE), F32),
+                pltpu.VMEM((3, (HALF + 2) * 16, total), BF16),
+            ],
+            compiler_params=pltpu.CompilerParams(vmem_limit_bytes=36 << 20),
+            name="late",
+        )(every, others, *early, wf, w2, w3, dn, un, rd, bs, cell_bias.reshape(1, HEIGHT * WIDTH))
     return pl.pallas_call(
         functools.partial(main_kernel, (devices, steps, exact)),
         out_shape=jax.ShapeDtypeStruct((COUNT, DEPTH, HEIGHT * WIDTH), F32),

time: 39.5 us -> 34.5 us (0.87)
  the two profiles are of different devices: /device:TPU:0 before, /device:TPU:9 now
where the time goes in v3:
time: 34.5 us; the launch traced here: 34.3 us
  Pallas kernels  18.5 us (54%)
  starting transfers between devices  11.4 us (33%)
  waiting for transfers between devices  3.56 us (10%)
  between operations  0.75 us (2%)
    pallas_call x1, Pallas kernels, shards(): pl.pallas_call(late_kernel, out_shape=jax.ShapeDtypeStruct((COUNT, DEPTH,...  13.8 us
    ppermute x4, starting transfers between devices, swapped(): return lax.ppermute(block, axis, [(i, i ^ mask) for i in range(count)])  6.85 us
    ppermute x3, starting transfers between devices, shards(): lax.ppermute(mine, 'tm', [(i, i ^ k) for i in range(steps) if abs(i - (i...  4.6 us
    ppermute x4, waiting for transfers between devices, swapped(): return lax.ppermute(block, axis, [(i, i ^ mask) for i in range(count)])  3.56 us
    pallas_call x1, Pallas kernels, shards(): pl.pallas_call(weights_kernel, out_shape=[jax.ShapeDtypeStruct((WIDE, tot...  2.31 us
    pallas_call x1, Pallas kernels, shards(): pl.pallas_call(functools.partial(early_kernel, (devices, steps)), out_sha...  1.31 us
    pallas_call x1, Pallas kernels, shards(): pl.pallas_call(pack_kernel, out_shape=jax.ShapeDtypeStruct((8, FLAT + LAN...  1.11 us
  transfers between devices with their start and end apart: 7, of which 3 were waited for; matrix products, arithmetic and copies ran while one was open for 0% of the time, Pallas kernels for 11%

profile of v3, /device:TPU:9, one launch (start us, length us, event | category | flops | bytes accessed | tf_op | source)
XLA Modules:
  0.0 34.3 jit_solution(17905732792225605739)
XLA Ops:
  0.7 1.1 %pack.1 = bf16[8,768]{1,0:T(8,128)(2,1)S(1)} custom-call(s32[4,2,24,26]{3,2,1,0:T(8,128)} %bitcast.4, s32[1,32]{1,0:T(1,128)} %partners_hbm.1, s32[1]{0:T(128)S(6)} %copy.11.gate_ref), custom_call_target="tpu_custom_call" | custom-call | tf_op jit(solution)/shard_map/pack/pallas_call | solution.py:705
  1.8 0.1 collective-permute-start
  1.8 2.5 %collective-permute-start.1 = (bf16[8,768]{1,0:T(8,128)(2,1)S(1)}, bf16[8,768]{1,0:T(8,128)(2,1)S(1)}, u32[]{:S(2)}, u32[]{:S(2)}) collective-permute-start(bf16[8,768]{1,0:T(8,128)(2,1)S(1)} %pack.1), channel_id=1, source_target_pairs={{0,2},{1,3},{2,0},{3,1},{4,6},{5,7},{6,4},{7,5},{8,10},{9,11},{10,... | collective-permute-start | bytes 36872 | tf_op jit(solution)/shard_map/ppermute | solution.py:722
  4.3 2.1 %collective-permute-start.2 = (bf16[8,768]{1,0:T(8,128)(2,1)S(1)}, bf16[8,768]{1,0:T(8,128)(2,1)S(1)}, u32[]{:S(2)}, u32[]{:S(2)}) collective-permute-start(bf16[8,768]{1,0:T(8,128)(2,1)S(1)} %pack.1), channel_id=1, source_target_pairs={{1,2},{2,1},{5,6},{6,5},{9,10},{10,9},{13,14},{14,13},{17,18},{18,... | collective-permute-start | bytes 36872 | tf_op jit(solution)/shard_map/ppermute | solution.py:722
  6.4 0.0 copy-start
  6.4 2.3 %weights.1 = (bf16[256,1024]{1,0:T(8,128)(2,1)S(1)}, bf16[2304,256]{1,0:T(8,128)(2,1)S(1)}, bf16[2304,256]{1,0:T(8,128)(2,1)S(1)}, bf16[512,128]{1,0:T(8,128)(2,...) custom-call(bf16[3,3,3,32]{3,2,1,0:T(4,128)(2,1)} %first_hbm.1, ...), custom_call_target="tpu_custom_call" | custom-call | flops 1000000000 | bytes 10000000 | tf_op jit(solution)/shard_map/weights/pallas_call | solution.py:736
  8.7 0.0 collective-permute-done
  8.7 0.0 collective-permute-done.1
  8.7 0.0 collective-permute-done.2
  8.8 1.3 %collective-permute-start.3 = (bf16[32,640]{1,0:T(8,128)(2,1)S(1)}, bf16[32,640]{1,0:T(8,128)(2,1)S(1)}, u32[]{:S(2)}, u32[]{:S(2)}) collective-permute-start(bf16[32,640]{1,0:T(8,128)(2,1)S(1)} %slice.3), channel_id=1, source_target_pairs={{0,8},{4,12},{8,0},{12,4},{16,24},{20,28},{24,16},{28,20},{1,9},{5... | collective-permute-start | bytes 122888 | tf_op jit(solution)/shard_map/ppermute | solution.py:689
  10.1 1.2 %collective-permute-start.4 = (bf16[32,640]{1,0:T(8,128)(2,1)S(1)}, bf16[32,640]{1,0:T(8,128)(2,1)S(1)}, u32[]{:S(2)}, u32[]{:S(2)}) collective-permute-start(bf16[32,640]{1,0:T(8,128)(2,1)S(1)} %slice.3), channel_id=1, source_target_pairs={{0,16},{4,20},{8,24},{12,28},{16,0},{20,4},{24,8},{28,12},{1,17},{... | collective-permute-start | bytes 122888 | tf_op jit(solution)/shard_map/ppermute | solution.py:689
  11.3 0.2 collective-permute-start.5
  11.5 0.2 collective-permute-done.3
  11.7 1.2 %collective-permute-done.4 = bf16[32,640]{1,0:T(8,128)(2,1)S(1)} collective-permute-done((bf16[32,640]{1,0:T(8,128)(2,1)S(1)}, bf16[32,640]{1,0:T(8,128)(2,1)S(1)}, u32[]{:S(2)}, u32[]{:S(2)}) %collective-permute-start.4) | collective-permute-done | bytes 40992 | tf_op jit(solution)/shard_map/ppermute | solution.py:689
  12.9 2.1 %collective-permute-done.5 = bf16[32,640]{1,0:T(8,128)(2,1)S(1)} collective-permute-done((bf16[32,640]{1,0:T(8,128)(2,1)S(1)}, bf16[32,640]{1,0:T(8,128)(2,1)S(1)}, u32[]{:S(2)}, u32[]{:S(2)}) %collective-permute-start.5) | collective-permute-done | bytes 40992 | tf_op jit(solution)/shard_map/ppermute | solution.py:689
  15.1 4.1 %collective-permute-start.6 = (bf16[128,640]{1,0:T(8,128)(2,1)S(1)}, bf16[128,640]{1,0:T(8,128)(2,1)S(1)}, u32[]{:S(2)}, u32[]{:S(2)}) collective-permute-start(bf16[128,640]{1,0:T(8,128)(2,1)S(1)} %pad_maximum_fusion.here_ref), channel_id=1, source_target_pairs={{0,4},{4,0},{8,12},{12,8},{16,20},{20,16},{24,28},{28,24},{1,5},{5... | collective-permute-start | bytes 491528 | tf_op jit(solution)/shard_map/ppermute | solution.py:689
  19.2 0.0 copy-done
  19.2 1.3 %early.1 = (f32[26,24,1024]{2,1,0:T(8,128)S(1)}, f32[4,26,8,128]{3,2,1,0:T(8,128)S(1)}, bf16[144,256]{1,0:T(8,128)(2,1)S(1)}, f32[168,128]{1,0:T(8,128)S(1)}) custom-call(bf16[32,768]{1,0:T(8,128)(2,1)S(1)} %pad_maximum_fusion.1.near_ref, bf16[256,1024]{1,0:T(8,128)(2,1)S(1)} %get-tuple-element.32.wf_ref, bf16[512,128]{1,0:T(8,128)(2,1)S(1)} %get-tuple-element.33.dn_ref, ...), custom_call_target="tpu_custom_call" | custom-call | flops 1000000000 | bytes 10000000 | tf_op jit(solution)/shard_map/early/pallas_call | solution.py:765
  20.5 0.0 collective-permute-done.6.there_ref
  20.5 13.8 %late.1 = f32[4,2,624]{2,1,0:T(2,128)} custom-call(bf16[128,640]{1,0:T(8,128)(2,1)S(1)} %pad_maximum_fusion.here_ref, bf16[128,640]{1,0:T(8,128)(2,1)S(1)} %collective-permute-done.6.there_ref, f32[26,24,1024]{2,1,0:T(8,128)S(1)} %get-tuple-element.35.own_ref, f32[4,26,8,128]{3,2,1,0:T(8,128)S(1)} %get-tuple-element.36.pick_ref, ...), custom_call_target="tpu_custom_call" | custom-call | tf_op jit(solution)/shard_map/late/pallas_call | solution.py:780
  (4 shorter events, 0.0 us)
Async XLA Ops:
  1.8 7.0 %collective-permute-start = (bf16[8,768]{1,0:T(8,128)(2,1)S(1)}, bf16[8,768]{1,0:T(8,128)(2,1)S(1)}, u32[]{:S(2)}, u32[]{:S(2)}) collective-permute-start(bf16[8,768]{1,0:T(8,128)(2,1)S(1)} %pack.1), channel_id=1, source_target_pairs={{0,1},{1,0},{2,3},{3,2},{4,5},{5,4},{6,7},{7,6},{8,9},{9,8},{10,11... | collective-permute-start | bytes 36872 | tf_op jit(solution)/shard_map/ppermute | solution.py:722
  1.8 6.9 %collective-permute-start.1 = (bf16[8,768]{1,0:T(8,128)(2,1)S(1)}, bf16[8,768]{1,0:T(8,128)(2,1)S(1)}, u32[]{:S(2)}, u32[]{:S(2)}) collective-permute-start(bf16[8,768]{1,0:T(8,128)(2,1)S(1)} %pack.1), channel_id=1, source_target_pairs={{0,2},{1,3},{2,0},{3,1},{4,6},{5,7},{6,4},{7,5},{8,10},{9,11},{10,... | collective-permute-start | bytes 36872 | tf_op jit(solution)/shard_map/ppermute | solution.py:722
  4.3 4.4 %collective-permute-start.2 = (bf16[8,768]{1,0:T(8,128)(2,1)S(1)}, bf16[8,768]{1,0:T(8,128)(2,1)S(1)}, u32[]{:S(2)}, u32[]{:S(2)}) collective-permute-start(bf16[8,768]{1,0:T(8,128)(2,1)S(1)} %pack.1), channel_id=1, source_target_pairs={{1,2},{2,1},{5,6},{6,5},{9,10},{10,9},{13,14},{14,13},{17,18},{18,... | collective-permute-start | bytes 36872 | tf_op jit(solution)/shard_map/ppermute | solution.py:722
  6.4 12.8 %copy-start = (f32[624]{0:T(1024)S(1)}, f32[624]{0:T(1024)}, u32[]{:S(2)}) copy-start(f32[624]{0:T(1024)} %param.19) | copy-start | bytes 7492
  8.8 2.9 %collective-permute-start.3 = (bf16[32,640]{1,0:T(8,128)(2,1)S(1)}, bf16[32,640]{1,0:T(8,128)(2,1)S(1)}, u32[]{:S(2)}, u32[]{:S(2)}) collective-permute-start(bf16[32,640]{1,0:T(8,128)(2,1)S(1)} %slice.3), channel_id=1, source_target_pairs={{0,8},{4,12},{8,0},{12,4},{16,24},{20,28},{24,16},{28,20},{1,9},{5... | collective-permute-start | bytes 122888 | tf_op jit(solution)/shard_map/ppermute | solution.py:689
  10.1 2.9 %collective-permute-start.4 = (bf16[32,640]{1,0:T(8,128)(2,1)S(1)}, bf16[32,640]{1,0:T(8,128)(2,1)S(1)}, u32[]{:S(2)}, u32[]{:S(2)}) collective-permute-start(bf16[32,640]{1,0:T(8,128)(2,1)S(1)} %slice.3), channel_id=1, source_target_pairs={{0,16},{4,20},{8,24},{12,28},{16,0},{20,4},{24,8},{28,12},{1,17},{... | collective-permute-start | bytes 122888 | tf_op jit(solution)/shard_map/ppermute | solution.py:689
  11.3 3.8 %collective-permute-start.5 = (bf16[32,640]{1,0:T(8,128)(2,1)S(1)}, bf16[32,640]{1,0:T(8,128)(2,1)S(1)}, u32[]{:S(2)}, u32[]{:S(2)}) collective-permute-start(bf16[32,640]{1,0:T(8,128)(2,1)S(1)} %slice.3), channel_id=1, source_target_pairs={{0,24},{4,28},{8,16},{12,20},{16,8},{20,12},{24,0},{28,4},{1,25},{... | collective-permute-start | bytes 122888 | tf_op jit(solution)/shard_map/ppermute | solution.py:689
  15.1 5.5 %collective-permute-start.6 = (bf16[128,640]{1,0:T(8,128)(2,1)S(1)}, bf16[128,640]{1,0:T(8,128)(2,1)S(1)}, u32[]{:S(2)}, u32[]{:S(2)}) collective-permute-start(bf16[128,640]{1,0:T(8,128)(2,1)S(1)} %pad_maximum_fusion.here_ref), channel_id=1, source_target_pairs={{0,4},{4,0},{8,12},{12,8},{16,20},{20,16},{24,28},{28,24},{1,5},{5... | collective-permute-start | bytes 491528 | tf_op jit(solution)/shard_map/ppermute | solution.py:689

commit v4 on v3

--- a/solution.py
+++ b/solution.py
@@ -546,33 +546,43 @@
     size = HEIGHT * 16
     part = HALF * 16
     zero = jnp.zeros((8, WIDE), F32)
-    s_ref[:, :, 0:16, :] = jnp.zeros((2, 3, 16, WIDE), BF16)
-    s_ref[:, :, 27 * 16 :, :] = jnp.zeros((2, 3, 16, WIDE), BF16)
-
-    for b in range(BLOCKS):
+    s_ref[:, :, 0:16, :] = jnp.zeros((BLOCKS, 3, 16, WIDE), BF16)
+    s_ref[:, :, 27 * 16 :, :] = jnp.zeros((BLOCKS, 3, 16, WIDE), BF16)
+
+    def prepare(b):
         lanes = slice(b * WIDE, (b + 1) * WIDE)
         turn = b % 2
-        bias1 = bs_ref[0:1, lanes]
-        bias2 = bs_ref[1:2, lanes]
-        total = dot(x_ref[...], wf_ref[:, lanes])
-        f_ref[turn] = rounded(jnp.maximum(total + bias1, 0.0)).reshape(HEIGHT, MATES, WIDE)
-        packed = f_ref[turn, :, 0:32, :].reshape(HEIGHT * 32, WIDE).astype(BF16)
-        latent = rounded(dot(packed, dn_ref[0:WIDE, :])).reshape(HEIGHT, 32, LANES)
-        given = jnp.concatenate([latent[:, 0:24], pick_ref[b], latent[:, 24:32]], axis=1)
-        both = jnp.concatenate([jnp.where(up_mask, given, 0.0), jnp.where(up_mask, 0.0, given)], axis=2)
-        added = dot(both.reshape(HEIGHT * 40, WIDE).astype(BF16), un_ref[0:WIDE, :]).reshape(HEIGHT, 40, WIDE)
+        held = {}
+
+        def first():
+            held["total"] = dot(x_ref[...], wf_ref[:, lanes])
+
+        def keep():
+            total = jnp.maximum(held.pop("total") + bs_ref[0:1, lanes], 0.0)
+            f_ref[turn] = rounded(total).reshape(HEIGHT, MATES, WIDE)
+
+        def latents():
+            packed = f_ref[turn, :, 0:32, :].reshape(HEIGHT * 32, WIDE).astype(BF16)
+            held["latent"] = rounded(dot(packed, dn_ref[0:WIDE, :])).reshape(HEIGHT, 32, LANES)
+
+        def ups():
+            latent = held.pop("latent")
+            given = jnp.concatenate([latent[:, 0:24], pick_ref[b], latent[:, 24:32]], axis=1)
+            both = jnp.concatenate([jnp.where(up_mask, given, 0.0), jnp.where(up_mask, 0.0, given)], axis=2)
+            both = both.reshape(HEIGHT * 40, WIDE).astype(BF16)
+            held["added"] = dot(both, un_ref[0:WIDE, :]).reshape(HEIGHT, 40, WIDE)
 
         def mate(y):
             here = f_ref[turn, y]
-            add = added[y]
+            add = held["added"][y]
             own = rounded(own_ref[y, :, lanes] + jnp.where(gate24, add[0:24], 0.0))
             own = jnp.where(ok24, own, 0.0)
             turned = [swap(own[8 * j : 8 * j + 8]) for j in range(3)]
             center = jnp.concatenate([half(turned[0], turned[1]), half(turned[1], turned[2])], axis=0)
             top = (y + 1) * 16
-            s_ref[turn, 0, top : top + 16, :] = own[0:16].astype(BF16)
-            s_ref[turn, 1, top : top + 16, :] = center.astype(BF16)
-            s_ref[turn, 2, top : top + 16, :] = own[8:24].astype(BF16)
+            s_ref[b, 0, top : top + 16, :] = own[0:16].astype(BF16)
+            s_ref[b, 1, top : top + 16, :] = center.astype(BF16)
+            s_ref[b, 2, top : top + 16, :] = own[8:24].astype(BF16)
             middle = half(here[8:16], jnp.where(late, here[16:24], here[0:8]))
             middle = rounded(middle + add[24:32])
             far = add[32:40]
@@ -582,10 +592,10 @@
 
         def put(r, top, bottom):
             for dt in range(3):
-                t_ref[turn, dt, r * 16 : (r + 1) * 16, :] = jnp.concatenate([top[dt], bottom[dt]], axis=0).astype(BF16)
-
-        nothing = (zero, zero, zero)
-        for y in range(HALF):
+                t_ref[b, dt, r * 16 : (r + 1) * 16, :] = jnp.concatenate([top[dt], bottom[dt]], axis=0).astype(BF16)
+
+        def rows(y):
+            nothing = (zero, zero, zero)
             top, bottom = mate(y), mate(y + HALF)
             put(y + 1, top, bottom)
             if y == 0:
@@ -593,73 +603,137 @@
             if y == HALF - 1:
                 put(0, nothing, top)
 
-        acc = jnp.zeros((size + part, WIDE), F32)
-        for tap in range(9):
+        return [first, keep, latents, ups], [functools.partial(rows, y) for y in range(HALF)]
+
+    def convolve(b, held):
+        def step(tap):
             dt, dr = divmod(tap, 3)
             lhs = jnp.concatenate(
-                [s_ref[turn, dt, dr * 16 : dr * 16 + size, :], t_ref[turn, dt, dr * 16 : dr * 16 + part, :]], axis=0
+                [s_ref[b, dt, dr * 16 : dr * 16 + size, :], t_ref[b, dt, dr * 16 : dr * 16 + part, :]], axis=0
             )
-            acc = acc + dot(lhs, w2_ref[tap * WIDE : (tap + 1) * WIDE, :])
-        acc = jnp.maximum(acc + bias2, 0.0)
-        mates = acc[size:] + t_ref[turn, 1, 16 : 16 + part, :].astype(F32)
-        latent = rounded(dot(mates.astype(BF16), dn_ref[WIDE:, :])).reshape(HALF, 16, LANES)
-        both = jnp.concatenate([jnp.where(own_mask, latent, 0.0), jnp.where(own_mask, 0.0, latent)], axis=2)
-        added = dot(both.reshape(part, WIDE).astype(BF16), un_ref[WIDE:, :]).reshape(HALF, 16, WIDE)
-        second = rounded(acc[:size] + s_ref[turn, 1, 16 : 16 + size, :].astype(F32)).reshape(HEIGHT, 16, WIDE)
-        for y in range(HEIGHT):
+            held["acc"] = held.get("acc", jnp.zeros((size + part, WIDE), F32)) + dot(
+                lhs, w2_ref[tap * WIDE : (tap + 1) * WIDE, :]
+            )
+
+        return [functools.partial(step, tap) for tap in range(9)]
+
+    def conclude(b, held):
+        bias2 = bs_ref[1:2, b * WIDE : (b + 1) * WIDE]
+
+        def begin():
+            acc = jnp.maximum(held.pop("acc") + bias2, 0.0)
+            mates = acc[size:] + t_ref[b, 1, 16 : 16 + part, :].astype(F32)
+            held["latent"] = rounded(dot(mates.astype(BF16), dn_ref[WIDE:, :])).reshape(HALF, 16, LANES)
+            held["second"] = rounded(acc[:size] + s_ref[b, 1, 16 : 16 + size, :].astype(F32)).reshape(HEIGHT, 16, WIDE)
+
+        def ups():
+            latent = held.pop("latent")
+            both = jnp.concatenate([jnp.where(own_mask, latent, 0.0), jnp.where(own_mask, 0.0, latent)], axis=2)
+            held["added"] = dot(both.reshape(part, WIDE).astype(BF16), un_ref[WIDE:, :]).reshape(HALF, 16, WIDE)
+
+        def row(y):
             at = (y // HALF) * 8
-            add = added[y % HALF, at : at + 8]
+            add = held["added"][y % HALF, at : at + 8]
             add = jnp.concatenate([swap(add), add], axis=0)
-            two = rounded(second[y] + jnp.where(gate16, add, 0.0))
+            two = rounded(held["second"][y] + jnp.where(gate16, add, 0.0))
             c2_ref[b, y] = jnp.where(ok16, two, 0.0)
+
+        return [begin, ups] + [functools.partial(row, y) for y in range(HEIGHT)]
+
+    def weave(*streams):
+        order = []
+        for s, stream in enumerate(streams):
+            order += [((i + 0.5) / len(stream), s, i) for i in range(len(stream))]
+        for _, s, i in sorted(order):
+            streams[s][i]()
 
     lane = iota((16, LANES), 1)
     left, right = lane < CHANS, lane >= LANES - CHANS
 
-    def filled(y):
-        tiles = []
-        for b in range(BLOCKS):
-            old = pltpu.roll(c2_ref[b - 1, y, :, LANES:], 64, 1) if b else jnp.zeros((16, LANES), F32)
-            tiles.append(jnp.where(left, old, c2_ref[b, y, :, :LANES]))
-            old = pltpu.roll(c2_ref[b + 1, y, :, :LANES], 64, 1) if b + 1 < BLOCKS else jnp.zeros((16, LANES), F32)
-            tiles.append(jnp.where(right, old, c2_ref[b, y, :, LANES:]))
-        whole = jnp.concatenate(tiles, axis=1)
-        low, high = whole[0:8], whole[8:16]
-        keep = iota((8, BLOCKS * WIDE), 0) < 4
-        return low, jnp.where(keep, swap(low), swap(high)), high
-
-    def store(r, top, bottom):
-        for dt in range(3):
-            s3_ref[dt, r * 16 : (r + 1) * 16, :] = jnp.concatenate([top[dt], bottom[dt]], axis=0).astype(BF16)
-
-    nothing = (jnp.zeros((8, BLOCKS * WIDE), F32),) * 3
-    for y in range(HALF):
-        top, bottom = filled(y), filled(y + HALF)
-        store(y + 1, top, bottom)
-        if y == 0:
-            store(HALF + 1, bottom, nothing)
-        if y == HALF - 1:
-            store(0, nothing, top)
-
-    def windows(dt, start):
-        return jnp.concatenate(
-            [s3_ref[dt, start : start + part, b * WIDE : (b + 1) * WIDE] for b in range(BLOCKS)], axis=0
-        )
-
-    acc = jnp.zeros((BLOCKS * part, WIDE), F32)
-    for tap in range(9):
-        dt, dr = divmod(tap, 3)
-        acc = acc + dot(windows(dt, dr * 16), w3_ref[tap * WIDE : (tap + 1) * WIDE, :])
-    logits = jnp.zeros((part, LANES), F32)
+    def spread_rows(pair):
+        width = 2 * WIDE
+        keep = iota((8, width), 0) < 4
+        nothing = (jnp.zeros((8, width), F32),) * 3
+
+        def filled(y):
+            tiles = []
+            for b in (2 * pair, 2 * pair + 1):
+                old = pltpu.roll(c2_ref[b - 1, y, :, LANES:], 64, 1) if b else jnp.zeros((16, LANES), F32)
+                tiles.append(jnp.where(left, old, c2_ref[b, y, :, :LANES]))
+                old = pltpu.roll(c2_ref[b + 1, y, :, :LANES], 64, 1) if b + 1 < BLOCKS else jnp.zeros((16, LANES), F32)
+                tiles.append(jnp.where(right, old, c2_ref[b, y, :, LANES:]))
+            whole = jnp.concatenate(tiles, axis=1)
+            low, high = whole[0:8], whole[8:16]
+            return low, jnp.where(keep, swap(low), swap(high)), high
+
+        def store(r, top, bottom):
+            for dt in range(3):
+                s3_ref[dt, r * 16 : (r + 1) * 16, pair * width : (pair + 1) * width] = jnp.concatenate(
+                    [top[dt], bottom[dt]], axis=0
+                ).astype(BF16)
+
+        def step(y):
+            top, bottom = filled(y), filled(y + HALF)
+            store(y + 1, top, bottom)
+            if y == 0:
+                store(HALF + 1, bottom, nothing)
+            if y == HALF - 1:
+                store(0, nothing, top)
+
+        return [functools.partial(step, y) for y in range(HALF)]
+
+    def last_layer(pair, held):
+        def step(tap):
+            dt, dr = divmod(tap, 3)
+            lhs = jnp.concatenate(
+                [
+                    s3_ref[dt, dr * 16 : dr * 16 + part, b * WIDE : (b + 1) * WIDE]
+                    for b in (2 * pair, 2 * pair + 1)
+                ],
+                axis=0,
+            )
+            held["acc"] = held.get("acc", jnp.zeros((2 * part, WIDE), F32)) + dot(
+                lhs, w3_ref[tap * WIDE : (tap + 1) * WIDE, :]
+            )
+
+        return [functools.partial(step, tap) for tap in range(9)]
+
+    logits = []
+
+    def readout(pair, held):
+        def step(i):
+            b = 2 * pair + i
+            lanes = slice(b * WIDE, (b + 1) * WIDE)
+            third = jnp.maximum(held["acc"][i * part : (i + 1) * part] + bs_ref[2:3, lanes], 0.0)
+            third = third + s3_ref[1, 16 : 16 + part, lanes].astype(F32)
+            high = third.astype(BF16)
+            rest = (third - high.astype(F32)).astype(BF16)
+            sums = dot(jnp.concatenate([high, rest], axis=0), rd_ref[lanes, :])
+            logits.append(sums[:part] + sums[part:])
+
+        return [functools.partial(step, i) for i in range(2)]
+
+    plans = [prepare(b) for b in range(BLOCKS)]
+    helds = [{} for _ in range(BLOCKS)]
+    weave(plans[0][0])
+    weave(plans[0][1], plans[1][0])
     for b in range(BLOCKS):
-        lanes = slice(b * WIDE, (b + 1) * WIDE)
-        third = jnp.maximum(acc[b * part : (b + 1) * part] + bs_ref[2:3, lanes], 0.0)
-        third = third + s3_ref[1, 16 : 16 + part, lanes].astype(F32)
-        high = third.astype(BF16)
-        rest = (third - high.astype(F32)).astype(BF16)
-        sums = dot(jnp.concatenate([high, rest], axis=0), rd_ref[lanes, :])
-        logits = logits + sums[:part] + sums[part:]
-    finish(logits.reshape(HALF, 16, LANES), cell_ref, out_ref)
+        streams = [convolve(b, helds[b])]
+        ends = conclude(b - 1, helds[b - 1]) if b else []
+        if b + 1 < BLOCKS:
+            if ends:
+                streams.append(ends)
+            streams.append(plans[b + 1][1])
+        else:
+            streams.append(ends + spread_rows(0))
+        if b + 2 < BLOCKS:
+            streams.append(plans[b + 2][0])
+        weave(*streams)
+    thirds = [{}, {}]
+    weave(last_layer(0, thirds[0]), conclude(BLOCKS - 1, helds[-1]) + spread_rows(1))
+    weave(last_layer(1, thirds[1]), readout(0, thirds[0]))
+    weave(readout(1, thirds[1]))
+    finish(sum(logits[1:], logits[0]).reshape(HALF, 16, LANES), cell_ref, out_ref)
 
 
 def finish(logits, cell_ref, out_ref):
@@ -719,8 +793,8 @@
     exact = steps == 4 and devices > 1
     if exact:
         blocks = [mine] + [
-            lax.ppermute(mine, "tm", [(i, i ^ k) for i in range(steps) if abs(i - (i ^ k)) <= 2])
-            for k in range(1, steps)
+            lax.ppermute(mine, "tm", [(i, i ^ k if abs(i - (i ^ k)) <= 2 else i) for i in range(steps)])
+            for k in (1, 2, 3)
         ]
     else:
         blocks = [mine] + [shifted(mine, "tm", k) for k in (1, -1, 2, -2)]
@@ -754,10 +828,10 @@
         name="weights",
     )(*map(in_hbm, params))
 
-    near, weights = lax.optimization_barrier((near, weights))
     every = near[:, :FLAT]
     parts = [every] + [swapped(every, "patch", 2 * m) for m in range(1, devices // 2)]
     every = jnp.concatenate(parts, axis=0)
+    every, weights = lax.optimization_barrier((every, weights))
     others = swapped(every, "patch", 1)
 
     if exact:
@@ -785,8 +859,8 @@
             scratch_shapes=[
                 pltpu.VMEM((HEIGHT * MATES, WIDE), BF16),
                 pltpu.VMEM((2, HEIGHT, MATES, WIDE), F32),
-                pltpu.VMEM((2, 3, 28 * 16, WIDE), BF16),
-                pltpu.VMEM((2, 3, (HALF + 2) * 16, WIDE), BF16),
+                pltpu.VMEM((BLOCKS, 3, 28 * 16, WIDE), BF16),
+                pltpu.VMEM((BLOCKS, 3, (HALF + 2) * 16, WIDE), BF16),
                 pltpu.VMEM((BLOCKS, HEIGHT, 16, WIDE), F32),
                 pltpu.VMEM((3, (HALF + 2) * 16, total), BF16),
             ],

time: 34.5 us -> 32.1 us (0.930)
  Pallas kernels: 18.5 us -> 16.1 us
    pallas_call x1, Pallas kernels: 13.8 us -> 11.4 us  [shards(): pl.pallas_call(late_kernel, out_shape=jax.ShapeDtypeStruct((COUNT, DEPTH,...]
    ppermute x4, waiting for transfers between devices: 3.56 us -> 1.21 us  [swapped(): return lax.ppermute(block, axis, [(i, i ^ mask) for i in range(count)])]
    ppermute x3, waiting for transfers between devices: 0.01 us -> 2.34 us  [shards(): lax.ppermute(mine, 'tm', [(i, i ^ k if abs(i - (i ^ k)) <= 2 else i) for...]
  transfers between devices with their start and end apart: 7 -> 7, of which waited for: 3 -> 2; matrix products, arithmetic and copies ran while one was open for 0% -> 0% of each run, Pallas kernels for 11% -> 11%
where the time goes in v4:
time: 32.1 us; the launch traced here: 31.9 us
  Pallas kernels  16.1 us (50%)
  starting transfers between devices  11.5 us (36%)
  waiting for transfers between devices  3.55 us (11%)
  between operations  0.74 us (2%)
    pallas_call x1, Pallas kernels, shards(): pl.pallas_call(late_kernel, out_shape=jax.ShapeDtypeStruct((COUNT, DEPTH,...  11.4 us
    ppermute x4, starting transfers between devices, swapped(): return lax.ppermute(block, axis, [(i, i ^ mask) for i in range(count)])  6.87 us
    ppermute x3, starting transfers between devices, shards(): lax.ppermute(mine, 'tm', [(i, i ^ k if abs(i - (i ^ k)) <= 2 else i) for...  4.6 us
    ppermute x3, waiting for transfers between devices, shards(): lax.ppermute(mine, 'tm', [(i, i ^ k if abs(i - (i ^ k)) <= 2 else i) for...  2.34 us
    pallas_call x1, Pallas kernels, shards(): pl.pallas_call(weights_kernel, out_shape=[jax.ShapeDtypeStruct((WIDE, tot...  2.32 us
    pallas_call x1, Pallas kernels, shards(): pl.pallas_call(functools.partial(early_kernel, (devices, steps)), out_sha...  1.31 us
    ppermute x4, waiting for transfers between devices, swapped(): return lax.ppermute(block, axis, [(i, i ^ mask) for i in range(count)])  1.21 us
    pallas_call x1, Pallas kernels, shards(): pl.pallas_call(pack_kernel, out_shape=jax.ShapeDtypeStruct((8, FLAT + LAN...  1.11 us
  transfers between devices with their start and end apart: 7, of which 2 were waited for; matrix products, arithmetic and copies ran while one was open for 0% of the time, Pallas kernels for 11%

profile of v4, /device:TPU:9, one launch (start us, length us, event | category | flops | bytes accessed | tf_op | source)
XLA Modules:
  0.0 31.9 jit_solution(17557435701681810891)
XLA Ops:
  0.7 1.1 %pack.1 = bf16[8,768]{1,0:T(8,128)(2,1)S(1)} custom-call(s32[4,2,24,26]{3,2,1,0:T(8,128)} %bitcast.4, s32[1,32]{1,0:T(1,128)} %partners_hbm.1, s32[1]{0:T(128)S(6)} %copy.11.gate_ref), custom_call_target="tpu_custom_call" | custom-call | tf_op jit(solution)/shard_map/pack/pallas_call | solution.py:779
  1.8 0.1 collective-permute-start
  1.8 2.5 %collective-permute-start.1 = (bf16[8,768]{1,0:T(8,128)(2,1)S(1)}, bf16[8,768]{1,0:T(8,128)(2,1)S(1)}, u32[]{:S(2)}, u32[]{:S(2)}) collective-permute-start(bf16[8,768]{1,0:T(8,128)(2,1)S(1)} %pack.1), channel_id=1, source_target_pairs={{0,2},{1,3},{2,0},{3,1},{4,6},{5,7},{6,4},{7,5},{8,10},{9,11},{10,... | collective-permute-start | bytes 36872 | tf_op jit(solution)/shard_map/ppermute | solution.py:796
  4.3 2.1 %collective-permute-start.2 = (bf16[8,768]{1,0:T(8,128)(2,1)S(1)}, bf16[8,768]{1,0:T(8,128)(2,1)S(1)}, u32[]{:S(2)}, u32[]{:S(2)}) collective-permute-start(bf16[8,768]{1,0:T(8,128)(2,1)S(1)} %pack.1), channel_id=1, source_target_pairs={{0,0},{1,2},{2,1},{3,3},{4,4},{5,6},{6,5},{7,7},{8,8},{9,10},{10,9... | collective-permute-start | bytes 36872 | tf_op jit(solution)/shard_map/ppermute | solution.py:796
  6.4 0.0 collective-permute-done
  6.4 0.0 collective-permute-done.1
  6.4 2.3 %collective-permute-done.2 = bf16[8,768]{1,0:T(8,128)(2,1)S(1)} collective-permute-done((bf16[8,768]{1,0:T(8,128)(2,1)S(1)}, bf16[8,768]{1,0:T(8,128)(2,1)S(1)}, u32[]{:S(2)}, u32[]{:S(2)}) %collective-permute-start.2) | collective-permute-done | bytes 12320 | tf_op jit(solution)/shard_map/ppermute | solution.py:796
  8.8 1.3 %collective-permute-start.3 = (bf16[32,640]{1,0:T(8,128)(2,1)S(1)}, bf16[32,640]{1,0:T(8,128)(2,1)S(1)}, u32[]{:S(2)}, u32[]{:S(2)}) collective-permute-start(bf16[32,640]{1,0:T(8,128)(2,1)S(1)} %slice.4), channel_id=1, source_target_pairs={{0,8},{4,12},{8,0},{12,4},{16,24},{20,28},{24,16},{28,20},{1,9},{5... | collective-permute-start | bytes 122888 | tf_op jit(solution)/shard_map/ppermute | solution.py:763
  10.0 1.2 %collective-permute-start.4 = (bf16[32,640]{1,0:T(8,128)(2,1)S(1)}, bf16[32,640]{1,0:T(8,128)(2,1)S(1)}, u32[]{:S(2)}, u32[]{:S(2)}) collective-permute-start(bf16[32,640]{1,0:T(8,128)(2,1)S(1)} %slice.4), channel_id=1, source_target_pairs={{0,16},{4,20},{8,24},{12,28},{16,0},{20,4},{24,8},{28,12},{1,17},{... | collective-permute-start | bytes 122888 | tf_op jit(solution)/shard_map/ppermute | solution.py:763
  11.3 0.2 collective-permute-start.5
  11.5 0.0 copy-start
  11.5 2.3 %weights.1 = (bf16[256,1024]{1,0:T(8,128)(2,1)S(1)}, bf16[2304,256]{1,0:T(8,128)(2,1)S(1)}, bf16[2304,256]{1,0:T(8,128)(2,1)S(1)}, bf16[512,128]{1,0:T(8,128)(2,...) custom-call(bf16[3,3,3,32]{3,2,1,0:T(4,128)(2,1)} %first_hbm.1, ...), custom_call_target="tpu_custom_call" | custom-call | flops 1000000000 | bytes 10000000 | tf_op jit(solution)/shard_map/weights/pallas_call | solution.py:810
  13.8 0.0 collective-permute-done.3
  13.8 0.0 collective-permute-done.4
  13.8 1.2 %collective-permute-done.5 = bf16[32,640]{1,0:T(8,128)(2,1)S(1)} collective-permute-done((bf16[32,640]{1,0:T(8,128)(2,1)S(1)}, bf16[32,640]{1,0:T(8,128)(2,1)S(1)}, u32[]{:S(2)}, u32[]{:S(2)}) %collective-permute-start.5) | collective-permute-done | bytes 40992 | tf_op jit(solution)/shard_map/ppermute | solution.py:763
  15.0 4.2 %collective-permute-start.6 = (bf16[128,640]{1,0:T(8,128)(2,1)S(1)}, bf16[128,640]{1,0:T(8,128)(2,1)S(1)}, u32[]{:S(2)}, u32[]{:S(2)}) collective-permute-start(bf16[128,640]{1,0:T(8,128)(2,1)S(1)} %pad_maximum_fusion.here_ref), channel_id=1, source_target_pairs={{0,4},{4,0},{8,12},{12,8},{16,20},{20,16},{24,28},{28,24},{1,5},{5... | collective-permute-start | bytes 491528 | tf_op jit(solution)/shard_map/ppermute | solution.py:763
  19.2 0.0 copy-done
  19.2 1.3 %early.1 = (f32[26,24,1024]{2,1,0:T(8,128)S(1)}, f32[4,26,8,128]{3,2,1,0:T(8,128)S(1)}, bf16[144,256]{1,0:T(8,128)(2,1)S(1)}, f32[168,128]{1,0:T(8,128)S(1)}) custom-call(bf16[32,768]{1,0:T(8,128)(2,1)S(1)} %pad_maximum_fusion.1.near_ref, bf16[256,1024]{1,0:T(8,128)(2,1)S(1)} %get-tuple-element.32.wf_ref, bf16[512,128]{1,0:T(8,128)(2,1)S(1)} %get-tuple-element.33.dn_ref, ...), custom_call_target="tpu_custom_call" | custom-call | flops 1000000000 | bytes 10000000 | tf_op jit(solution)/shard_map/early/pallas_call | solution.py:839
  20.5 0.0 collective-permute-done.6.there_ref
  20.5 11.4 %late.1 = f32[4,2,624]{2,1,0:T(2,128)} custom-call(bf16[128,640]{1,0:T(8,128)(2,1)S(1)} %pad_maximum_fusion.here_ref, bf16[128,640]{1,0:T(8,128)(2,1)S(1)} %collective-permute-done.6.there_ref, f32[26,24,1024]{2,1,0:T(8,128)S(1)} %get-tuple-element.35.own_ref, f32[4,26,8,128]{3,2,1,0:T(8,128)S(1)} %get-tuple-element.36.pick_ref, ...), custom_call_target="tpu_custom_call" | custom-call | tf_op jit(solution)/shard_map/late/pallas_call | solution.py:854
  (4 shorter events, 0.0 us)
Async XLA Ops:
  1.8 4.6 %collective-permute-start = (bf16[8,768]{1,0:T(8,128)(2,1)S(1)}, bf16[8,768]{1,0:T(8,128)(2,1)S(1)}, u32[]{:S(2)}, u32[]{:S(2)}) collective-permute-start(bf16[8,768]{1,0:T(8,128)(2,1)S(1)} %pack.1), channel_id=1, source_target_pairs={{0,1},{1,0},{2,3},{3,2},{4,5},{5,4},{6,7},{7,6},{8,9},{9,8},{10,11... | collective-permute-start | bytes 36872 | tf_op jit(solution)/shard_map/ppermute | solution.py:796
  1.8 4.6 %collective-permute-start.1 = (bf16[8,768]{1,0:T(8,128)(2,1)S(1)}, bf16[8,768]{1,0:T(8,128)(2,1)S(1)}, u32[]{:S(2)}, u32[]{:S(2)}) collective-permute-start(bf16[8,768]{1,0:T(8,128)(2,1)S(1)} %pack.1), channel_id=1, source_target_pairs={{0,2},{1,3},{2,0},{3,1},{4,6},{5,7},{6,4},{7,5},{8,10},{9,11},{10,... | collective-permute-start | bytes 36872 | tf_op jit(solution)/shard_map/ppermute | solution.py:796
  4.3 4.4 %collective-permute-start.2 = (bf16[8,768]{1,0:T(8,128)(2,1)S(1)}, bf16[8,768]{1,0:T(8,128)(2,1)S(1)}, u32[]{:S(2)}, u32[]{:S(2)}) collective-permute-start(bf16[8,768]{1,0:T(8,128)(2,1)S(1)} %pack.1), channel_id=1, source_target_pairs={{0,0},{1,2},{2,1},{3,3},{4,4},{5,6},{6,5},{7,7},{8,8},{9,10},{10,9... | collective-permute-start | bytes 36872 | tf_op jit(solution)/shard_map/ppermute | solution.py:796
  8.8 5.0 %collective-permute-start.3 = (bf16[32,640]{1,0:T(8,128)(2,1)S(1)}, bf16[32,640]{1,0:T(8,128)(2,1)S(1)}, u32[]{:S(2)}, u32[]{:S(2)}) collective-permute-start(bf16[32,640]{1,0:T(8,128)(2,1)S(1)} %slice.4), channel_id=1, source_target_pairs={{0,8},{4,12},{8,0},{12,4},{16,24},{20,28},{24,16},{28,20},{1,9},{5... | collective-permute-start | bytes 122888 | tf_op jit(solution)/shard_map/ppermute | solution.py:763
  10.0 3.8 %collective-permute-start.4 = (bf16[32,640]{1,0:T(8,128)(2,1)S(1)}, bf16[32,640]{1,0:T(8,128)(2,1)S(1)}, u32[]{:S(2)}, u32[]{:S(2)}) collective-permute-start(bf16[32,640]{1,0:T(8,128)(2,1)S(1)} %slice.4), channel_id=1, source_target_pairs={{0,16},{4,20},{8,24},{12,28},{16,0},{20,4},{24,8},{28,12},{1,17},{... | collective-permute-start | bytes 122888 | tf_op jit(solution)/shard_map/ppermute | solution.py:763
  11.3 3.8 %collective-permute-start.5 = (bf16[32,640]{1,0:T(8,128)(2,1)S(1)}, bf16[32,640]{1,0:T(8,128)(2,1)S(1)}, u32[]{:S(2)}, u32[]{:S(2)}) collective-permute-start(bf16[32,640]{1,0:T(8,128)(2,1)S(1)} %slice.4), channel_id=1, source_target_pairs={{0,24},{4,28},{8,16},{12,20},{16,8},{20,12},{24,0},{28,4},{1,25},{... | collective-permute-start | bytes 122888 | tf_op jit(solution)/shard_map/ppermute | solution.py:763
  11.5 7.7 %copy-start = (f32[624]{0:T(1024)S(1)}, f32[624]{0:T(1024)}, u32[]{:S(2)}) copy-start(f32[624]{0:T(1024)} %param.19) | copy-start | bytes 7492
  15.0 5.5 %collective-permute-start.6 = (bf16[128,640]{1,0:T(8,128)(2,1)S(1)}, bf16[128,640]{1,0:T(8,128)(2,1)S(1)}, u32[]{:S(2)}, u32[]{:S(2)}) collective-permute-start(bf16[128,640]{1,0:T(8,128)(2,1)S(1)} %pad_maximum_fusion.here_ref), channel_id=1, source_target_pairs={{0,4},{4,0},{8,12},{12,8},{16,20},{20,16},{24,28},{28,24},{1,5},{5... | collective-permute-start | bytes 491528 | tf_op jit(solution)/shard_map/ppermute | solution.py:763

commit v5 on v4

--- a/solution.py
+++ b/solution.py
@@ -499,13 +499,14 @@
         choose = (patch_of == unit % COUNT) & (round_of == first_round + unit // 4 + (dt - 1))
         gathered.append(dot(choose.astype(F32).astype(BF16), near_ref[:, :FLAT]))
     event_rows(gathered, x_ref, OWN)
+    kept = jnp.concatenate([values["ok24"]] * 2, axis=1) > 0.5
     ahead = [moments[j] == round24[8 * j : 8 * j + 8] for j in range(3)]
     for b in range(BLOCKS):
         lanes = slice(b * WIDE, (b + 1) * WIDE)
         total = dot(x_ref[...], wf_ref[:, lanes])
         own = rounded(jnp.maximum(total + bs_ref[0:1, lanes], 0.0))
-        own_ref[:, :, lanes] = own.reshape(HEIGHT, OWN, WIDE)
-        latent = rounded(dot(own.astype(BF16), dn_ref[0:WIDE, :])).reshape(HEIGHT, OWN, LANES)
+        own_ref[:, :, lanes] = jnp.where(kept, own.reshape(HEIGHT, OWN, WIDE), 0.0)
+        latent = dot(own.astype(BF16), dn_ref[0:WIDE, :]).reshape(HEIGHT, OWN, LANES)
         for y in range(HEIGHT):
             mine = [latent[y, 8 * j : 8 * j + 8] for j in range(3)]
             mine = [jnp.where(ahead[j], mine[j], pltpu.roll(mine[j], 4, 0)) for j in range(3)]
@@ -539,7 +540,7 @@
         return jnp.where(half_mask, a, b)
 
     up_mask = mask("up", False)
-    gate24, ok24 = mask("gate24"), mask("ok24")
+    gate24 = mask("gate24")
     ok_low, ok_high, far_low, far_high = mask("low"), mask("high"), mask("far_low"), mask("far_high")
     own_mask = mask("own", False)
     gate16, ok16 = mask("gate16"), mask("ok16")
@@ -559,11 +560,11 @@
 
         def keep():
             total = jnp.maximum(held.pop("total") + bs_ref[0:1, lanes], 0.0)
-            f_ref[turn] = rounded(total).reshape(HEIGHT, MATES, WIDE)
+            f_ref[turn] = total.astype(BF16).reshape(HEIGHT, MATES, WIDE)
 
         def latents():
-            packed = f_ref[turn, :, 0:32, :].reshape(HEIGHT * 32, WIDE).astype(BF16)
-            held["latent"] = rounded(dot(packed, dn_ref[0:WIDE, :])).reshape(HEIGHT, 32, LANES)
+            packed = f_ref[turn, :, 0:32, :].reshape(HEIGHT * 32, WIDE)
+            held["latent"] = dot(packed, dn_ref[0:WIDE, :]).reshape(HEIGHT, 32, LANES)
 
         def ups():
             latent = held.pop("latent")
@@ -573,10 +574,9 @@
             held["added"] = dot(both, un_ref[0:WIDE, :]).reshape(HEIGHT, 40, WIDE)
 
         def mate(y):
-            here = f_ref[turn, y]
+            here = f_ref[turn, y].astype(F32)
             add = held["added"][y]
-            own = rounded(own_ref[y, :, lanes] + jnp.where(gate24, add[0:24], 0.0))
-            own = jnp.where(ok24, own, 0.0)
+            own = own_ref[y, :, lanes] + jnp.where(gate24, add[0:24], 0.0)
             turned = [swap(own[8 * j : 8 * j + 8]) for j in range(3)]
             center = jnp.concatenate([half(turned[0], turned[1]), half(turned[1], turned[2])], axis=0)
             top = (y + 1) * 16
@@ -584,10 +584,10 @@
             s_ref[b, 1, top : top + 16, :] = center.astype(BF16)
             s_ref[b, 2, top : top + 16, :] = own[8:24].astype(BF16)
             middle = half(here[8:16], jnp.where(late, here[16:24], here[0:8]))
-            middle = rounded(middle + add[24:32])
+            middle = middle + add[24:32]
             far = add[32:40]
-            lower = jnp.where(ok_low, rounded(here[32:40] + jnp.where(far_low, far, 0.0)), 0.0)
-            upper = jnp.where(ok_high, rounded(here[40:48] + jnp.where(far_high, far, 0.0)), 0.0)
+            lower = jnp.where(ok_low, here[32:40] + jnp.where(far_low, far, 0.0), 0.0)
+            upper = jnp.where(ok_high, here[40:48] + jnp.where(far_high, far, 0.0), 0.0)
             return lower, middle, upper
 
         def put(r, top, bottom):
@@ -604,6 +604,17 @@
                 put(0, nothing, top)
 
         return [first, keep, latents, ups], [functools.partial(rows, y) for y in range(HALF)]
+
+    def convolve_part(b, held, name):
+        ref, rows = (t_ref, part) if name == "mates" else (s_ref, size)
+
+        def step(tap):
+            dt, dr = divmod(tap, 3)
+            held[name] = held.get(name, jnp.zeros((rows, WIDE), F32)) + dot(
+                ref[b, dt, dr * 16 : dr * 16 + rows, :], w2_ref[tap * WIDE : (tap + 1) * WIDE, :]
+            )
+
+        return [functools.partial(step, tap) for tap in range(9)]
 
     def convolve(b, held):
         def step(tap):
@@ -621,10 +632,11 @@
         bias2 = bs_ref[1:2, b * WIDE : (b + 1) * WIDE]
 
         def begin():
-            acc = jnp.maximum(held.pop("acc") + bias2, 0.0)
-            mates = acc[size:] + t_ref[b, 1, 16 : 16 + part, :].astype(F32)
-            held["latent"] = rounded(dot(mates.astype(BF16), dn_ref[WIDE:, :])).reshape(HALF, 16, LANES)
-            held["second"] = rounded(acc[:size] + s_ref[b, 1, 16 : 16 + size, :].astype(F32)).reshape(HEIGHT, 16, WIDE)
+            if "acc" in held:
+                acc = held.pop("acc")
+                held["own"], held["mates"] = acc[:size], acc[size:]
+            mates = jnp.maximum(held.pop("mates") + bias2, 0.0) + t_ref[b, 1, 16 : 16 + part, :].astype(F32)
+            held["latent"] = dot(mates.astype(BF16), dn_ref[WIDE:, :]).reshape(HALF, 16, LANES)
 
         def ups():
             latent = held.pop("latent")
@@ -635,7 +647,9 @@
             at = (y // HALF) * 8
             add = held["added"][y % HALF, at : at + 8]
             add = jnp.concatenate([swap(add), add], axis=0)
-            two = rounded(held["second"][y] + jnp.where(gate16, add, 0.0))
+            second = jnp.maximum(held["own"][y * 16 : y * 16 + 16] + bias2, 0.0)
+            second = rounded(second + s_ref[b, 1, (y + 1) * 16 : (y + 2) * 16, :].astype(F32))
+            two = second + jnp.where(gate16, add, 0.0)
             c2_ref[b, y] = jnp.where(ok16, two, 0.0)
 
         return [begin, ups] + [functools.partial(row, y) for y in range(HEIGHT)]
@@ -717,20 +731,24 @@
     helds = [{} for _ in range(BLOCKS)]
     weave(plans[0][0])
     weave(plans[0][1], plans[1][0])
-    for b in range(BLOCKS):
+    for b in range(BLOCKS - 1):
         streams = [convolve(b, helds[b])]
-        ends = conclude(b - 1, helds[b - 1]) if b else []
-        if b + 1 < BLOCKS:
-            if ends:
-                streams.append(ends)
-            streams.append(plans[b + 1][1])
-        else:
-            streams.append(ends + spread_rows(0))
+        if b:
+            streams.append(conclude(b - 1, helds[b - 1]))
+        streams.append(plans[b + 1][1])
         if b + 2 < BLOCKS:
             streams.append(plans[b + 2][0])
         weave(*streams)
+    final = BLOCKS - 1
+    weave(convolve_part(final, helds[final], "mates"), conclude(final - 1, helds[final - 1]))
+    ends = conclude(final, helds[final])
+    weave(convolve_part(final, helds[final], "own"), ends[:2], spread_rows(0))
     thirds = [{}, {}]
-    weave(last_layer(0, thirds[0]), conclude(BLOCKS - 1, helds[-1]) + spread_rows(1))
+    places = spread_rows(1)
+    rest = []
+    for y in range(HALF):
+        rest += [ends[2 + y], ends[2 + y + HALF], places[y]]
+    weave(last_layer(0, thirds[0]), rest)
     weave(last_layer(1, thirds[1]), readout(0, thirds[0]))
     weave(readout(1, thirds[1]))
     finish(sum(logits[1:], logits[0]).reshape(HALF, 16, LANES), cell_ref, out_ref)
@@ -858,7 +876,7 @@
             out_specs=vmem,
             scratch_shapes=[
                 pltpu.VMEM((HEIGHT * MATES, WIDE), BF16),
-                pltpu.VMEM((2, HEIGHT, MATES, WIDE), F32),
+                pltpu.VMEM((2, HEIGHT, MATES, WIDE), BF16),
                 pltpu.VMEM((BLOCKS, 3, 28 * 16, WIDE), BF16),
                 pltpu.VMEM((BLOCKS, 3, (HALF + 2) * 16, WIDE), BF16),
                 pltpu.VMEM((BLOCKS, HEIGHT, 16, WIDE), F32),

time: 32.1 us -> 31.4 us (0.978)
  Pallas kernels: 16.1 us -> 15.5 us
    pallas_call x1, Pallas kernels: 11.4 us -> 10.7 us  [shards(): pl.pallas_call(late_kernel, out_shape=jax.ShapeDtypeStruct((COUNT, DEPTH,...]
  transfers between devices with their start and end apart: 7 -> 7, of which waited for: 2 -> 2; matrix products, arithmetic and copies ran while one was open for 0% -> 0% of each run, Pallas kernels for 11% -> 12%
where the time goes in v5:
time: 31.4 us; the launch traced here: 31.3 us
  Pallas kernels  15.5 us (49%)
  starting transfers between devices  11.5 us (37%)
  waiting for transfers between devices  3.55 us (11%)
  between operations  0.74 us (2%)
    pallas_call x1, Pallas kernels, shards(): pl.pallas_call(late_kernel, out_shape=jax.ShapeDtypeStruct((COUNT, DEPTH,...  10.7 us
    ppermute x4, starting transfers between devices, swapped(): return lax.ppermute(block, axis, [(i, i ^ mask) for i in range(count)])  6.87 us
    ppermute x3, starting transfers between devices, shards(): lax.ppermute(mine, 'tm', [(i, i ^ k if abs(i - (i ^ k)) <= 2 else i) for...  4.6 us
    ppermute x3, waiting for transfers between devices, shards(): lax.ppermute(mine, 'tm', [(i, i ^ k if abs(i - (i ^ k)) <= 2 else i) for...  2.34 us
    pallas_call x1, Pallas kernels, shards(): pl.pallas_call(weights_kernel, out_shape=[jax.ShapeDtypeStruct((WIDE, tot...  2.32 us
    pallas_call x1, Pallas kernels, shards(): pl.pallas_call(functools.partial(early_kernel, (devices, steps)), out_sha...  1.31 us
    ppermute x4, waiting for transfers between devices, swapped(): return lax.ppermute(block, axis, [(i, i ^ mask) for i in range(count)])  1.21 us
    pallas_call x1, Pallas kernels, shards(): pl.pallas_call(pack_kernel, out_shape=jax.ShapeDtypeStruct((8, FLAT + LAN...  1.11 us
  transfers between devices with their start and end apart: 7, of which 2 were waited for; matrix products, arithmetic and copies ran while one was open for 0% of the time, Pallas kernels for 12%

profile of v5, /device:TPU:9, one launch (start us, length us, event | category | flops | bytes accessed | tf_op | source)
XLA Modules:
  0.0 31.3 jit_solution(8014472493770197758)
XLA Ops:
  0.7 1.1 %pack.1 = bf16[8,768]{1,0:T(8,128)(2,1)S(1)} custom-call(s32[4,2,24,26]{3,2,1,0:T(8,128)} %bitcast.4, s32[1,32]{1,0:T(1,128)} %partners_hbm.1, s32[1]{0:T(128)S(6)} %copy.11.gate_ref), custom_call_target="tpu_custom_call" | custom-call | tf_op jit(solution)/shard_map/pack/pallas_call | solution.py:797
  1.8 0.1 collective-permute-start
  1.8 2.5 %collective-permute-start.1 = (bf16[8,768]{1,0:T(8,128)(2,1)S(1)}, bf16[8,768]{1,0:T(8,128)(2,1)S(1)}, u32[]{:S(2)}, u32[]{:S(2)}) collective-permute-start(bf16[8,768]{1,0:T(8,128)(2,1)S(1)} %pack.1), channel_id=1, source_target_pairs={{0,2},{1,3},{2,0},{3,1},{4,6},{5,7},{6,4},{7,5},{8,10},{9,11},{10,... | collective-permute-start | bytes 36872 | tf_op jit(solution)/shard_map/ppermute | solution.py:814
  4.3 2.1 %collective-permute-start.2 = (bf16[8,768]{1,0:T(8,128)(2,1)S(1)}, bf16[8,768]{1,0:T(8,128)(2,1)S(1)}, u32[]{:S(2)}, u32[]{:S(2)}) collective-permute-start(bf16[8,768]{1,0:T(8,128)(2,1)S(1)} %pack.1), channel_id=1, source_target_pairs={{0,0},{1,2},{2,1},{3,3},{4,4},{5,6},{6,5},{7,7},{8,8},{9,10},{10,9... | collective-permute-start | bytes 36872 | tf_op jit(solution)/shard_map/ppermute | solution.py:814
  6.4 0.0 collective-permute-done
  6.4 0.0 collective-permute-done.1
  6.4 2.3 %collective-permute-done.2 = bf16[8,768]{1,0:T(8,128)(2,1)S(1)} collective-permute-done((bf16[8,768]{1,0:T(8,128)(2,1)S(1)}, bf16[8,768]{1,0:T(8,128)(2,1)S(1)}, u32[]{:S(2)}, u32[]{:S(2)}) %collective-permute-start.2) | collective-permute-done | bytes 12320 | tf_op jit(solution)/shard_map/ppermute | solution.py:814
  8.8 1.3 %collective-permute-start.3 = (bf16[32,640]{1,0:T(8,128)(2,1)S(1)}, bf16[32,640]{1,0:T(8,128)(2,1)S(1)}, u32[]{:S(2)}, u32[]{:S(2)}) collective-permute-start(bf16[32,640]{1,0:T(8,128)(2,1)S(1)} %slice.4), channel_id=1, source_target_pairs={{0,8},{4,12},{8,0},{12,4},{16,24},{20,28},{24,16},{28,20},{1,9},{5... | collective-permute-start | bytes 122888 | tf_op jit(solution)/shard_map/ppermute | solution.py:781
  10.0 1.2 %collective-permute-start.4 = (bf16[32,640]{1,0:T(8,128)(2,1)S(1)}, bf16[32,640]{1,0:T(8,128)(2,1)S(1)}, u32[]{:S(2)}, u32[]{:S(2)}) collective-permute-start(bf16[32,640]{1,0:T(8,128)(2,1)S(1)} %slice.4), channel_id=1, source_target_pairs={{0,16},{4,20},{8,24},{12,28},{16,0},{20,4},{24,8},{28,12},{1,17},{... | collective-permute-start | bytes 122888 | tf_op jit(solution)/shard_map/ppermute | solution.py:781
  11.3 0.2 collective-permute-start.5
  11.5 0.0 copy-start
  11.5 2.3 %weights.1 = (bf16[256,1024]{1,0:T(8,128)(2,1)S(1)}, bf16[2304,256]{1,0:T(8,128)(2,1)S(1)}, bf16[2304,256]{1,0:T(8,128)(2,1)S(1)}, bf16[512,128]{1,0:T(8,128)(2,...) custom-call(bf16[3,3,3,32]{3,2,1,0:T(4,128)(2,1)} %first_hbm.1, ...), custom_call_target="tpu_custom_call" | custom-call | flops 1000000000 | bytes 10000000 | tf_op jit(solution)/shard_map/weights/pallas_call | solution.py:828
  13.8 0.0 collective-permute-done.3
  13.8 0.0 collective-permute-done.4
  13.8 1.2 %collective-permute-done.5 = bf16[32,640]{1,0:T(8,128)(2,1)S(1)} collective-permute-done((bf16[32,640]{1,0:T(8,128)(2,1)S(1)}, bf16[32,640]{1,0:T(8,128)(2,1)S(1)}, u32[]{:S(2)}, u32[]{:S(2)}) %collective-permute-start.5) | collective-permute-done | bytes 40992 | tf_op jit(solution)/shard_map/ppermute | solution.py:781
  15.0 4.2 %collective-permute-start.6 = (bf16[128,640]{1,0:T(8,128)(2,1)S(1)}, bf16[128,640]{1,0:T(8,128)(2,1)S(1)}, u32[]{:S(2)}, u32[]{:S(2)}) collective-permute-start(bf16[128,640]{1,0:T(8,128)(2,1)S(1)} %pad_maximum_fusion.here_ref), channel_id=1, source_target_pairs={{0,4},{4,0},{8,12},{12,8},{16,20},{20,16},{24,28},{28,24},{1,5},{5... | collective-permute-start | bytes 491528 | tf_op jit(solution)/shard_map/ppermute | solution.py:781
  19.2 0.0 copy-done
  19.2 1.3 %early.1 = (f32[26,24,1024]{2,1,0:T(8,128)S(1)}, f32[4,26,8,128]{3,2,1,0:T(8,128)S(1)}, bf16[144,256]{1,0:T(8,128)(2,1)S(1)}, f32[168,128]{1,0:T(8,128)S(1)}) custom-call(bf16[32,768]{1,0:T(8,128)(2,1)S(1)} %pad_maximum_fusion.1.near_ref, bf16[256,1024]{1,0:T(8,128)(2,1)S(1)} %get-tuple-element.32.wf_ref, bf16[512,128]{1,0:T(8,128)(2,1)S(1)} %get-tuple-element.33.dn_ref, ...), custom_call_target="tpu_custom_call" | custom-call | flops 1000000000 | bytes 10000000 | tf_op jit(solution)/shard_map/early/pallas_call | solution.py:857
  20.5 0.0 collective-permute-done.6.there_ref
  20.5 10.7 %late.1 = f32[4,2,624]{2,1,0:T(2,128)} custom-call(bf16[128,640]{1,0:T(8,128)(2,1)S(1)} %pad_maximum_fusion.here_ref, bf16[128,640]{1,0:T(8,128)(2,1)S(1)} %collective-permute-done.6.there_ref, f32[26,24,1024]{2,1,0:T(8,128)S(1)} %get-tuple-element.35.own_ref, f32[4,26,8,128]{3,2,1,0:T(8,128)S(1)} %get-tuple-element.36.pick_ref, ...), custom_call_target="tpu_custom_call" | custom-call | tf_op jit(solution)/shard_map/late/pallas_call | solution.py:872
  (4 shorter events, 0.0 us)
Async XLA Ops:
  1.8 4.6 %collective-permute-start = (bf16[8,768]{1,0:T(8,128)(2,1)S(1)}, bf16[8,768]{1,0:T(8,128)(2,1)S(1)}, u32[]{:S(2)}, u32[]{:S(2)}) collective-permute-start(bf16[8,768]{1,0:T(8,128)(2,1)S(1)} %pack.1), channel_id=1, source_target_pairs={{0,1},{1,0},{2,3},{3,2},{4,5},{5,4},{6,7},{7,6},{8,9},{9,8},{10,11... | collective-permute-start | bytes 36872 | tf_op jit(solution)/shard_map/ppermute | solution.py:814
  1.8 4.6 %collective-permute-start.1 = (bf16[8,768]{1,0:T(8,128)(2,1)S(1)}, bf16[8,768]{1,0:T(8,128)(2,1)S(1)}, u32[]{:S(2)}, u32[]{:S(2)}) collective-permute-start(bf16[8,768]{1,0:T(8,128)(2,1)S(1)} %pack.1), channel_id=1, source_target_pairs={{0,2},{1,3},{2,0},{3,1},{4,6},{5,7},{6,4},{7,5},{8,10},{9,11},{10,... | collective-permute-start | bytes 36872 | tf_op jit(solution)/shard_map/ppermute | solution.py:814
  4.3 4.4 %collective-permute-start.2 = (bf16[8,768]{1,0:T(8,128)(2,1)S(1)}, bf16[8,768]{1,0:T(8,128)(2,1)S(1)}, u32[]{:S(2)}, u32[]{:S(2)}) collective-permute-start(bf16[8,768]{1,0:T(8,128)(2,1)S(1)} %pack.1), channel_id=1, source_target_pairs={{0,0},{1,2},{2,1},{3,3},{4,4},{5,6},{6,5},{7,7},{8,8},{9,10},{10,9... | collective-permute-start | bytes 36872 | tf_op jit(solution)/shard_map/ppermute | solution.py:814
  8.8 5.0 %collective-permute-start.3 = (bf16[32,640]{1,0:T(8,128)(2,1)S(1)}, bf16[32,640]{1,0:T(8,128)(2,1)S(1)}, u32[]{:S(2)}, u32[]{:S(2)}) collective-permute-start(bf16[32,640]{1,0:T(8,128)(2,1)S(1)} %slice.4), channel_id=1, source_target_pairs={{0,8},{4,12},{8,0},{12,4},{16,24},{20,28},{24,16},{28,20},{1,9},{5... | collective-permute-start | bytes 122888 | tf_op jit(solution)/shard_map/ppermute | solution.py:781
  10.0 3.8 %collective-permute-start.4 = (bf16[32,640]{1,0:T(8,128)(2,1)S(1)}, bf16[32,640]{1,0:T(8,128)(2,1)S(1)}, u32[]{:S(2)}, u32[]{:S(2)}) collective-permute-start(bf16[32,640]{1,0:T(8,128)(2,1)S(1)} %slice.4), channel_id=1, source_target_pairs={{0,16},{4,20},{8,24},{12,28},{16,0},{20,4},{24,8},{28,12},{1,17},{... | collective-permute-start | bytes 122888 | tf_op jit(solution)/shard_map/ppermute | solution.py:781
  11.3 3.8 %collective-permute-start.5 = (bf16[32,640]{1,0:T(8,128)(2,1)S(1)}, bf16[32,640]{1,0:T(8,128)(2,1)S(1)}, u32[]{:S(2)}, u32[]{:S(2)}) collective-permute-start(bf16[32,640]{1,0:T(8,128)(2,1)S(1)} %slice.4), channel_id=1, source_target_pairs={{0,24},{4,28},{8,16},{12,20},{16,8},{20,12},{24,0},{28,4},{1,25},{... | collective-permute-start | bytes 122888 | tf_op jit(solution)/shard_map/ppermute | solution.py:781
  11.5 7.7 %copy-start = (f32[624]{0:T(1024)S(1)}, f32[624]{0:T(1024)}, u32[]{:S(2)}) copy-start(f32[624]{0:T(1024)} %param.19) | copy-start | bytes 7492
  15.0 5.5 %collective-permute-start.6 = (bf16[128,640]{1,0:T(8,128)(2,1)S(1)}, bf16[128,640]{1,0:T(8,128)(2,1)S(1)}, u32[]{:S(2)}, u32[]{:S(2)}) collective-permute-start(bf16[128,640]{1,0:T(8,128)(2,1)S(1)} %pad_maximum_fusion.here_ref), channel_id=1, source_target_pairs={{0,4},{4,0},{8,12},{12,8},{16,20},{20,16},{24,28},{28,24},{1,5},{5... | collective-permute-start | bytes 491528 | tf_op jit(solution)/shard_map/ppermute | solution.py:781

commit v6 on v5

--- a/solution.py
+++ b/solution.py
@@ -6,6 +6,7 @@
 from jax.experimental import pallas as pl
 from jax.experimental.pallas import tpu as pltpu
 from jax.sharding import PartitionSpec as P
+
 
 F32 = jnp.float32
 BF16 = jnp.bfloat16
@@ -20,7 +21,7 @@
 BLOCKS = WIDTH // WINDOW
 WIDE = SLOTS * CHANS
 FLAT = 640
-OWN, MATE, UNITS = 24, 16, 96
+OWN, UNITS = 24, 96
 HALF = HEIGHT // 2
 
 
@@ -810,10 +811,10 @@
 
     exact = steps == 4 and devices > 1
     if exact:
-        blocks = [mine] + [
-            lax.ppermute(mine, "tm", [(i, i ^ k if abs(i - (i ^ k)) <= 2 else i) for i in range(steps)])
-            for k in (1, 2, 3)
-        ]
+        blocks = [mine]
+        for k in range(1, steps):
+            pairs = [(i, i ^ k if abs(i - (i ^ k)) <= 2 else i) for i in range(steps)]
+            blocks.append(lax.ppermute(mine, "tm", pairs))
     else:
         blocks = [mine] + [shifted(mine, "tm", k) for k in (1, -1, 2, -2)]
     near = jnp.concatenate(blocks, axis=0)
@@ -847,7 +848,9 @@
     )(*map(in_hbm, params))
 
     every = near[:, :FLAT]
-    parts = [every] + [swapped(every, "patch", 2 * m) for m in range(1, devices // 2)]
+    parts = [every]
+    for m in range(1, devices // 2):
+        parts.append(swapped(every, "patch", 2 * m))
     every = jnp.concatenate(parts, axis=0)
     every, weights = lax.optimization_barrier((every, weights))
     others = swapped(every, "patch", 1)

time: 31.4 us -> 31.4 us (level)
  no operation moved by 1% of the time
where the time goes in v6:
time: 31.4 us; the launch traced here: 31.3 us
  Pallas kernels  15.5 us (49%)
  starting transfers between devices  11.5 us (37%)
  waiting for transfers between devices  3.55 us (11%)
  between operations  0.74 us (2%)
    pallas_call x1, Pallas kernels, shards(): pl.pallas_call(late_kernel, out_shape=jax.ShapeDtypeStruct((COUNT, DEPTH,...  10.7 us
    ppermute x4, starting transfers between devices, swapped(): return lax.ppermute(block, axis, [(i, i ^ mask) for i in range(count)])  6.87 us
    ppermute x3, starting transfers between devices, shards(): blocks.append(lax.ppermute(mine, 'tm', pairs))  4.6 us
    ppermute x3, waiting for transfers between devices, shards(): blocks.append(lax.ppermute(mine, 'tm', pairs))  2.34 us
    pallas_call x1, Pallas kernels, shards(): pl.pallas_call(weights_kernel, out_shape=[jax.ShapeDtypeStruct((WIDE, tot...  2.32 us
    pallas_call x1, Pallas kernels, shards(): pl.pallas_call(functools.partial(early_kernel, (devices, steps)), out_sha...  1.31 us
    ppermute x4, waiting for transfers between devices, swapped(): return lax.ppermute(block, axis, [(i, i ^ mask) for i in range(count)])  1.21 us
    pallas_call x1, Pallas kernels, shards(): pl.pallas_call(pack_kernel, out_shape=jax.ShapeDtypeStruct((8, FLAT + LAN...  1.11 us
  transfers between devices with their start and end apart: 7, of which 2 were waited for; matrix products, arithmetic and copies ran while one was open for 0% of the time, Pallas kernels for 12%

profile of v6, /device:TPU:9, one launch (start us, length us, event | category | flops | bytes accessed | tf_op | source)
XLA Modules:
  0.0 31.3 jit_solution(8014472493770197758)
XLA Ops:
  0.7 1.1 %pack.1 = bf16[8,768]{1,0:T(8,128)(2,1)S(1)} custom-call(s32[4,2,24,26]{3,2,1,0:T(8,128)} %bitcast.4, s32[1,32]{1,0:T(1,128)} %partners_hbm.1, s32[1]{0:T(128)S(6)} %copy.11.gate_ref), custom_call_target="tpu_custom_call" | custom-call | tf_op jit(solution)/shard_map/pack/pallas_call | solution.py:798
  1.8 0.1 collective-permute-start
  1.8 2.5 %collective-permute-start.1 = (bf16[8,768]{1,0:T(8,128)(2,1)S(1)}, bf16[8,768]{1,0:T(8,128)(2,1)S(1)}, u32[]{:S(2)}, u32[]{:S(2)}) collective-permute-start(bf16[8,768]{1,0:T(8,128)(2,1)S(1)} %pack.1), channel_id=1, source_target_pairs={{0,2},{1,3},{2,0},{3,1},{4,6},{5,7},{6,4},{7,5},{8,10},{9,11},{10,... | collective-permute-start | bytes 36872 | tf_op jit(solution)/shard_map/ppermute | solution.py:817
  4.3 2.1 %collective-permute-start.2 = (bf16[8,768]{1,0:T(8,128)(2,1)S(1)}, bf16[8,768]{1,0:T(8,128)(2,1)S(1)}, u32[]{:S(2)}, u32[]{:S(2)}) collective-permute-start(bf16[8,768]{1,0:T(8,128)(2,1)S(1)} %pack.1), channel_id=1, source_target_pairs={{0,0},{1,2},{2,1},{3,3},{4,4},{5,6},{6,5},{7,7},{8,8},{9,10},{10,9... | collective-permute-start | bytes 36872 | tf_op jit(solution)/shard_map/ppermute | solution.py:817
  6.4 0.0 collective-permute-done
  6.4 0.0 collective-permute-done.1
  6.4 2.3 %collective-permute-done.2 = bf16[8,768]{1,0:T(8,128)(2,1)S(1)} collective-permute-done((bf16[8,768]{1,0:T(8,128)(2,1)S(1)}, bf16[8,768]{1,0:T(8,128)(2,1)S(1)}, u32[]{:S(2)}, u32[]{:S(2)}) %collective-permute-start.2) | collective-permute-done | bytes 12320 | tf_op jit(solution)/shard_map/ppermute | solution.py:817
  8.8 1.3 %collective-permute-start.3 = (bf16[32,640]{1,0:T(8,128)(2,1)S(1)}, bf16[32,640]{1,0:T(8,128)(2,1)S(1)}, u32[]{:S(2)}, u32[]{:S(2)}) collective-permute-start(bf16[32,640]{1,0:T(8,128)(2,1)S(1)} %slice.4), channel_id=1, source_target_pairs={{0,8},{4,12},{8,0},{12,4},{16,24},{20,28},{24,16},{28,20},{1,9},{5... | collective-permute-start | bytes 122888 | tf_op jit(solution)/shard_map/ppermute | solution.py:782
  10.0 1.2 %collective-permute-start.4 = (bf16[32,640]{1,0:T(8,128)(2,1)S(1)}, bf16[32,640]{1,0:T(8,128)(2,1)S(1)}, u32[]{:S(2)}, u32[]{:S(2)}) collective-permute-start(bf16[32,640]{1,0:T(8,128)(2,1)S(1)} %slice.4), channel_id=1, source_target_pairs={{0,16},{4,20},{8,24},{12,28},{16,0},{20,4},{24,8},{28,12},{1,17},{... | collective-permute-start | bytes 122888 | tf_op jit(solution)/shard_map/ppermute | solution.py:782
  11.3 0.2 collective-permute-start.5
  11.5 0.0 copy-start
  11.5 2.3 %weights.1 = (bf16[256,1024]{1,0:T(8,128)(2,1)S(1)}, bf16[2304,256]{1,0:T(8,128)(2,1)S(1)}, bf16[2304,256]{1,0:T(8,128)(2,1)S(1)}, bf16[512,128]{1,0:T(8,128)(2,...) custom-call(bf16[3,3,3,32]{3,2,1,0:T(4,128)(2,1)} %first_hbm.1, ...), custom_call_target="tpu_custom_call" | custom-call | flops 1000000000 | bytes 10000000 | tf_op jit(solution)/shard_map/weights/pallas_call | solution.py:829
  13.8 0.0 collective-permute-done.3
  13.8 0.0 collective-permute-done.4
  13.8 1.2 %collective-permute-done.5 = bf16[32,640]{1,0:T(8,128)(2,1)S(1)} collective-permute-done((bf16[32,640]{1,0:T(8,128)(2,1)S(1)}, bf16[32,640]{1,0:T(8,128)(2,1)S(1)}, u32[]{:S(2)}, u32[]{:S(2)}) %collective-permute-start.5) | collective-permute-done | bytes 40992 | tf_op jit(solution)/shard_map/ppermute | solution.py:782
  15.0 4.2 %collective-permute-start.6 = (bf16[128,640]{1,0:T(8,128)(2,1)S(1)}, bf16[128,640]{1,0:T(8,128)(2,1)S(1)}, u32[]{:S(2)}, u32[]{:S(2)}) collective-permute-start(bf16[128,640]{1,0:T(8,128)(2,1)S(1)} %pad_maximum_fusion.here_ref), channel_id=1, source_target_pairs={{0,4},{4,0},{8,12},{12,8},{16,20},{20,16},{24,28},{28,24},{1,5},{5... | collective-permute-start | bytes 491528 | tf_op jit(solution)/shard_map/ppermute | solution.py:782
  19.2 0.0 copy-done
  19.2 1.3 %early.1 = (f32[26,24,1024]{2,1,0:T(8,128)S(1)}, f32[4,26,8,128]{3,2,1,0:T(8,128)S(1)}, bf16[144,256]{1,0:T(8,128)(2,1)S(1)}, f32[168,128]{1,0:T(8,128)S(1)}) custom-call(bf16[32,768]{1,0:T(8,128)(2,1)S(1)} %pad_maximum_fusion.1.near_ref, bf16[256,1024]{1,0:T(8,128)(2,1)S(1)} %get-tuple-element.32.wf_ref, bf16[512,128]{1,0:T(8,128)(2,1)S(1)} %get-tuple-element.33.dn_ref, ...), custom_call_target="tpu_custom_call" | custom-call | flops 1000000000 | bytes 10000000 | tf_op jit(solution)/shard_map/early/pallas_call | solution.py:860
  20.5 0.0 collective-permute-done.6.there_ref
  20.5 10.7 %late.1 = f32[4,2,624]{2,1,0:T(2,128)} custom-call(bf16[128,640]{1,0:T(8,128)(2,1)S(1)} %pad_maximum_fusion.here_ref, bf16[128,640]{1,0:T(8,128)(2,1)S(1)} %collective-permute-done.6.there_ref, f32[26,24,1024]{2,1,0:T(8,128)S(1)} %get-tuple-element.35.own_ref, f32[4,26,8,128]{3,2,1,0:T(8,128)S(1)} %get-tuple-element.36.pick_ref, ...), custom_call_target="tpu_custom_call" | custom-call | tf_op jit(solution)/shard_map/late/pallas_call | solution.py:875
  (4 shorter events, 0.0 us)
Async XLA Ops:
  1.8 4.6 %collective-permute-start = (bf16[8,768]{1,0:T(8,128)(2,1)S(1)}, bf16[8,768]{1,0:T(8,128)(2,1)S(1)}, u32[]{:S(2)}, u32[]{:S(2)}) collective-permute-start(bf16[8,768]{1,0:T(8,128)(2,1)S(1)} %pack.1), channel_id=1, source_target_pairs={{0,1},{1,0},{2,3},{3,2},{4,5},{5,4},{6,7},{7,6},{8,9},{9,8},{10,11... | collective-permute-start | bytes 36872 | tf_op jit(solution)/shard_map/ppermute | solution.py:817
  1.8 4.6 %collective-permute-start.1 = (bf16[8,768]{1,0:T(8,128)(2,1)S(1)}, bf16[8,768]{1,0:T(8,128)(2,1)S(1)}, u32[]{:S(2)}, u32[]{:S(2)}) collective-permute-start(bf16[8,768]{1,0:T(8,128)(2,1)S(1)} %pack.1), channel_id=1, source_target_pairs={{0,2},{1,3},{2,0},{3,1},{4,6},{5,7},{6,4},{7,5},{8,10},{9,11},{10,... | collective-permute-start | bytes 36872 | tf_op jit(solution)/shard_map/ppermute | solution.py:817
  4.3 4.4 %collective-permute-start.2 = (bf16[8,768]{1,0:T(8,128)(2,1)S(1)}, bf16[8,768]{1,0:T(8,128)(2,1)S(1)}, u32[]{:S(2)}, u32[]{:S(2)}) collective-permute-start(bf16[8,768]{1,0:T(8,128)(2,1)S(1)} %pack.1), channel_id=1, source_target_pairs={{0,0},{1,2},{2,1},{3,3},{4,4},{5,6},{6,5},{7,7},{8,8},{9,10},{10,9... | collective-permute-start | bytes 36872 | tf_op jit(solution)/shard_map/ppermute | solution.py:817
  8.8 5.0 %collective-permute-start.3 = (bf16[32,640]{1,0:T(8,128)(2,1)S(1)}, bf16[32,640]{1,0:T(8,128)(2,1)S(1)}, u32[]{:S(2)}, u32[]{:S(2)}) collective-permute-start(bf16[32,640]{1,0:T(8,128)(2,1)S(1)} %slice.4), channel_id=1, source_target_pairs={{0,8},{4,12},{8,0},{12,4},{16,24},{20,28},{24,16},{28,20},{1,9},{5... | collective-permute-start | bytes 122888 | tf_op jit(solution)/shard_map/ppermute | solution.py:782
  10.0 3.8 %collective-permute-start.4 = (bf16[32,640]{1,0:T(8,128)(2,1)S(1)}, bf16[32,640]{1,0:T(8,128)(2,1)S(1)}, u32[]{:S(2)}, u32[]{:S(2)}) collective-permute-start(bf16[32,640]{1,0:T(8,128)(2,1)S(1)} %slice.4), channel_id=1, source_target_pairs={{0,16},{4,20},{8,24},{12,28},{16,0},{20,4},{24,8},{28,12},{1,17},{... | collective-permute-start | bytes 122888 | tf_op jit(solution)/shard_map/ppermute | solution.py:782
  11.3 3.8 %collective-permute-start.5 = (bf16[32,640]{1,0:T(8,128)(2,1)S(1)}, bf16[32,640]{1,0:T(8,128)(2,1)S(1)}, u32[]{:S(2)}, u32[]{:S(2)}) collective-permute-start(bf16[32,640]{1,0:T(8,128)(2,1)S(1)} %slice.4), channel_id=1, source_target_pairs={{0,24},{4,28},{8,16},{12,20},{16,8},{20,12},{24,0},{28,4},{1,25},{... | collective-permute-start | bytes 122888 | tf_op jit(solution)/shard_map/ppermute | solution.py:782
  11.5 7.7 %copy-start = (f32[624]{0:T(1024)S(1)}, f32[624]{0:T(1024)}, u32[]{:S(2)}) copy-start(f32[624]{0:T(1024)} %param.19) | copy-start | bytes 7492
  15.0 5.5 %collective-permute-start.6 = (bf16[128,640]{1,0:T(8,128)(2,1)S(1)}, bf16[128,640]{1,0:T(8,128)(2,1)S(1)}, u32[]{:S(2)}, u32[]{:S(2)}) collective-permute-start(bf16[128,640]{1,0:T(8,128)(2,1)S(1)} %pad_maximum_fusion.here_ref), channel_id=1, source_target_pairs={{0,4},{4,0},{8,12},{12,8},{16,20},{20,16},{24,28},{28,24},{1,5},{5... | collective-permute-start | bytes 491528 | tf_op jit(solution)/shard_map/ppermute | solution.py:782
